TPU v7x, 128 devices: a whole 4x4x4 slice. The times are simulated.
128 devices in a mesh: lat: 8 (over x, z_hi), lon: 16 (over z_lo, y, core).
Axes of the slice: x: 4, y: 4, z: 4 (z_hi: 2, z_lo: 2; z = z_hi * 2 + z_lo), core: 2. Of those that a mesh axis runs over, the one named last changes fastest.
Arguments:
- east_flow_speed: float32 [4, 1024, 5760], P(None, 'lat', 'lon'), may hold values from -6 to 6
- north_flow_speed: float32 [4, 1024, 5760], P(None, 'lat', 'lon'), may hold values from -6 to 6
- thermal_anomaly: float32 [4, 1024, 5760], P(None, 'lat', 'lon'), may hold values from -6 to 6
- moisture_anomaly: float32 [4, 1024, 5760], P(None, 'lat', 'lon'), may hold values from -6 to 6
Outputs:
- next_zonal: float32 [4, 1024, 5760], P(None, 'lat', 'lon')
- next_meridional: float32 [4, 1024, 5760], P(None, 'lat', 'lon')
- next_temperature: float32 [4, 1024, 5760], P(None, 'lat', 'lon')
- next_humidity: float32 [4, 1024, 5760], P(None, 'lat', 'lon')
All inputs are finite; a program needn't handle non-finite values.
Results may differ from a plain program's by a relative error of at most 0.000078.
Values sent between devices are 32-bit elements; how exact they have to be, the bound alone decides.
No kernel may reach another device: no remote copies, remote signals or barrier semaphores. Data moves between devices by JAX's collectives and lax.ppermute only.
A program may use at most 128 MiB of HBM per device.

v0:
```python
import math

import jax
import jax.numpy as jnp
from jax import lax
from jax.sharding import Mesh
from jax.sharding import PartitionSpec as P

LON = ("lon_0", "lon_1", "lon_2")


ADV_COEF = 0.25
DIFF_COEF = 0.15
COS_CUT = math.cos(55.0 * math.pi / 180.0)
HIGHEST = lax.Precision.HIGHEST


def split_up(array, dim, peers):
    lengths = array.shape
    blocks = array.reshape(*lengths[:dim], peers, lengths[dim] // peers, *lengths[dim + 1 :])
    return jnp.moveaxis(blocks, dim, 0)


def joined_along(blocks, dim):
    blocks = jnp.moveaxis(blocks, 0, dim)
    lengths = blocks.shape
    return blocks.reshape(*lengths[:dim], lengths[dim] * lengths[dim + 1], *lengths[dim + 2 :])


def turned_blocks(blocks, axes, turns):
    lengths = [lax.axis_size(a) for a in axes]
    blocks = blocks.reshape(*lengths, *blocks.shape[1:])
    for k in turns:
        blocks = lax.all_to_all(blocks, axes[k], split_axis=k, concat_axis=k, tiled=True)
    return blocks.reshape(-1, *blocks.shape[len(axes) :])


def core_and_chips(array, groups, turns, split_dim, concat_dim):
    peers = lax.axis_size(groups[0]) * lax.axis_size(groups[1])
    blocks = split_up(array, split_dim, peers)
    return joined_along(turned_blocks(blocks, groups, turns), concat_dim)


def from_behind(array, axis, by):
    peers = lax.axis_size(axis)
    return lax.ppermute(array, axis, [(i, (i + by) % peers) for i in range(peers)])


def padded_2(array, sides, width):
    edges = {}
    for axis, dim in sides:
        peers, length = (lax.axis_size(axis), array.shape[dim])
        up = [(i, (i + 1) % peers) for i in range(peers)]
        last = lax.slice_in_dim(array, length - width, length, axis=dim)
        first = lax.slice_in_dim(array, 0, width, axis=dim)
        edges[dim] = (
            lax.ppermute(last, axis, up),
            lax.ppermute(first, axis, [(b, a) for a, b in up]),
        )
    done = []
    for _, dim in sides:
        low, high = edges[dim]
        around = [(width, width) if d in done else (0, 0) for d in range(array.ndim)]
        array = jnp.concatenate([jnp.pad(low, around), array, jnp.pad(high, around)], axis=dim)
        done.append(dim)
    return array


def update(padded, centre, lower_edge, upper_edge):
    centre_cells = padded[..., 1:-1, 1:-1]
    eastern = padded[..., 1:-1, 2:]
    western = padded[..., 1:-1, :-2]
    northern = padded[..., 2:, 1:-1]
    southern = padded[..., :-2, 1:-1]
    wind_u = centre_cells[0]
    wind_v = centre_cells[1]
    advect = wind_u * (eastern - western) * 0.5 + wind_v * (northern - southern) * 0.5
    zonal_term = eastern - 2.0 * centre_cells + western
    meridional = (
        upper_edge[:, None] * (northern - centre_cells)
        - lower_edge[:, None] * (centre_cells - southern)
    ) / centre[:, None]
    return centre_cells - ADV_COEF * advect + DIFF_COEF * (zonal_term + meridional)


def polar_rows(blocks, row_ids, total_rows):
    groups, fields_here, part_rows, points = blocks.shape
    block_width = math.gcd(points // 2, 320)
    centre = jnp.sin((row_ids.astype(jnp.float32) + 0.5) * (math.pi / total_rows))
    retain = (centre / COS_CUT) ** 2
    wave_blocks = points // 2 // block_width
    block_ends = (jnp.arange(wave_blocks, dtype=jnp.int32) + 1) * block_width - 1
    top_sine = jnp.sin(block_ends.astype(jnp.float32) * (math.pi / points)) ** 2
    needed = top_sine[None, :] > jnp.min(retain, axis=1)[:, None]
    starts = wave_blocks - jnp.sum(needed.astype(jnp.int32), axis=1)
    flat = blocks.reshape(groups, fields_here * part_rows, points)
    retain_rows = jnp.broadcast_to(retain[:, None, :], (groups, fields_here, part_rows)).reshape(
        groups, fields_here * part_rows
    )
    positions = jnp.arange(points, dtype=jnp.int32)

    def one_block(index, total):
        wave = index * block_width + jnp.arange(block_width, dtype=jnp.int32)
        phase = wave[:, None] * positions[None, :] % points
        angle = phase.astype(jnp.float32) * (2.0 * math.pi / points)
        cosine = jnp.cos(angle)
        sine = jnp.sin(angle)
        sine_sq = jnp.sin(wave.astype(jnp.float32) * (math.pi / points)) ** 2
        weight = jnp.where(wave == 0, 1.0, 2.0).astype(jnp.float32) / points

        def per_group(group, carry):

            def apply(current):
                group_rows = lax.dynamic_index_in_dim(flat, group, 0, keepdims=False)
                group_keep = lax.dynamic_index_in_dim(retain_rows, group, 0, keepdims=False)
                damping = group_keep[:, None] / jnp.maximum(sine_sq[None, :], group_keep[:, None])
                scale = (1.0 - damping) * weight[None, :]
                cos_part = lax.dot_general(
                    group_rows,
                    cosine,
                    (((1,), (1,)), ((), ())),
                    precision=HIGHEST,
                    preferred_element_type=jnp.float32,
                )
                sin_part = lax.dot_general(
                    group_rows,
                    sine,
                    (((1,), (1,)), ((), ())),
                    precision=HIGHEST,
                    preferred_element_type=jnp.float32,
                )
                back = jnp.dot(
                    cos_part * scale, cosine, precision=HIGHEST, preferred_element_type=jnp.float32
                )
                back = back + jnp.dot(
                    sin_part * scale, sine, precision=HIGHEST, preferred_element_type=jnp.float32
                )
                previous = lax.dynamic_index_in_dim(current, group, 0, keepdims=False)
                return lax.dynamic_update_index_in_dim(current, previous + back, group, 0)

            return lax.cond(index >= starts[group], apply, lambda current: current, carry)

        return lax.fori_loop(0, groups, per_group, total)

    correction = lax.fori_loop(jnp.min(starts), wave_blocks, one_block, jnp.zeros_like(flat))
    alternate = jnp.where(positions % 2 == 0, 1.0, -1.0).astype(jnp.float32)
    top_coef = jnp.sum(flat * alternate, axis=-1)
    top_damp = retain_rows / jnp.maximum(1.0, retain_rows)
    correction = correction + ((1.0 - top_damp) * top_coef / points)[..., None] * alternate
    return (flat - correction).reshape(groups, fields_here, part_rows, points)


def on_device(east_flow_speed, north_flow_speed, thermal_anomaly, moisture_anomaly):
    height_layer_sequence, rows, cols = east_flow_speed.shape
    lat_parts = lax.axis_size("lat")
    lon_parts = lax.axis_size(LON)
    total_rows = rows * lat_parts
    band = lax.axis_index("lat")
    column = lax.axis_index(LON)
    part_rows = rows // lon_parts
    flow_components = jnp.concatenate([east_flow_speed, north_flow_speed], axis=0)
    local_rows = jnp.arange(part_rows, dtype=jnp.int32)
    circles = lax.all_to_all(flow_components, LON, split_axis=1, concat_axis=2, tiled=True)
    row_ids = (band * rows + column * part_rows + local_rows)[None, :]
    filtered = polar_rows(circles[None], row_ids, total_rows)[0]
    flow_components = core_and_chips(filtered, (("lon_0", "lon_1"), "lon_2"), (1, 0), 2, 1)
    tracer_bundle = jnp.stack(
        [
            flow_components[:height_layer_sequence],
            flow_components[height_layer_sequence:],
            thermal_anomaly,
            moisture_anomaly,
        ]
    )
    rim_rows = jnp.concatenate([tracer_bundle[:, :, :1, :], tracer_bundle[:, :, -1:, :]], axis=2)
    across = from_behind(rim_rows, LON, lon_parts // 2)
    flip_sign = jnp.array([-1.0, -1.0, 1.0, 1.0], dtype=jnp.float32)[:, None, None, None]
    across = across * flip_sign
    padded = padded_2(tracer_bundle, (("lat", 2), (LON, 3)), 1)
    south_rim = jnp.where(band == 0, across[:, :, 0, :], padded[:, :, 0, 1:-1])
    north_rim = jnp.where(band == lat_parts - 1, across[:, :, 1, :], padded[:, :, -1, 1:-1])
    padded = padded.at[:, :, 0, 1:-1].set(south_rim).at[:, :, -1, 1:-1].set(north_rim)
    row_index = (band * rows + jnp.arange(rows, dtype=jnp.int32)).astype(jnp.float32)
    centre = jnp.sin((row_index + 0.5) * (math.pi / total_rows))
    lower_edge = jnp.sin(row_index * (math.pi / total_rows))
    upper_edge = jnp.sin((row_index + 1.0) * (math.pi / total_rows))
    stepped = update(padded, centre, lower_edge, upper_edge)
    return (stepped[0], stepped[1], stepped[2], stepped[3])


def solution(mesh):
    torus = Mesh(
        mesh.devices.reshape(mesh.shape["lat"], 2, 4, 2), ("lat", "lon_0", "lon_1", "lon_2")
    )
    placed = (P(None, "lat", LON), P(None, "lat", LON), P(None, "lat", LON), P(None, "lat", LON))
    return jax.shard_map(
        on_device,
        mesh=torus,
        in_specs=placed,
        out_specs=(
            P(None, "lat", LON),
            P(None, "lat", LON),
            P(None, "lat", LON),
            P(None, "lat", LON),
        ),
        check_vma=False,
    )
```

profile of v0, /device:TPU:6, one launch (start us, length us, event | category | flops | bytes accessed | tf_op | source)
XLA Modules:
  0.0 1333.3 jit_solution(4970226679590426763)
XLA Ops:
  0.6 1.4 copy.45
  2.1 1.4 copy.46
  3.5 1.5 pad_maximum_fusion.1
  5.0 5.9 all-to-all-start
  11.0 0.6 multiply_multiply_fusion
  11.6 1.3 fusion.50
  13.7 19.3 %all-to-all-done = f32[8,128,360]{2,0,1:T(8,128)S(1)} async-done(((f32[8,128,360]{2,0,1:T(8,128)}), f32[8,128,360]{2,0,1:T(8,128)S(1)}, u32[]{:S(2)}, u32[]{:S(2)}) %all-to-all-start) | async-done | bytes 1474592 | tf_op jit(solution)/shard_map/all_to_all | solution.py:163
  33.1 1.2 copy-done.5
  34.3 0.9 copy.48
  35.2 0.6 reshape_broadcast_in_dim.3
  35.8 0.1 broadcast_in_dim.61
  36.0 0.4 while.24
  36.4 1.9 fusion.37
  38.3 1.4 add_subtract_fusion
  39.7 2.6 reshape_squeeze_reshape.3
  42.3 0.5 copy.49
  42.9 0.2 copy.50
  43.0 5.0 all_to_all.25
  48.0 1.3 copy.51
  49.3 683.3 %all-to-all-start.2 = ((f32[8,2,8,8,360]{4,3,1,2,0:T(8,128)}), f32[8,2,8,8,360]{4,3,1,2,0:T(8,128)S(1)}, u32[]{:S(2)}, u32[]{:S(2)}) async-start(f32[8,2,8,8,360]{4,3,1,2,0:T(8,128)} %copy.51), calls=%async_computation.2 | async-start | bytes 3145728 | tf_op jit(solution)/shard_map/all_to_all | solution.py:34
  732.7 0.3 copy.55
  732.9 1.7 copy.56
  734.7 0.6 fusion.54
  735.4 18.9 %all-to-all-done.2 = f32[8,2,8,8,360]{4,3,1,2,0:T(8,128)S(1)} async-done(((f32[8,2,8,8,360]{4,3,1,2,0:T(8,128)}), f32[8,2,8,8,360]{4,3,1,2,0:T(8,128)S(1)}, u32[]{:S(2)}, u32[]{:S(2)}) %all-to-all-start.2) | async-done | bytes 1474592 | tf_op jit(solution)/shard_map/all_to_all | solution.py:34
  754.3 0.2 copy.52
  754.4 0.1 fusion.53
  754.8 0.2 pad_maximum_fusion
  755.0 0.5 copy-done.3
  755.5 0.3 copy-done.4
  755.9 548.1 %collective-permute-start.1 = (f32[4,4,1,360]{3,2,1,0:T(1,128)S(1)}, f32[4,4,1,360]{3,2,1,0:T(1,128)S(1)}, u32[]{:S(2)}, u32[]{:S(2)}) collective-permute-start(f32[4,4,1,360]{3,2,1,0:T(1,128)S(1)} %get-tuple-element.284), channel_id=1, source_target_pairs={{0,16},{16,32},{32,48},{48,64},{64,80},{80,96},{96,112},{112,0},{1... | collective-permute-start | bytes 69128 | tf_op jit(solution)/shard_map/ppermute | solution.py:57
  1304.0 0.3 slice.152
  1304.3 0.3 copy.57
  1304.7 0.3 copy.59
  1305.0 3.9 collective-permute-start.3
  1309.0 0.3 collective-permute-start.4
  1309.3 0.6 collective-permute-done
  1309.9 1.4 copy.58
  1311.2 1.4 copy.60
  1312.6 4.6 select_maximum_fusion
  1317.4 4.1 scatter.6
  1321.5 2.8 scatter.9
  1324.3 0.5 slice_bitcast_fusion.5
  1324.8 3.6 multiply_add_fusion
  1328.5 0.2 slice_bitcast_fusion
  1328.8 1.1 copy.61
  1329.9 1.1 copy.62
  1331.0 1.1 copy.63
  1332.1 1.1 copy.64
  (33 shorter events, 0.8 us)
Async XLA Ops:
  5.0 28.0 %all-to-all-start = ((f32[8,128,360]{2,0,1:T(8,128)}), f32[8,128,360]{2,0,1:T(8,128)S(1)}, u32[]{:S(2)}, u32[]{:S(2)}) async-start(f32[8,128,360]{2,0,1:T(8,128)} %pad_maximum_fusion.1), calls=%async_computation | async-start | bytes 3145728 | tf_op jit(solution)/shard_map/all_to_all | solution.py:163
  33.1 1.2 copy-start.5
  48.0 684.6 %copy-start.6 = (f32[4,128,360]{1,2,0:T(8,128)S(1)}, f32[4,128,360]{1,2,0:T(8,128)}, u32[]{:S(2)}) copy-start(f32[4,128,360]{1,2,0:T(8,128)} %param.15) | copy-start | bytes 2211844
  49.3 704.9 %all-to-all-start.2 = ((f32[8,2,8,8,360]{4,3,1,2,0:T(8,128)}), f32[8,2,8,8,360]{4,3,1,2,0:T(8,128)S(1)}, u32[]{:S(2)}, u32[]{:S(2)}) async-start(f32[8,2,8,8,360]{4,3,1,2,0:T(8,128)} %copy.51), calls=%async_computation.2 | async-start | bytes 3145728 | tf_op jit(solution)/shard_map/all_to_all | solution.py:34
  732.9 22.1 %copy-start.1 = (f32[4,128,360]{2,1,0:T(8,128)}, f32[4,128,360]{2,1,0:T(8,128)S(1)}, u32[]{:S(2)}) copy-start(f32[4,128,360]{2,1,0:T(8,128)S(1)} %copy.55) | copy-start | bytes 2211844
  734.6 20.4 %copy-start.2 = (f32[4,128,360]{2,1,0:T(8,128)}, f32[4,128,360]{2,1,0:T(8,128)S(1)}, u32[]{:S(2)}) copy-start(f32[4,128,360]{2,1,0:T(8,128)S(1)} %copy.56) | copy-start | bytes 2211844
  754.6 0.9 copy-start.3
  754.7 1.1 copy-start.4
  755.9 556.7 %collective-permute-start.1 = (f32[4,4,1,360]{3,2,1,0:T(1,128)S(1)}, f32[4,4,1,360]{3,2,1,0:T(1,128)S(1)}, u32[]{:S(2)}, u32[]{:S(2)}) collective-permute-start(f32[4,4,1,360]{3,2,1,0:T(1,128)S(1)} %get-tuple-element.284), channel_id=1, source_target_pairs={{0,16},{16,32},{32,48},{48,64},{64,80},{80,96},{96,112},{112,0},{1... | collective-permute-start | bytes 69128 | tf_op jit(solution)/shard_map/ppermute | solution.py:57
  1304.0 8.6 collective-permute-start.2
  1304.7 5.2 collective-permute-start
  1305.0 6.2 collective-permute-start.3
  1309.0 8.2 collective-permute-start.4
  1312.6 4.6 copy-start.7
where the time goes:
time: 1340 us; the launch traced here: 1330 us
  starting transfers between devices  1240 us (93%)
  waiting for transfers between devices  38.8 us (3%)
  local copies, waits for them, and re-layouts  30.2 us (2%)
  other arithmetic  15.6 us (1%)
    all_to_all x1, starting transfers between devices, turned_blocks(): lax.all_to_all(blocks, axes[k], split_axis=k, concat_axis=k, tiled=True)  683 us
    ppermute x2, starting transfers between devices, padded_2(): lax.ppermute(last, axis, up)  548 us
  transfers between devices with their start and end apart: 7, of which 3 were waited for; matrix products, arithmetic and copies ran while one was open for 1% of the time, Pallas kernels for 0%

commit v1 on v0

v1 whole, which is shorter than its diff:
```python
import math

import jax
import jax.numpy as jnp
import numpy as np
from jax import lax
from jax.experimental import pallas as pl
from jax.experimental.pallas import tpu as pltpu
from jax.sharding import Mesh
from jax.sharding import PartitionSpec as P

LON = ("lon_0", "lon_1", "lon_2")
ALL = ("lat",) + LON
ADV_COEF = 0.25
DIFF_COEF = 0.15
COS_CUT = math.cos(55.0 * math.pi / 180.0)
LANES = 128
SUB = 8
VMEM_LIMIT = 56 * 1024 * 1024


def fourier_tables(parts, width, wide):
    points = parts * width
    m = np.arange(width)
    angle = 2.0 * np.pi * (np.outer(m, m) % width) / width
    matrix = np.zeros((2 * wide, 2 * wide))
    matrix[:width, :width] = np.cos(angle)
    matrix[:width, wide : wide + width] = -np.sin(angle)
    matrix[wide : wide + width, :width] = np.sin(angle)
    matrix[wide : wide + width, wide : wide + width] = np.cos(angle)
    high = matrix.astype(np.float32).astype(jnp.bfloat16)
    low = (matrix - high.astype(np.float64)).astype(np.float32).astype(jnp.bfloat16)
    k1 = np.arange(parts)
    turn = 2.0 * np.pi * np.outer(k1, m) / points
    twiddle = np.zeros((2, parts, wide), np.float32)
    twiddle[0, :, :width] = np.cos(turn)
    twiddle[1, :, :width] = -np.sin(turn)
    wave = k1[:, None] + parts * m[None, :]
    sine_sq = np.ones((parts, wide), np.float32)
    sine_sq[:, :width] = np.sin(np.pi * wave / points) ** 2
    return high, low, twiddle, sine_sq


def four_point(a, b, c, d):
    pr, pi = a[0] + c[0], a[1] + c[1]
    mr, mi = a[0] - c[0], a[1] - c[1]
    qr, qi = b[0] + d[0], b[1] + d[1]
    nr, ni = b[0] - d[0], b[1] - d[1]
    return (pr + qr, pi + qi), (mr + ni, mi - nr), (pr - qr, pi - qi), (mr - ni, mi + nr)


def turned(x, e):
    re, im = x
    if e == 0:
        return x
    if e == 4:
        return im, -re
    h = math.sqrt(0.5)
    if e == 2:
        return (re + im) * h, (im - re) * h
    if e == 6:
        return (im - re) * h, -(re + im) * h
    c, s = math.cos(2 * math.pi * e / 16), math.sin(2 * math.pi * e / 16)
    return re * c + im * s, im * c - re * s


def sixteen_point(x):
    inner = [four_point(x[s], x[4 + s], x[8 + s], x[12 + s]) for s in range(4)]
    out = [None] * 16
    for a in range(4):
        col = four_point(*[turned(inner[s][a], s * a) for s in range(4)])
        for b in range(4):
            out[a + 4 * b] = col[b]
    return out


def pack_kernel(u_ref, v_ref, out_ref):
    parts, _, sub, wide = out_ref.shape
    width = u_ref.shape[-1]
    for i, ref in enumerate((u_ref, v_ref)):
        out_ref[:, i, :, :width] = ref[0].reshape(parts, sub, width)
        out_ref[:, i, :, width:] = jnp.zeros((parts, sub, wide - width), jnp.float32)


def pack(u, v, parts, wide):
    levels, rows, width = u.shape
    sub = rows // parts
    spec = pl.BlockSpec((1, rows, width), lambda g: (g, 0, 0))
    return pl.pallas_call(
        pack_kernel,
        grid=(levels,),
        in_specs=[spec, spec],
        out_specs=pl.BlockSpec((parts, 2, sub, wide), lambda g: (0, g, 0, 0)),
        out_shape=jax.ShapeDtypeStruct((parts, 2 * levels, sub, wide), jnp.float32),
        name="pack",
    )(u, v)


def split_dot(x, high, low):
    top = x.astype(jnp.bfloat16)
    rest = (x - top.astype(jnp.float32)).astype(jnp.bfloat16)

    def dot(a, b):
        return jnp.dot(a, b, preferred_element_type=jnp.float32)

    return dot(top, high) + (dot(rest, high) + dot(top, low))


def filter_kernel(width, x_ref, keep_ref, high_ref, low_ref, twiddle_ref, sine_ref, out_ref, a_ref):
    parts, planes, sub, wide = x_ref.shape
    levels = planes // 2
    chunks = wide // LANES
    group = levels * sub
    points = parts * width

    for c in range(chunks):
        lanes = slice(c * LANES, (c + 1) * LANES)
        lanes_im = slice(wide + c * LANES, wide + (c + 1) * LANES)
        for level in range(levels):
            x = [(x_ref[d, 2 * level, :, lanes], x_ref[d, 2 * level + 1, :, lanes]) for d in range(parts)]
            y = sixteen_point(x)
            rows = slice(level * sub, (level + 1) * sub)
            for k in range(parts):
                re, im = y[k]
                co = twiddle_ref[0, k : k + 1, lanes]
                si = twiddle_ref[1, k : k + 1, lanes]
                a_ref[k, rows, lanes] = re * co - im * si
                a_ref[k, rows, lanes_im] = re * si + im * co

    z = split_dot(a_ref[...].reshape(parts * group, 2 * wide), high_ref[...], low_ref[...])
    z = z.reshape(parts, levels, sub, 2 * wide)
    keep = jnp.broadcast_to(keep_ref[...], (sub, wide))[None]
    damping = keep / jnp.maximum(sine_ref[...][:, None, :], keep) * (1.0 / points)
    damping = damping[:, None]
    a_ref[:, :, :wide] = (z[..., :wide] * damping).reshape(parts, group, wide)
    a_ref[:, :, wide:] = (z[..., wide:] * -damping).reshape(parts, group, wide)
    z = split_dot(a_ref[...].reshape(parts * group, 2 * wide), high_ref[...], low_ref[...])
    a_ref[...] = z.reshape(parts, group, 2 * wide)

    for c in range(chunks):
        lanes = slice(c * LANES, (c + 1) * LANES)
        lanes_im = slice(wide + c * LANES, wide + (c + 1) * LANES)
        for level in range(levels):
            rows = slice(level * sub, (level + 1) * sub)
            x = []
            for k in range(parts):
                re = a_ref[k, rows, lanes]
                im = a_ref[k, rows, lanes_im]
                co = twiddle_ref[0, k : k + 1, lanes]
                si = twiddle_ref[1, k : k + 1, lanes]
                x.append((re * co - im * si, re * si + im * co))
            y = sixteen_point(x)
            for d in range(parts):
                out_ref[d, 2 * level, :, lanes] = y[d][0]
                out_ref[d, 2 * level + 1, :, lanes] = -y[d][1]

    tail = slice((chunks - 1) * LANES, chunks * LANES)
    at = width - (chunks - 1) * LANES
    lane = lax.broadcasted_iota(jnp.int32, (planes, sub, LANES), 2)
    firsts = [out_ref[d, :, :, :LANES] for d in range(parts)]
    lasts = [out_ref[d, :, :, tail] for d in range(parts)]
    for d in range(parts):
        west = pltpu.roll(lasts[(d - 1) % parts], 1, 2)
        east = pltpu.roll(firsts[(d + 1) % parts], at + 1, 2)
        out_ref[d, :, :, tail] = jnp.where(
            lane == at, west, jnp.where(lane == at + 1, east, lasts[d])
        )


def polar_filter(blocks, keep, width):
    parts, planes, sub, wide = blocks.shape
    high, low, twiddle, sine_sq = fourier_tables(parts, width, wide)
    return pl.pallas_call(
        lambda *refs: filter_kernel(width, *refs),
        out_shape=jax.ShapeDtypeStruct(blocks.shape, jnp.float32),
        scratch_shapes=[pltpu.VMEM((parts, planes // 2 * sub, 2 * wide), jnp.float32)],
        compiler_params=pltpu.CompilerParams(vmem_limit_bytes=VMEM_LIMIT),
        name="polar_filter",
    )(blocks, keep, jnp.asarray(high), jnp.asarray(low), jnp.asarray(twiddle), jnp.asarray(sine_sq))


def stepped(f, east, west, south, north, u, v, upper, lower):
    rows = f.shape[0]
    row = lax.broadcasted_iota(jnp.int32, f.shape, 0)
    above = jnp.where(row == rows - 1, north, pltpu.roll(f, rows - 1, 0))
    below = jnp.where(row == 0, south, pltpu.roll(f, 1, 0))
    advect = u * (east - west) * 0.5 + v * (above - below) * 0.5
    spread = (east - 2.0 * f + west) + (upper * (above - f) - lower * (f - below))
    return f - ADV_COEF * advect + DIFF_COEF * spread


def tracer_kernel(t_ref, q_ref, w_ref, edge_ref, side_ref, row_ref, t_out, q_out):
    parts, _, sub, wide = w_ref.shape
    rows, width = t_ref.shape[1:]
    u = w_ref[:, 0].reshape(rows, wide)[:, :width]
    v = w_ref[:, 1].reshape(rows, wide)[:, :width]
    upper, lower = row_ref[:, 0:1], row_ref[:, 1:2]
    lane = lax.broadcasted_iota(jnp.int32, (rows, width), 1)
    for i, (ref, out) in enumerate(((t_ref, t_out), (q_ref, q_out))):
        f = ref[0]
        west = jnp.where(lane == 0, side_ref[0, :, i : i + 1], jnp.roll(f, 1, 1))
        east = jnp.where(lane == width - 1, side_ref[0, :, 2 + i : 3 + i], jnp.roll(f, -1, 1))
        out[0] = stepped(
            f, east, west, edge_ref[0, i : i + 1], edge_ref[0, 2 + i : 3 + i], u, v, upper, lower
        )


def wind_kernel(w_ref, edge_ref, row_ref, u_out, v_out):
    parts, _, sub, wide = w_ref.shape
    rows, width = u_out.shape[1:]
    upper, lower = row_ref[:, 0:1], row_ref[:, 1:2]
    full = [w_ref[:, i].reshape(rows, wide) for i in range(2)]
    lane = lax.broadcasted_iota(jnp.int32, (rows, wide), 1)
    for i, out in enumerate((u_out, v_out)):
        f = full[i]
        west = pltpu.roll(f, 1, 1)
        east = pltpu.roll(f, wide - 1, 1)
        west = jnp.where(lane == 0, f[:, width : width + 1], west)
        east = jnp.where(lane == width - 1, f[:, width + 1 : width + 2], east)
        f, west, east = f[:, :width], west[:, :width], east[:, :width]
        out[0] = stepped(
            f,
            east,
            west,
            edge_ref[0, i : i + 1],
            edge_ref[0, 2 + i : 3 + i],
            full[0][:, :width],
            full[1][:, :width],
            upper,
            lower,
        )


def lat_edges(fields, band, bands, z_low, flip):
    last, first = fields[:, :, -1], fields[:, :, 0]
    lon_rest = lax.axis_size(LON) // 2

    def place(step):
        half, at = divmod(step % (2 * bands), bands)
        return half, (at if half == 0 else bands - 1 - at)

    pairs = []
    for step in range(2 * bands):
        for rest in range(lon_rest):
            (h0, b0), (h1, b1) = place(step), place(step + 1)
            pairs.append(((b0 * 2 + h0) * lon_rest + rest, (b1 * 2 + h1) * lon_rest + rest))
    onward = jnp.where(z_low == 0, last, first)
    backward = jnp.where(z_low == 0, first, last)
    from_before = lax.ppermute(onward, ALL, pairs)
    from_after = lax.ppermute(backward, ALL, [(b, a) for a, b in pairs])
    south = jnp.where(z_low == 0, from_before, from_after)
    north = jnp.where(z_low == 0, from_after, from_before)
    south = jnp.where(band == 0, flip * south, south)
    north = jnp.where(band == bands - 1, flip * north, north)
    return jnp.concatenate([south, north], axis=1)


def on_device(east_flow_speed, north_flow_speed, thermal_anomaly, moisture_anomaly):
    levels, rows, width = east_flow_speed.shape
    bands = lax.axis_size("lat")
    parts = lax.axis_size(LON)
    total_rows = rows * bands
    band = lax.axis_index("lat")
    column = lax.axis_index(LON)
    z_low = lax.axis_index("lon_0")
    wide = -(-(width + 2) // LANES) * LANES
    sub = rows // parts

    sent = pack(east_flow_speed, north_flow_speed, parts, wide)
    circles = lax.all_to_all(sent, LON, split_axis=0, concat_axis=0, tiled=True)
    own_rows = (band * rows + column * sub + jnp.arange(sub, dtype=jnp.int32)).astype(jnp.float32)
    keep = ((jnp.sin((own_rows + 0.5) * (math.pi / total_rows))) / COS_CUT) ** 2
    filtered = polar_filter(circles, keep[:, None], width)
    winds = lax.all_to_all(filtered, LON, split_axis=0, concat_axis=0, tiled=True)

    row_index = (band * rows + jnp.arange(rows, dtype=jnp.int32)).astype(jnp.float32)
    centre = jnp.sin((row_index + 0.5) * (math.pi / total_rows))
    lower_edge = jnp.sin(row_index * (math.pi / total_rows))
    upper_edge = jnp.sin((row_index + 1.0) * (math.pi / total_rows))
    factors = jnp.stack([upper_edge / centre, lower_edge / centre], axis=1)

    tracers = jnp.stack([thermal_anomaly, moisture_anomaly], axis=1)
    tracer_edges = lat_edges(tracers, band, bands, z_low, 1.0)
    ring = [(i, (i + 1) % parts) for i in range(parts)]
    west_side = lax.ppermute(tracers[:, :, :, -1], LON, ring)
    east_side = lax.ppermute(tracers[:, :, :, 0], LON, [(b, a) for a, b in ring])
    sides = jnp.swapaxes(jnp.concatenate([west_side, east_side], axis=1), 1, 2)

    field = pl.BlockSpec((1, rows, width), lambda g: (g, 0, 0))
    wind = pl.BlockSpec((parts, 2, sub, wide), lambda g: (0, g, 0, 0))
    edge = pl.BlockSpec((1, 4, width), lambda g: (g, 0, 0))
    side = pl.BlockSpec((1, rows, 4), lambda g: (g, 0, 0))
    factor = pl.BlockSpec((rows, 2), lambda g: (0, 0))
    shape = jax.ShapeDtypeStruct((levels, rows, width), jnp.float32)
    next_t, next_q = pl.pallas_call(
        tracer_kernel,
        grid=(levels,),
        in_specs=[field, field, wind, edge, side, factor],
        out_specs=[field, field],
        out_shape=[shape, shape],
        name="tracers",
    )(thermal_anomaly, moisture_anomaly, winds, tracer_edges, sides, factors)

    by_row = jnp.stack([winds[0, :, 0, :width], winds[-1, :, -1, :width]], axis=1)
    wind_edges = lat_edges(by_row.reshape(levels, 2, 2, width), band, bands, z_low, -1.0)
    next_u, next_v = pl.pallas_call(
        wind_kernel,
        grid=(levels,),
        in_specs=[wind, edge, factor],
        out_specs=[field, field],
        out_shape=[shape, shape],
        name="winds",
    )(winds, wind_edges, factors)
    return next_u, next_v, next_t, next_q


def solution(mesh):
    torus = Mesh(
        mesh.devices.reshape(mesh.shape["lat"], 2, 4, 2), ("lat", "lon_0", "lon_1", "lon_2")
    )
    placed = (P(None, "lat", LON),) * 4
    return jax.shard_map(
        on_device, mesh=torus, in_specs=placed, out_specs=placed, check_vma=False
    )
```

time: 1340 us -> 97.9 us (0.07)
  starting transfers between devices: 1240 us -> 22.2 us
  Pallas kernels: 0 us -> 24.4 us
    all_to_all x2, starting transfers between devices: 689 us -> 9.77 us  [the longest x1 5.93 us: on_device(): circles = lax.all_to_all(sent, LON, split_axis=0, concat_axis=0, tiled=True)]
    ppermute x5 -> x6, starting transfers between devices: 552 us -> 12.4 us  [the longest x2 4.83 us: lat_edges(): from_after = lax.ppermute(backward, ALL, [(b, a) for a, b in pairs])]
    pallas_call x0 -> x4, Pallas kernels: none -> 24.4 us  [the longest x1 11.2 us: polar_filter(): pl.pallas_call(lambda *refs: filter_kernel(width, *refs), out_shape=jax.S...]
    all_to_all x2, waiting for transfers between devices: 38.2 us -> 21.4 us  [the longest x1 21.4 us: on_device(): circles = lax.all_to_all(sent, LON, split_axis=0, concat_axis=0, tiled=True)]
  transfers between devices with their start and end apart: 7 -> 8, of which waited for: 3 -> 2; matrix products, arithmetic and copies ran while one was open for 1% -> 15% of each run, Pallas kernels for 0% -> 5%
where the time goes in v1:
time: 97.9 us; the launch traced here: 97.3 us
  waiting for transfers between devices  26.5 us (27%)
  Pallas kernels  24.4 us (25%)
  starting transfers between devices  22.2 us (23%)
  local copies, waits for them, and re-layouts  19.2 us (20%)
  other arithmetic  4.13 us (4%)
    all_to_all x1, waiting for transfers between devices, on_device(): circles = lax.all_to_all(sent, LON, split_axis=0, concat_axis=0, tiled=True)  21.4 us
    unnamed x24, local copies, waits for them, and re-layouts  17.6 us
    pallas_call x1, Pallas kernels, polar_filter(): pl.pallas_call(lambda *refs: filter_kernel(width, *refs), out_shape=jax.S...  11.2 us
    all_to_all x1, starting transfers between devices, on_device(): circles = lax.all_to_all(sent, LON, split_axis=0, concat_axis=0, tiled=True)  5.93 us
    pallas_call x1, Pallas kernels, on_device(): pl.pallas_call(tracer_kernel, grid=(levels,), in_specs=[field, field, win...  5.09 us
    ppermute x1, waiting for transfers between devices, on_device(): west_side = lax.ppermute(tracers[:, :, :, -1], LON, ring)  5.06 us
    ppermute x2, starting transfers between devices, lat_edges(): from_after = lax.ppermute(backward, ALL, [(b, a) for a, b in pairs])  4.83 us
    pallas_call x1, Pallas kernels, on_device(): pl.pallas_call(wind_kernel, grid=(levels,), in_specs=[wind, edge, factor]...  4.43 us
  transfers between devices with their start and end apart: 8, of which 2 were waited for; matrix products, arithmetic and copies ran while one was open for 15% of the time, Pallas kernels for 5%

profile of v1, /device:TPU:6, one launch (start us, length us, event | category | flops | bytes accessed | tf_op | source)
XLA Modules:
  0.0 97.3 jit_solution(12707319491176894272)
XLA Ops:
  0.6 0.0 copy-start.6
  0.6 2.3 %copy.48.u_ref = f32[4,128,360]{2,1,0:T(8,128)} copy(f32[4,128,360]{1,2,0:T(8,128)} %param.8) | data formatting | bytes 1474560 | tf_op args[0]
  3.0 0.0 copy-done.6
  3.0 1.2 %copy.49.v_ref = f32[4,128,360]{2,1,0:T(8,128)} copy(f32[4,128,360]{1,2,0:T(8,128)S(1)} %copy-done.6) | data formatting | bytes 1474560 | tf_op args[1]
  4.1 3.7 %pack.1 = f32[16,8,8,384]{3,2,1,0:T(8,128)} custom-call(f32[4,128,360]{2,1,0:T(8,128)} %copy.48.u_ref, f32[4,128,360]{2,1,0:T(8,128)} %copy.49.v_ref), custom_call_target="tpu_custom_call" | custom-call | tf_op jit(solution)/shard_map/pack/pallas_call | solution.py:89
  7.8 5.9 %all-to-all-start = ((f32[16,8,8,384]{3,2,1,0:T(8,128)}), f32[16,8,8,384]{3,2,1,0:T(8,128)S(1)}, u32[]{:S(2)}, u32[]{:S(2)}) async-start(f32[16,8,8,384]{3,2,1,0:T(8,128)} %pack.1), calls=%async_computation | async-start | bytes 3145728 | tf_op jit(solution)/shard_map/all_to_all | solution.py:270
  13.8 0.6 multiply_multiply_fusion.refs_1_
  14.4 21.4 %all-to-all-done.refs_0_ = f32[16,8,8,384]{3,2,1,0:T(8,128)S(1)} async-done(((f32[16,8,8,384]{3,2,1,0:T(8,128)}), f32[16,8,8,384]{3,2,1,0:T(8,128)S(1)}, u32[]{:S(2)}, u32[]{:S(2)}) %all-to-all-start) | async-done | bytes 1572896 | tf_op jit(solution)/shard_map/all_to_all | solution.py:270
  35.9 1.1 %copy-done.3 = f32[16,8,8,384]{3,2,1,0:T(8,128)} copy-done((f32[16,8,8,384]{3,2,1,0:T(8,128)}, f32[16,8,8,384]{3,2,1,0:T(8,128)S(1)}, u32[]{:S(2)}) %copy-start.3) | copy-done | bytes 1572888
  37.0 11.2 %polar_filter.1 = f32[16,8,8,384]{3,2,1,0:T(8,128)} custom-call(f32[16,8,8,384]{3,2,1,0:T(8,128)} %copy-done.3, f32[8,1]{1,0:T(8,128)} %multiply_multiply_fusion.refs_1_, bf16[768,768]{1,0:T(8,128)(2,1)} %constant.47.clone.refs_2_, bf16[768,768]{1,0:T(8,128)(2,1)} %constant.48.clone.refs_3_, f32[2,16,384]{2,1,0:T(8,128)} %constant.49.clone.refs_4_, ...), custom_call_target="tpu_custom_call" | custom-call | tf_op jit(solution)/shard_map/polar_filter/pallas_call | solution.py:173
  48.2 0.0 copy-start.1
  48.2 3.8 %all-to-all-start.1 = ((f32[16,8,8,384]{3,2,1,0:T(8,128)}), f32[16,8,8,384]{3,2,1,0:T(8,128)S(1)}, u32[]{:S(2)}, u32[]{:S(2)}) async-start(f32[16,8,8,384]{3,2,1,0:T(8,128)} %polar_filter.1), calls=%async_computation.1 | async-start | bytes 3145728 | tf_op jit(solution)/shard_map/all_to_all | solution.py:274
  52.0 0.0 copy-done.1
  52.0 0.0 copy-done.2
  52.1 2.1 %fusion = (f32[4,2,1,360]{2,3,1,0:T(8,128)}, f32[4,2,1,360]{2,3,1,0:T(8,128)}) fusion(f32[4,1,128,360]{2,3,1,0:T(8,128)S(1)} %bitcast.13, f32[4,1,128,360]{2,3,1,0:T(8,128)S(1)} %bitcast.15), kind=kLoop, calls=%fused_computation.6 | loop fusion | flops 5760 | bytes 1497600 | tf_op jit(solution)/shard_map/stack | solution.py:282
  54.1 1.8 %copy.69 = f32[4,2,1,360]{3,0,1,2:T(4,128)S(1)} copy(f32[4,2,1,360]{2,3,1,0:T(8,128)} %get-tuple-element.28) | data formatting | bytes 23040
  55.9 1.9 %copy.70 = f32[4,2,1,360]{3,0,1,2:T(4,128)S(1)} copy(f32[4,2,1,360]{2,3,1,0:T(8,128)} %get-tuple-element.29) | data formatting | bytes 23040
  57.8 3.9 %collective-permute-start.3 = (f32[4,2,360]{2,0,1:T(4,128)S(1)}, f32[4,2,360]{2,0,1:T(4,128)S(1)}, u32[]{:S(2)}, u32[]{:S(2)}) collective-permute-start(f32[4,2,360]{2,0,1:T(4,128)S(1)} %get-tuple-element.33), channel_id=1, source_target_pairs={{16,0},{17,1},{18,2},{19,3},{20,4},{21,5},{22,6},{23,7},{32,16},{3... | collective-permute-start | bytes 34568 | tf_op jit(solution)/shard_map/ppermute | solution.py:250
  61.7 0.0 collective-permute-start.2
  61.7 0.1 collective-permute-start.4
  61.8 3.8 %collective-permute-start.5 = (f32[4,2,128]{2,1,0:T(2,128)S(1)}, f32[4,2,128]{2,1,0:T(2,128)S(1)}, u32[]{:S(2)}, u32[]{:S(2)}) collective-permute-start(f32[4,2,128]{2,1,0:T(2,128)S(1)} %bitcast.22), channel_id=1, source_target_pairs={{1,0},{2,1},{3,2},{4,3},{5,4},{6,5},{7,6},{8,7},{9,8},{10,9},{11,1... | collective-permute-start | bytes 12296 | tf_op jit(solution)/shard_map/ppermute | solution.py:286
  65.7 0.1 sine_divide_fusion
  65.8 1.1 %copy.60.t_ref = f32[4,128,360]{2,1,0:T(8,128)} copy(f32[4,128,360]{1,2,0:T(8,128)S(1)} %copy-done.1) | data formatting | bytes 1474560 | tf_op args[2]
  66.9 1.2 %copy.61.q_ref = f32[4,128,360]{2,1,0:T(8,128)} copy(f32[4,128,360]{1,2,0:T(8,128)S(1)} %copy-done.2) | data formatting | bytes 1474560 | tf_op args[3]
  68.1 0.7 copy.54.row_ref
  68.8 5.1 %collective-permute-done.4 = f32[4,2,128]{2,1,0:T(2,128)S(1)} collective-permute-done((f32[4,2,128]{2,1,0:T(2,128)S(1)}, f32[4,2,128]{2,1,0:T(2,128)S(1)}, u32[]{:S(2)}, u32[]{:S(2)}) %collective-permute-start.4) | collective-permute-done | bytes 4128 | tf_op jit(solution)/shard_map/ppermute | solution.py:285
  73.9 0.0 collective-permute-done.5
  73.9 0.9 copy.59
  74.7 0.0 collective-permute-done.3
  74.7 0.0 collective-permute-done.2
  74.8 0.0 all-to-all-done.1.w_ref
  74.8 0.0 copy-start
  74.8 0.1 fusion.2
  74.9 3.7 %collective-permute-start = (f32[4,2,360]{2,0,1:T(4,128)S(1)}, f32[4,2,360]{2,0,1:T(4,128)S(1)}, u32[]{:S(2)}, u32[]{:S(2)}) collective-permute-start(f32[4,2,360]{2,0,1:T(4,128)S(1)} %copy.50), channel_id=1, source_target_pairs={{0,16},{1,17},{2,18},{3,19},{4,20},{5,21},{6,22},{7,23},{16,32},{1... | collective-permute-start | bytes 34568 | tf_op jit(solution)/shard_map/ppermute | solution.py:249
  78.6 0.9 collective-permute-start.1
  79.5 0.6 pad_maximum_fusion.1.edge_ref
  80.1 0.0 copy-done
  80.1 5.1 %tracers.1 = (f32[4,128,360]{2,1,0:T(8,128)}, f32[4,128,360]{2,1,0:T(8,128)}) custom-call(f32[4,128,360]{2,1,0:T(8,128)} %copy.60.t_ref, f32[4,128,360]{2,1,0:T(8,128)} %copy.61.q_ref, f32[16,8,8,384]{3,2,1,0:T(8,128)} %copy-done, f32[4,4,360]{2,1,0:T(4,128)} %pad_maximum_fusion.1.edge_ref, f32[4,128,4]{2,1,0:T(8,128)} %bitcast.17, f32[128,2]{1,0:T(8,128)} %copy.54.row_ref), custom_call_target="tpu_custom_call" | custom-call | tf_op jit(solution)/shard_map/tracers/pallas_call | solution.py:295
  85.2 2.3 %copy.65 = f32[4,128,360]{1,2,0:T(8,128)} copy(f32[4,128,360]{2,1,0:T(8,128)} %get-tuple-element.22) | data formatting | bytes 1474560
  87.6 0.0 copy-done.4
  87.6 1.1 %copy.66 = f32[4,128,360]{1,2,0:T(8,128)} copy(f32[4,128,360]{2,1,0:T(8,128)S(1)} %copy-done.4) | data formatting | bytes 1474560
  88.7 0.0 collective-permute-done
  88.7 0.0 collective-permute-done.1
  88.8 0.6 pad_maximum_fusion.edge_ref
  89.4 4.4 %winds.1 = (f32[4,128,360]{2,1,0:T(8,128)}, f32[4,128,360]{2,1,0:T(8,128)}) custom-call(f32[16,8,8,384]{3,2,1,0:T(8,128)} %copy-done, f32[4,4,360]{2,1,0:T(4,128)} %pad_maximum_fusion.edge_ref, f32[128,2]{1,0:T(8,128)} %copy.54.row_ref), custom_call_target="tpu_custom_call" | custom-call | tf_op jit(solution)/shard_map/winds/pallas_call | solution.py:306
  93.8 2.3 %copy.63 = f32[4,128,360]{1,2,0:T(8,128)} copy(f32[4,128,360]{2,1,0:T(8,128)} %get-tuple-element.20) | data formatting | bytes 1474560
  96.1 0.0 copy-done.5
  96.1 1.1 %copy.64 = f32[4,128,360]{1,2,0:T(8,128)} copy(f32[4,128,360]{2,1,0:T(8,128)S(1)} %copy-done.5) | data formatting | bytes 1474560
  (18 shorter events, 0.1 us)
Async XLA Ops:
  0.6 2.3 %copy-start.6 = (f32[4,128,360]{1,2,0:T(8,128)S(1)}, f32[4,128,360]{1,2,0:T(8,128)}, u32[]{:S(2)}) copy-start(f32[4,128,360]{1,2,0:T(8,128)} %param.9) | copy-start | bytes 2211844
  7.8 28.0 %all-to-all-start = ((f32[16,8,8,384]{3,2,1,0:T(8,128)}), f32[16,8,8,384]{3,2,1,0:T(8,128)S(1)}, u32[]{:S(2)}, u32[]{:S(2)}) async-start(f32[16,8,8,384]{3,2,1,0:T(8,128)} %pack.1), calls=%async_computation | async-start | bytes 3145728 | tf_op jit(solution)/shard_map/all_to_all | solution.py:270
  35.9 1.1 %copy-start.3 = (f32[16,8,8,384]{3,2,1,0:T(8,128)}, f32[16,8,8,384]{3,2,1,0:T(8,128)S(1)}, u32[]{:S(2)}) copy-start(f32[16,8,8,384]{3,2,1,0:T(8,128)S(1)} %all-to-all-done.refs_0_) | copy-start | bytes 4718596
  48.2 3.9 %copy-start.1 = (f32[4,128,360]{1,2,0:T(8,128)S(1)}, f32[4,128,360]{1,2,0:T(8,128)}, u32[]{:S(2)}) copy-start(f32[4,128,360]{1,2,0:T(8,128)} %param.10) | copy-start | bytes 2211844
  48.2 3.9 %copy-start.2 = (f32[4,128,360]{1,2,0:T(8,128)S(1)}, f32[4,128,360]{1,2,0:T(8,128)}, u32[]{:S(2)}) copy-start(f32[4,128,360]{1,2,0:T(8,128)} %param.11) | copy-start | bytes 2211844
  48.2 26.6 %all-to-all-start.1 = ((f32[16,8,8,384]{3,2,1,0:T(8,128)}), f32[16,8,8,384]{3,2,1,0:T(8,128)S(1)}, u32[]{:S(2)}, u32[]{:S(2)}) async-start(f32[16,8,8,384]{3,2,1,0:T(8,128)} %polar_filter.1), calls=%async_computation.1 | async-start | bytes 3145728 | tf_op jit(solution)/shard_map/all_to_all | solution.py:274
  57.8 16.9 %collective-permute-start.3 = (f32[4,2,360]{2,0,1:T(4,128)S(1)}, f32[4,2,360]{2,0,1:T(4,128)S(1)}, u32[]{:S(2)}, u32[]{:S(2)}) collective-permute-start(f32[4,2,360]{2,0,1:T(4,128)S(1)} %get-tuple-element.33), channel_id=1, source_target_pairs={{16,0},{17,1},{18,2},{19,3},{20,4},{21,5},{22,6},{23,7},{32,16},{3... | collective-permute-start | bytes 34568 | tf_op jit(solution)/shard_map/ppermute | solution.py:250
  61.7 13.0 %collective-permute-start.2 = (f32[4,2,360]{2,0,1:T(4,128)S(1)}, f32[4,2,360]{2,0,1:T(4,128)S(1)}, u32[]{:S(2)}, u32[]{:S(2)}) collective-permute-start(f32[4,2,360]{2,0,1:T(4,128)S(1)} %get-tuple-element.32), channel_id=1, source_target_pairs={{0,16},{1,17},{2,18},{3,19},{4,20},{5,21},{6,22},{7,23},{16,32},{1... | collective-permute-start | bytes 34568 | tf_op jit(solution)/shard_map/ppermute | solution.py:249
  61.7 12.1 %collective-permute-start.4 = (f32[4,2,128]{2,1,0:T(2,128)S(1)}, f32[4,2,128]{2,1,0:T(2,128)S(1)}, u32[]{:S(2)}, u32[]{:S(2)}) collective-permute-start(f32[4,2,128]{2,1,0:T(2,128)S(1)} %bitcast.23), channel_id=1, source_target_pairs={{0,1},{1,2},{2,3},{3,4},{4,5},{5,6},{6,7},{7,8},{8,9},{9,10},{10,1... | collective-permute-start | bytes 12296 | tf_op jit(solution)/shard_map/ppermute | solution.py:285
  61.8 12.0 %collective-permute-start.5 = (f32[4,2,128]{2,1,0:T(2,128)S(1)}, f32[4,2,128]{2,1,0:T(2,128)S(1)}, u32[]{:S(2)}, u32[]{:S(2)}) collective-permute-start(f32[4,2,128]{2,1,0:T(2,128)S(1)} %bitcast.22), channel_id=1, source_target_pairs={{1,0},{2,1},{3,2},{4,3},{5,4},{6,5},{7,6},{8,7},{9,8},{10,9},{11,1... | collective-permute-start | bytes 12296 | tf_op jit(solution)/shard_map/ppermute | solution.py:286
  74.8 5.3 %copy-start = (f32[16,8,8,384]{3,2,1,0:T(8,128)}, f32[16,8,8,384]{3,2,1,0:T(8,128)S(1)}, u32[]{:S(2)}) copy-start(f32[16,8,8,384]{3,2,1,0:T(8,128)S(1)} %all-to-all-done.1.w_ref) | copy-start | bytes 4718596
  74.9 13.8 %collective-permute-start = (f32[4,2,360]{2,0,1:T(4,128)S(1)}, f32[4,2,360]{2,0,1:T(4,128)S(1)}, u32[]{:S(2)}, u32[]{:S(2)}) collective-permute-start(f32[4,2,360]{2,0,1:T(4,128)S(1)} %copy.50), channel_id=1, source_target_pairs={{0,16},{1,17},{2,18},{3,19},{4,20},{5,21},{6,22},{7,23},{16,32},{1... | collective-permute-start | bytes 34568 | tf_op jit(solution)/shard_map/ppermute | solution.py:249
  78.6 10.1 %collective-permute-start.1 = (f32[4,2,360]{2,0,1:T(4,128)S(1)}, f32[4,2,360]{2,0,1:T(4,128)S(1)}, u32[]{:S(2)}, u32[]{:S(2)}) collective-permute-start(f32[4,2,360]{2,0,1:T(4,128)S(1)} %copy.51), channel_id=1, source_target_pairs={{16,0},{17,1},{18,2},{19,3},{20,4},{21,5},{22,6},{23,7},{32,16},{3... | collective-permute-start | bytes 34568 | tf_op jit(solution)/shard_map/ppermute | solution.py:250
  85.2 2.3 %copy-start.4 = (f32[4,128,360]{2,1,0:T(8,128)S(1)}, f32[4,128,360]{2,1,0:T(8,128)}, u32[]{:S(2)}) copy-start(f32[4,128,360]{2,1,0:T(8,128)} %get-tuple-element.23) | copy-start | bytes 2211844
  93.8 2.3 %copy-start.5 = (f32[4,128,360]{2,1,0:T(8,128)S(1)}, f32[4,128,360]{2,1,0:T(8,128)}, u32[]{:S(2)}) copy-start(f32[4,128,360]{2,1,0:T(8,128)} %get-tuple-element.21) | copy-start | bytes 2211844

commit v2 on v1

v2 whole, which is shorter than its diff:
```python
import math

import jax
import jax.numpy as jnp
import numpy as np
from jax import lax
from jax.experimental import pallas as pl
from jax.experimental.pallas import tpu as pltpu
from jax.sharding import Mesh
from jax.sharding import PartitionSpec as P

LON = ("lon_0", "lon_1", "lon_2")
ALL = ("lat",) + LON
ADV_COEF = 0.25
DIFF_COEF = 0.15
COS_CUT = math.cos(55.0 * math.pi / 180.0)
LANES = 128
SUB = 8
MIB = 1024 * 1024


def fourier_tables(parts, width, wide):
    points = parts * width
    m = np.arange(width)
    angle = 2.0 * np.pi * (np.outer(m, m) % width) / width
    matrix = np.zeros((2 * wide, 2 * wide))
    matrix[:width, :width] = np.cos(angle)
    matrix[:width, wide : wide + width] = -np.sin(angle)
    matrix[wide : wide + width, :width] = np.sin(angle)
    matrix[wide : wide + width, wide : wide + width] = np.cos(angle)
    high = matrix.astype(np.float32).astype(jnp.bfloat16)
    low = (matrix - high.astype(np.float64)).astype(np.float32).astype(jnp.bfloat16)
    k1 = np.arange(parts)
    turn = 2.0 * np.pi * np.outer(k1, m) / points
    twiddle = np.zeros((2, parts, wide), np.float32)
    twiddle[0, :, :width] = np.cos(turn)
    twiddle[1, :, :width] = -np.sin(turn)
    wave = k1[:, None] + parts * m[None, :]
    sine_sq = np.ones((parts, wide), np.float32)
    sine_sq[:, :width] = np.sin(np.pi * wave / points) ** 2
    return high, low, twiddle, sine_sq


def four_point(a, b, c, d):
    pr, pi = a[0] + c[0], a[1] + c[1]
    mr, mi = a[0] - c[0], a[1] - c[1]
    qr, qi = b[0] + d[0], b[1] + d[1]
    nr, ni = b[0] - d[0], b[1] - d[1]
    return (pr + qr, pi + qi), (mr + ni, mi - nr), (pr - qr, pi - qi), (mr - ni, mi + nr)


def turned(x, e):
    re, im = x
    if e == 0:
        return x
    if e == 4:
        return im, -re
    h = math.sqrt(0.5)
    if e == 2:
        return (re + im) * h, (im - re) * h
    if e == 6:
        return (im - re) * h, -(re + im) * h
    c, s = math.cos(2 * math.pi * e / 16), math.sin(2 * math.pi * e / 16)
    return re * c + im * s, im * c - re * s


def sixteen_point(x):
    inner = [four_point(x[s], x[4 + s], x[8 + s], x[12 + s]) for s in range(4)]
    out = [None] * 16
    for a in range(4):
        col = four_point(*[turned(inner[s][a], s * a) for s in range(4)])
        for b in range(4):
            out[a + 4 * b] = col[b]
    return out


def pack_kernel(u_ref, v_ref, out_ref):
    parts, _, sub, wide = out_ref.shape
    width, rows = u_ref.shape[1:]
    blank = jnp.zeros((wide - width, rows), jnp.float32)
    for i, ref in enumerate((u_ref, v_ref)):
        turned_rows = jnp.concatenate([ref[0], blank], axis=0).T
        out_ref[:, i] = turned_rows.reshape(parts, sub, wide)


def pack(u, v, parts, wide):
    levels, width, rows = u.shape
    sub = rows // parts
    spec = pl.BlockSpec((1, width, rows), lambda g: (g, 0, 0))
    return pl.pallas_call(
        pack_kernel,
        grid=(levels,),
        in_specs=[spec, spec],
        out_specs=pl.BlockSpec((parts, 2, sub, wide), lambda g: (0, g, 0, 0)),
        out_shape=jax.ShapeDtypeStruct((parts, 2 * levels, sub, wide), jnp.float32),
        name="pack",
    )(u, v)


def split_dot(x, high, low):
    top = x.astype(jnp.bfloat16)
    rest = (x - top.astype(jnp.float32)).astype(jnp.bfloat16)

    def dot(a, b):
        return jnp.dot(a, b, preferred_element_type=jnp.float32)

    return dot(top, high) + (dot(rest, high) + dot(top, low))


def damped_circles(width, load, store, finish, keep, tables, a_ref):
    high_ref, low_ref, twiddle_ref, sine_ref = tables
    parts, group, wide = a_ref.shape
    wide //= 2
    blocks = group // SUB
    spans = [slice(c, c + LANES) for c in range(0, wide, LANES)]
    points = parts * width

    def twisted(k, lanes, re, im):
        co = twiddle_ref[0, k : k + 1, lanes]
        si = twiddle_ref[1, k : k + 1, lanes]
        return re * co - im * si, re * si + im * co

    for lanes in spans:
        lanes_im = slice(wide + lanes.start, wide + lanes.stop)
        for i in range(blocks):
            rows = slice(i * SUB, (i + 1) * SUB)
            y = sixteen_point([load(i, d, lanes) for d in range(parts)])
            for k in range(parts):
                a_ref[k, rows, lanes], a_ref[k, rows, lanes_im] = twisted(k, lanes, *y[k])

    z = split_dot(a_ref[...].reshape(parts * group, 2 * wide), high_ref[...], low_ref[...])
    z = z.reshape(parts, blocks, SUB, 2 * wide)
    damping = keep / jnp.maximum(sine_ref[...][:, None, :], keep) * (1.0 / points)
    damping = damping[:, None]
    a_ref[:, :, :wide] = (z[..., :wide] * damping).reshape(parts, group, wide)
    a_ref[:, :, wide:] = (z[..., wide:] * -damping).reshape(parts, group, wide)
    z = split_dot(a_ref[...].reshape(parts * group, 2 * wide), high_ref[...], low_ref[...])
    a_ref[...] = z.reshape(parts, group, 2 * wide)

    for i in range(blocks):
        rows = slice(i * SUB, (i + 1) * SUB)
        for lanes in spans:
            lanes_im = slice(wide + lanes.start, wide + lanes.stop)
            y = sixteen_point(
                [twisted(k, lanes, a_ref[k, rows, lanes], a_ref[k, rows, lanes_im]) for k in range(parts)]
            )
            store(i, lanes, [[y[d][0] for d in range(parts)], [-y[d][1] for d in range(parts)]])
        finish(i)


def filter_kernel(
    width, x_ref, keep_ref, high_hbm, low_hbm, twiddle_ref, sine_ref, out_hbm, a_ref, high_ref, low_ref, out_ref, sems
):
    parts, planes, sub, wide = x_ref.shape
    loads = [
        pltpu.make_async_copy(high_hbm, high_ref, sems.at[0]),
        pltpu.make_async_copy(low_hbm, low_ref, sems.at[1]),
    ]
    for load in loads:
        load.start()
    tail = wide - LANES
    at = width - tail
    lane = lax.broadcasted_iota(jnp.int32, (sub, LANES), 1)
    stores = []

    def load_rows(i, d, lanes):
        return x_ref[d, 2 * i, :, lanes], x_ref[d, 2 * i + 1, :, lanes]

    def store_rows(i, lanes, values):
        for n in range(2):
            plane = 2 * i + n
            for d in range(parts):
                value = values[n][d]
                if lanes.start == tail:
                    west = pltpu.roll(values[n][(d - 1) % parts], LANES - at, 1)
                    east = pltpu.roll(out_ref[(d + 1) % parts, plane, :, :LANES], at, 1)
                    value = jnp.where(lane == LANES - 1, west, jnp.where(lane == at, east, value))
                out_ref[d, plane, :, lanes] = value

    def finish(i):
        pair = slice(2 * i, 2 * i + 2)
        stores.append(pltpu.make_async_copy(out_ref.at[:, pair], out_hbm.at[:, pair], sems.at[2 + i]))
        stores[-1].start()

    for load in loads:
        load.wait()
    keep = jnp.broadcast_to(keep_ref[...], (sub, wide))[None]
    tables = (high_ref, low_ref, twiddle_ref, sine_ref)
    damped_circles(width, load_rows, store_rows, finish, keep, tables, a_ref)
    for store in stores:
        store.wait()


def polar_filter(blocks, keep, tables, width):
    parts, planes, sub, wide = blocks.shape
    high, low, twiddle, sine_sq = tables
    whole = pl.BlockSpec(memory_space=pltpu.VMEM)
    apart = pl.BlockSpec(memory_space=pltpu.HBM)
    high, low = [pltpu.with_memory_space_constraint(x, pltpu.HBM) for x in (high, low)]
    return pl.pallas_call(
        lambda *refs: filter_kernel(width, *refs),
        in_specs=[whole, whole, apart, apart, whole, whole],
        out_specs=apart,
        out_shape=pltpu.HBM(blocks.shape, jnp.float32),
        scratch_shapes=[
            pltpu.VMEM((parts, planes // 2 * sub, 2 * wide), jnp.float32),
            pltpu.VMEM(high.shape, jnp.bfloat16),
            pltpu.VMEM(low.shape, jnp.bfloat16),
            pltpu.VMEM(blocks.shape, jnp.float32),
            pltpu.SemaphoreType.DMA((2 + planes // 2,)),
        ],
        compiler_params=pltpu.CompilerParams(vmem_limit_bytes=16 * MIB),
        name="polar_filter",
    )(blocks, keep, high, low, twiddle, sine_sq)


def edges_kernel(t_ref, q_ref, rows_out, first_out, last_out):
    levels, width, rows = t_ref.shape
    wide = rows_out.shape[1]
    count = 2 * levels
    lane = lax.broadcasted_iota(jnp.int32, (width, rows), 1)
    picked = jnp.zeros((width, rows), jnp.float32)
    for i, ref in enumerate((t_ref, q_ref)):
        for level in range(levels):
            plane = i * levels + level
            x = ref[level]
            first_out[plane : plane + 1] = x[:1]
            last_out[plane : plane + 1] = x[width - 1 :]
            first = pltpu.roll(x, plane, 1) if plane else x
            picked = jnp.where(lane == plane, first, picked)
            picked = jnp.where(lane == count + plane, pltpu.roll(x, count + plane + 1, 1), picked)
    blank = jnp.zeros((wide - width, rows), jnp.float32)
    rows_out[...] = jnp.concatenate([picked, blank], axis=0).T[: 2 * count]


def edges_of(t, q, wide):
    levels, width, rows = t.shape
    whole = pl.BlockSpec(memory_space=pltpu.VMEM)
    column = jax.ShapeDtypeStruct((2 * levels, rows), jnp.float32)
    return pl.pallas_call(
        edges_kernel,
        in_specs=[whole] * 2,
        out_specs=[whole] * 3,
        out_shape=[jax.ShapeDtypeStruct((4 * levels, wide), jnp.float32), column, column],
        compiler_params=pltpu.CompilerParams(vmem_limit_bytes=4 * MIB),
        name="edges",
    )(t, q)


def stepped(f, east, west, south, north, u, v, upper, lower):
    rows = f.shape[1]
    row = lax.broadcasted_iota(jnp.int32, f.shape, 1)
    above = jnp.where(row == rows - 1, north, pltpu.roll(f, rows - 1, 1))
    below = jnp.where(row == 0, south, pltpu.roll(f, 1, 1))
    advect = u * (east - west) * 0.5 + v * (above - below) * 0.5
    spread = (east - 2.0 * f + west) + (upper * (above - f) - lower * (f - below))
    return f - ADV_COEF * advect + DIFF_COEF * spread


def rims_of(south_ref, north_ref, planes):
    rims = [ref[pl.ds(plane, 1)] for plane in planes for ref in (south_ref, north_ref)]
    return jnp.concatenate(rims + rims, axis=0).T


def tracer_kernel(w_ref, t_ref, q_ref, south_ref, north_ref, west_ref, east_ref, row_ref, t_out, q_out):
    parts, _, sub, wide = w_ref.shape
    levels, (_, width, rows) = pl.num_programs(0), t_ref.shape
    level = pl.program_id(0)
    upper, lower = row_ref[0:1], row_ref[1:2]
    u, v = [w_ref[:, 2 * level + i].reshape(rows, wide).T[:width] for i in range(2)]
    rims = rims_of(south_ref, north_ref, (level, levels + level))
    at = lax.broadcasted_iota(jnp.int32, (width, rows), 0)
    for i, (ref, out) in enumerate(((t_ref, t_out), (q_ref, q_out))):
        f = ref[0]
        side = pl.ds(i * levels + level, 1)
        west = jnp.where(at == 0, west_ref[side], pltpu.roll(f, 1, 0))
        east = jnp.where(at == width - 1, east_ref[side], pltpu.roll(f, width - 1, 0))
        south, north = rims[:width, 2 * i : 2 * i + 1], rims[:width, 2 * i + 1 : 2 * i + 2]
        out[0] = stepped(f, east, west, south, north, u, v, upper, lower)


def wind_kernel(w_ref, south_ref, north_ref, row_ref, u_out, v_out):
    parts, _, sub, wide = w_ref.shape
    width, rows = u_out.shape[1:]
    level = pl.program_id(0)
    upper, lower = row_ref[0:1], row_ref[1:2]
    full = [w_ref[:, 2 * level + i].reshape(rows, wide).T for i in range(2)]
    u, v = [x[:width] for x in full]
    rims = rims_of(south_ref, north_ref, (2 * level, 2 * level + 1))
    for i, out in enumerate((u_out, v_out)):
        west = pltpu.roll(full[i], 1, 0)[:width]
        east = pltpu.roll(full[i], wide - 1, 0)[:width]
        south, north = rims[:width, 2 * i : 2 * i + 1], rims[:width, 2 * i + 1 : 2 * i + 2]
        out[0] = stepped((u, v)[i], east, west, south, north, u, v, upper, lower)


def beyond_band(first, last, band, bands, z_low, sign):
    lon_rest = lax.axis_size(LON) // 2

    def place(step):
        half, at = divmod(step % (2 * bands), bands)
        return half, (at if half == 0 else bands - 1 - at)

    pairs = []
    for step in range(2 * bands):
        for rest in range(lon_rest):
            (h0, b0), (h1, b1) = place(step), place(step + 1)
            pairs.append(((b0 * 2 + h0) * lon_rest + rest, (b1 * 2 + h1) * lon_rest + rest))
    onward = jnp.where(z_low == 0, last, first)
    backward = jnp.where(z_low == 0, first, last)
    from_before = lax.ppermute(onward, ALL, pairs)
    from_after = lax.ppermute(backward, ALL, [(b, a) for a, b in pairs])
    south = jnp.where(z_low == 0, from_before, from_after)
    north = jnp.where(z_low == 0, from_after, from_before)
    south = jnp.where(band == 0, sign * south, south)
    north = jnp.where(band == bands - 1, sign * north, north)
    return south, north


def on_device(east_flow_speed, north_flow_speed, thermal_anomaly, moisture_anomaly):
    levels, rows, width = east_flow_speed.shape
    bands = lax.axis_size("lat")
    parts = lax.axis_size(LON)
    total_rows = rows * bands
    band = lax.axis_index("lat")
    column = lax.axis_index(LON)
    z_low = lax.axis_index("lon_0")
    wide = -(-(width + 2) // LANES) * LANES
    sub = rows // parts
    count = 2 * levels
    tables = [jnp.asarray(x) for x in fourier_tables(parts, width, wide)]
    u, v, t, q = [
        jnp.swapaxes(x, 1, 2)
        for x in (east_flow_speed, north_flow_speed, thermal_anomaly, moisture_anomaly)
    ]

    sent = pack(u, v, parts, wide)
    circles = lax.all_to_all(sent, LON, split_axis=0, concat_axis=0, tiled=True)

    edge_rows, firsts, lasts = edges_of(t, q, wide)
    south, north = beyond_band(edge_rows[:count], edge_rows[count:], band, bands, z_low, 1.0)
    ring = [(i, (i + 1) % parts) for i in range(parts)]
    west = lax.ppermute(lasts, LON, ring)
    east = lax.ppermute(firsts, LON, [(b, a) for a, b in ring])

    circles, south, north, west, east = lax.optimization_barrier((circles, south, north, west, east))
    own_rows = (band * rows + column * sub + jnp.arange(sub, dtype=jnp.int32)).astype(jnp.float32)
    keep = (jnp.sin((own_rows + 0.5) * (math.pi / total_rows)) / COS_CUT) ** 2
    filtered = polar_filter(circles, keep[:, None], tables, width)
    winds = lax.all_to_all(filtered, LON, split_axis=0, concat_axis=0, tiled=True)

    row_index = (band * rows + jnp.arange(rows, dtype=jnp.int32)).astype(jnp.float32)
    centre = jnp.sin((row_index + 0.5) * (math.pi / total_rows))
    lower_edge = jnp.sin(row_index * (math.pi / total_rows))
    upper_edge = jnp.sin((row_index + 1.0) * (math.pi / total_rows))
    factors = jnp.stack([upper_edge / centre, lower_edge / centre], axis=0)

    field = pl.BlockSpec((1, width, rows), lambda g: (g, 0, 0))
    whole = pl.BlockSpec(memory_space=pltpu.VMEM)
    shape = jax.ShapeDtypeStruct((levels, width, rows), jnp.float32)

    def all_of(x):
        return pl.BlockSpec(x.shape, lambda g: (0, 0))

    by_rows = [winds[at, :, row].reshape(levels, 2, wide) for at, row in ((0, 0), (-1, -1))]
    wind_rims = [x.reshape(2 * levels, wide) for x in beyond_band(*by_rows, band, bands, z_low, -1.0)]
    small = (south, north, west, east, factors)
    next_t, next_q = pl.pallas_call(
        tracer_kernel,
        grid=(levels,),
        in_specs=[whole, field, field] + [all_of(x) for x in small],
        out_specs=[field] * 2,
        out_shape=[shape] * 2,
        compiler_params=pltpu.CompilerParams(vmem_limit_bytes=12 * MIB),
        name="tracers",
    )(winds, t, q, *small)
    small = (*wind_rims, factors)
    next_u, next_v = pl.pallas_call(
        wind_kernel,
        grid=(levels,),
        in_specs=[whole] + [all_of(x) for x in small],
        out_specs=[field] * 2,
        out_shape=[shape] * 2,
        compiler_params=pltpu.CompilerParams(vmem_limit_bytes=12 * MIB),
        name="winds",
    )(winds, *small)
    return tuple(jnp.swapaxes(x, 1, 2) for x in (next_u, next_v, next_t, next_q))


def solution(mesh):
    torus = Mesh(
        mesh.devices.reshape(mesh.shape["lat"], 2, 4, 2), ("lat", "lon_0", "lon_1", "lon_2")
    )
    placed = (P(None, "lat", LON),) * 4
    return jax.shard_map(
        on_device, mesh=torus, in_specs=placed, out_specs=placed, check_vma=False
    )
```

time: 97.9 us -> 83.5 us (0.85)
  local copies, waits for them, and re-layouts: 19.2 us -> 0.07 us
  waiting for transfers between devices: 26.5 us -> 34.9 us
  other arithmetic: 4.13 us -> 0.22 us
  starting transfers between devices: 22.2 us -> 24.3 us
  Pallas kernels: 24.4 us -> 22.9 us
    all_to_all x1, waiting for transfers between devices: 0.01 us -> 22 us  [on_device(): lax.all_to_all(filtered, LON, split_axis=0, concat_axis=0, tiled=True)]
    all_to_all x1, waiting for transfers between devices: 21.4 us -> 0.28 us  [on_device(): circles = lax.all_to_all(sent, LON, split_axis=0, concat_axis=0, tiled=True)]
    unnamed x24 -> x8, local copies, waits for them, and re-layouts: 17.6 us -> 0.02 us
    ppermute x6, waiting for transfers between devices: 5.08 us -> 12.6 us  [the longest x2 10.6 us: beyond_band(): from_after = lax.ppermute(backward, ALL, [(b, a) for a, b in pairs])]
    another operation x3 -> x1, other arithmetic: 2.07 us -> 0.01 us  [on_device(): factors = jnp.stack([upper_edge / centre, lower_edge / centre], axis=0)]
    pallas_call x3 -> x4, Pallas kernels: 20.7 us -> 18.9 us  [the longest x1 10.7 us: polar_filter(): pl.pallas_call(lambda *refs: filter_kernel(width, *refs), in_specs=[whole...]
    all_to_all x1, starting transfers between devices: 3.84 us -> 5.34 us  [on_device(): lax.all_to_all(filtered, LON, split_axis=0, concat_axis=0, tiled=True)]
    concatenate x3 -> x0, other arithmetic: 1.25 us -> none  [the longest x2 1.25 us: lat_edges(): return jnp.concatenate([south, north], axis=1)]
  transfers between devices with their start and end apart: 8 -> 8, of which waited for: 2 -> 5; matrix products, arithmetic and copies ran while one was open for 15% -> 0% of each run, Pallas kernels for 5% -> 6%
where the time goes in v2:
time: 83.5 us; the launch traced here: 83.1 us
  waiting for transfers between devices  34.9 us (42%)
  starting transfers between devices  24.3 us (29%)
  Pallas kernels  22.9 us (27%)
    all_to_all x1, waiting for transfers between devices, on_device(): lax.all_to_all(filtered, LON, split_axis=0, concat_axis=0, tiled=True)  22 us
    pallas_call x1, Pallas kernels, polar_filter(): pl.pallas_call(lambda *refs: filter_kernel(width, *refs), in_specs=[whole...  10.7 us
    ppermute x2, waiting for transfers between devices, beyond_band(): from_after = lax.ppermute(backward, ALL, [(b, a) for a, b in pairs])  10.6 us
    all_to_all x1, starting transfers between devices, on_device(): circles = lax.all_to_all(sent, LON, split_axis=0, concat_axis=0, tiled=True)  6.06 us
    ppermute x2, starting transfers between devices, beyond_band(): from_before = lax.ppermute(onward, ALL, pairs)  5.63 us
    all_to_all x1, starting transfers between devices, on_device(): lax.all_to_all(filtered, LON, split_axis=0, concat_axis=0, tiled=True)  5.34 us
    pallas_call x1, Pallas kernels, pack(): pl.pallas_call(pack_kernel, grid=(levels,), in_specs=[spec, spec], out_sp...  3.99 us
    ppermute x1, starting transfers between devices, on_device(): east = lax.ppermute(firsts, LON, [(b, a) for a, b in ring])  3.85 us
  transfers between devices with their start and end apart: 8, of which 5 were waited for; matrix products, arithmetic and copies ran while one was open for 0% of the time, Pallas kernels for 6%

profile of v2, /device:TPU:6, one launch (start us, length us, event | category | flops | bytes accessed | tf_op | source)
XLA Modules:
  0.0 83.1 jit_solution(9522073237666416808)
XLA Ops:
  0.6 4.0 %pack.1 = f32[16,8,8,384]{3,2,1,0:T(8,128)} custom-call(f32[4,360,128]{2,1,0:T(8,128)} %bitcast.12, f32[4,360,128]{2,1,0:T(8,128)} %bitcast.13), custom_call_target="tpu_custom_call" | custom-call | tf_op jit(solution)/shard_map/pack/pallas_call | solution.py:90
  4.6 0.0 copy-start
  4.6 0.0 copy-start.1
  4.6 6.1 %all-to-all-start = ((f32[16,8,8,384]{3,2,1,0:T(8,128)}), f32[16,8,8,384]{3,2,1,0:T(8,128)S(1)}, u32[]{:S(2)}, u32[]{:S(2)}) async-start(f32[16,8,8,384]{3,2,1,0:T(8,128)} %pack.1), calls=%async_computation | async-start | bytes 3145728 | tf_op jit(solution)/shard_map/all_to_all | solution.py:338
  10.7 0.0 copy-start.2
  10.7 0.0 copy-start.3
  10.7 0.0 copy-done
  10.7 0.0 copy-done.1
  10.7 0.9 %edges.1 = (f32[16,384]{1,0:T(8,128)S(1)}, f32[8,128]{1,0:T(8,128)S(1)}, f32[8,128]{1,0:T(8,128)S(1)}) custom-call(f32[4,360,128]{2,1,0:T(8,128)S(1)} %bitcast.8, f32[4,360,128]{2,1,0:T(8,128)S(1)} %bitcast.10), custom_call_target="tpu_custom_call" | custom-call | tf_op jit(solution)/shard_map/edges/pallas_call | solution.py:240
  11.6 3.6 %collective-permute-start = (f32[8,384]{1,0:T(8,128)S(1)}, f32[8,384]{1,0:T(8,128)S(1)}, u32[]{:S(2)}, u32[]{:S(2)}) collective-permute-start(f32[8,384]{1,0:T(8,128)S(1)} %get-tuple-element.35), channel_id=1, source_target_pairs={{0,16},{1,17},{2,18},{3,19},{4,20},{5,21},{6,22},{7,23},{16,32},{1... | collective-permute-start | bytes 36872 | tf_op jit(solution)/shard_map/ppermute | solution.py:311
  15.2 0.8 %collective-permute-start.1 = (f32[8,384]{1,0:T(8,128)S(1)}, f32[8,384]{1,0:T(8,128)S(1)}, u32[]{:S(2)}, u32[]{:S(2)}) collective-permute-start(f32[8,384]{1,0:T(8,128)S(1)} %get-tuple-element.34), channel_id=1, source_target_pairs={{16,0},{17,1},{18,2},{19,3},{20,4},{21,5},{22,6},{23,7},{32,16},{3... | collective-permute-start | bytes 36872 | tf_op jit(solution)/shard_map/ppermute | solution.py:312
  16.1 0.0 collective-permute-start.2
  16.1 3.9 %collective-permute-start.3 = (f32[8,128]{1,0:T(8,128)S(1)}, f32[8,128]{1,0:T(8,128)S(1)}, u32[]{:S(2)}, u32[]{:S(2)}) collective-permute-start(f32[8,128]{1,0:T(8,128)S(1)} %get-tuple-element.18), channel_id=1, source_target_pairs={{1,0},{2,1},{3,2},{4,3},{5,4},{6,5},{7,6},{8,7},{9,8},{10,9},{11,1... | collective-permute-start | bytes 12296 | tf_op jit(solution)/shard_map/ppermute | solution.py:344
  20.0 1.2 %collective-permute-done = f32[8,384]{1,0:T(8,128)S(1)} collective-permute-done((f32[8,384]{1,0:T(8,128)S(1)}, f32[8,384]{1,0:T(8,128)S(1)}, u32[]{:S(2)}, u32[]{:S(2)}) %collective-permute-start) | collective-permute-done | bytes 12320 | tf_op jit(solution)/shard_map/ppermute | solution.py:311
  21.2 10.6 %collective-permute-done.1 = f32[8,384]{1,0:T(8,128)S(1)} collective-permute-done((f32[8,384]{1,0:T(8,128)S(1)}, f32[8,384]{1,0:T(8,128)S(1)}, u32[]{:S(2)}, u32[]{:S(2)}) %collective-permute-start.1) | collective-permute-done | bytes 12320 | tf_op jit(solution)/shard_map/ppermute | solution.py:312
  31.8 0.7 collective-permute-done.2.west_ref
  32.5 0.0 collective-permute-done.3.east_ref
  32.6 0.3 all-to-all-done.refs_0_
  32.8 0.0 copy-done.2
  32.8 0.0 copy-done.3
  32.8 10.7 %polar_filter.1 = f32[16,8,8,384]{3,2,1,0:T(8,128)} custom-call(f32[16,8,8,384]{3,2,1,0:T(8,128)S(1)} %all-to-all-done.refs_0_, f32[8,1]{1,0:T(8,128)S(1)} %multiply_multiply_fusion.refs_1_, bf16[768,768]{1,0:T(8,128)(2,1)} %constant.47.clone.refs_2_, bf16[768,768]{1,0:T(8,128)(2,1)} %constant.48.clone.refs_3_, f32[2,16,384]{2,1,0:T(8,128)S(1)} %copy-done.2, ...), custom_call_target="tpu_custom_call" | custom-call | tf_op jit(solution)/shard_map/polar_filter/pallas_call | solution.py:200
  43.5 5.3 %all-to-all-start.1 = ((f32[16,8,8,384]{3,2,1,0:T(8,128)}), f32[16,8,8,384]{3,2,1,0:T(8,128)S(1)}, u32[]{:S(2)}, u32[]{:S(2)}) async-start(f32[16,8,8,384]{3,2,1,0:T(8,128)} %polar_filter.1), calls=%async_computation.1 | async-start | bytes 3145728 | tf_op jit(solution)/shard_map/all_to_all | solution.py:350
  48.9 0.1 sine_divide_fusion
  49.0 22.0 %all-to-all-done.1.w_ref = f32[16,8,8,384]{3,2,1,0:T(8,128)S(1)} async-done(((f32[16,8,8,384]{3,2,1,0:T(8,128)}), f32[16,8,8,384]{3,2,1,0:T(8,128)S(1)}, u32[]{:S(2)}, u32[]{:S(2)}) %all-to-all-start.1) | async-done | bytes 1572896 | tf_op jit(solution)/shard_map/all_to_all | solution.py:350
  71.0 0.1 fusion.1
  71.1 2.0 %collective-permute-start.4 = (f32[4,2,384]{2,1,0:T(2,128)S(1)}, f32[4,2,384]{2,1,0:T(2,128)S(1)}, u32[]{:S(2)}, u32[]{:S(2)}) collective-permute-start(f32[4,2,384]{2,1,0:T(2,128)S(1)} %select_n.73), channel_id=1, source_target_pairs={{0,16},{1,17},{2,18},{3,19},{4,20},{5,21},{6,22},{7,23},{16,32},{1... | collective-permute-start | bytes 36872 | tf_op jit(solution)/shard_map/ppermute | solution.py:311
  73.1 2.6 %collective-permute-start.5 = (f32[4,2,384]{2,1,0:T(2,128)S(1)}, f32[4,2,384]{2,1,0:T(2,128)S(1)}, u32[]{:S(2)}, u32[]{:S(2)}) collective-permute-start(f32[4,2,384]{2,1,0:T(2,128)S(1)} %select_n.75), channel_id=1, source_target_pairs={{16,0},{17,1},{18,2},{19,3},{20,4},{21,5},{22,6},{23,7},{32,16},{3... | collective-permute-start | bytes 36872 | tf_op jit(solution)/shard_map/ppermute | solution.py:312
  75.7 3.8 %tracers.1 = (f32[4,360,128]{2,1,0:T(8,128)}, f32[4,360,128]{2,1,0:T(8,128)}) custom-call(f32[16,8,8,384]{3,2,1,0:T(8,128)S(1)} %all-to-all-done.1.w_ref, f32[4,360,128]{2,1,0:T(8,128)S(1)} %bitcast.9, f32[4,360,128]{2,1,0:T(8,128)S(1)} %bitcast.11, f32[8,384]{1,0:T(8,128)S(1)} %get-tuple-element.22.south_ref, f32[8,384]{1,0:T(8,128)S(1)} %get-tuple-element.23.north_ref, ...), custom_call_target="tpu_custom_call" | custom-call | tf_op jit(solution)/shard_map/tracers/pallas_call | solution.py:368
  79.5 0.0 collective-permute-done.4
  79.5 0.0 collective-permute-done.5
  79.5 3.6 %winds.1 = (f32[4,360,128]{2,1,0:T(8,128)}, f32[4,360,128]{2,1,0:T(8,128)}) custom-call(f32[16,8,8,384]{3,2,1,0:T(8,128)S(1)} %all-to-all-done.1.w_ref, f32[8,384]{1,0:T(8,128)S(1)} %reshape.84.south_ref, f32[8,384]{1,0:T(8,128)S(1)} %reshape.85.north_ref, f32[2,128]{1,0:T(2,128)S(1)} %pad_maximum_fusion.row_ref), custom_call_target="tpu_custom_call" | custom-call | tf_op jit(solution)/shard_map/winds/pallas_call | solution.py:378
  (9 shorter events, 0.1 us)
Async XLA Ops:
  4.6 6.1 %copy-start = (f32[4,128,360]{1,2,0:T(8,128)S(1)}, f32[4,128,360]{1,2,0:T(8,128)}, u32[]{:S(2)}) copy-start(f32[4,128,360]{1,2,0:T(8,128)} %param.10) | copy-start | bytes 2211844
  4.6 6.1 %copy-start.1 = (f32[4,128,360]{1,2,0:T(8,128)S(1)}, f32[4,128,360]{1,2,0:T(8,128)}, u32[]{:S(2)}) copy-start(f32[4,128,360]{1,2,0:T(8,128)} %param.11) | copy-start | bytes 2211844
  4.6 28.2 %all-to-all-start = ((f32[16,8,8,384]{3,2,1,0:T(8,128)}), f32[16,8,8,384]{3,2,1,0:T(8,128)S(1)}, u32[]{:S(2)}, u32[]{:S(2)}) async-start(f32[16,8,8,384]{3,2,1,0:T(8,128)} %pack.1), calls=%async_computation | async-start | bytes 3145728 | tf_op jit(solution)/shard_map/all_to_all | solution.py:338
  10.7 22.1 %copy-start.2 = (f32[2,16,384]{2,1,0:T(8,128)S(1)}, f32[2,16,384]{2,1,0:T(8,128)}, u32[]{:S(2)}) copy-start(f32[2,16,384]{2,1,0:T(8,128)} %constant.49.clone.refs_4_) | copy-start | bytes 147460
  10.7 22.1 %copy-start.3 = (f32[16,384]{1,0:T(8,128)S(1)}, f32[16,384]{1,0:T(8,128)}, u32[]{:S(2)}) copy-start(f32[16,384]{1,0:T(8,128)} %constant.50.clone.refs_5_) | copy-start | bytes 73732
  11.6 9.6 %collective-permute-start = (f32[8,384]{1,0:T(8,128)S(1)}, f32[8,384]{1,0:T(8,128)S(1)}, u32[]{:S(2)}, u32[]{:S(2)}) collective-permute-start(f32[8,384]{1,0:T(8,128)S(1)} %get-tuple-element.35), channel_id=1, source_target_pairs={{0,16},{1,17},{2,18},{3,19},{4,20},{5,21},{6,22},{7,23},{16,32},{1... | collective-permute-start | bytes 36872 | tf_op jit(solution)/shard_map/ppermute | solution.py:311
  15.2 16.6 %collective-permute-start.1 = (f32[8,384]{1,0:T(8,128)S(1)}, f32[8,384]{1,0:T(8,128)S(1)}, u32[]{:S(2)}, u32[]{:S(2)}) collective-permute-start(f32[8,384]{1,0:T(8,128)S(1)} %get-tuple-element.34), channel_id=1, source_target_pairs={{16,0},{17,1},{18,2},{19,3},{20,4},{21,5},{22,6},{23,7},{32,16},{3... | collective-permute-start | bytes 36872 | tf_op jit(solution)/shard_map/ppermute | solution.py:312
  16.1 16.5 %collective-permute-start.2 = (f32[8,128]{1,0:T(8,128)S(1)}, f32[8,128]{1,0:T(8,128)S(1)}, u32[]{:S(2)}, u32[]{:S(2)}) collective-permute-start(f32[8,128]{1,0:T(8,128)S(1)} %get-tuple-element.17), channel_id=1, source_target_pairs={{0,1},{1,2},{2,3},{3,4},{4,5},{5,6},{6,7},{7,8},{8,9},{9,10},{10,1... | collective-permute-start | bytes 12296 | tf_op jit(solution)/shard_map/ppermute | solution.py:343
  16.1 16.5 %collective-permute-start.3 = (f32[8,128]{1,0:T(8,128)S(1)}, f32[8,128]{1,0:T(8,128)S(1)}, u32[]{:S(2)}, u32[]{:S(2)}) collective-permute-start(f32[8,128]{1,0:T(8,128)S(1)} %get-tuple-element.18), channel_id=1, source_target_pairs={{1,0},{2,1},{3,2},{4,3},{5,4},{6,5},{7,6},{8,7},{9,8},{10,9},{11,1... | collective-permute-start | bytes 12296 | tf_op jit(solution)/shard_map/ppermute | solution.py:344
  43.5 27.4 %all-to-all-start.1 = ((f32[16,8,8,384]{3,2,1,0:T(8,128)}), f32[16,8,8,384]{3,2,1,0:T(8,128)S(1)}, u32[]{:S(2)}, u32[]{:S(2)}) async-start(f32[16,8,8,384]{3,2,1,0:T(8,128)} %polar_filter.1), calls=%async_computation.1 | async-start | bytes 3145728 | tf_op jit(solution)/shard_map/all_to_all | solution.py:350
  71.1 8.4 %collective-permute-start.4 = (f32[4,2,384]{2,1,0:T(2,128)S(1)}, f32[4,2,384]{2,1,0:T(2,128)S(1)}, u32[]{:S(2)}, u32[]{:S(2)}) collective-permute-start(f32[4,2,384]{2,1,0:T(2,128)S(1)} %select_n.73), channel_id=1, source_target_pairs={{0,16},{1,17},{2,18},{3,19},{4,20},{5,21},{6,22},{7,23},{16,32},{1... | collective-permute-start | bytes 36872 | tf_op jit(solution)/shard_map/ppermute | solution.py:311
  73.1 6.4 %collective-permute-start.5 = (f32[4,2,384]{2,1,0:T(2,128)S(1)}, f32[4,2,384]{2,1,0:T(2,128)S(1)}, u32[]{:S(2)}, u32[]{:S(2)}) collective-permute-start(f32[4,2,384]{2,1,0:T(2,128)S(1)} %select_n.75), channel_id=1, source_target_pairs={{16,0},{17,1},{18,2},{19,3},{20,4},{21,5},{22,6},{23,7},{32,16},{3... | collective-permute-start | bytes 36872 | tf_op jit(solution)/shard_map/ppermute | solution.py:312

commit v3 on v2

v3 whole, which is shorter than its diff:
```python
import math

import jax
import jax.numpy as jnp
import numpy as np
from jax import lax
from jax.experimental import pallas as pl
from jax.experimental.pallas import tpu as pltpu
from jax.sharding import Mesh
from jax.sharding import PartitionSpec as P

LON = ("lon_0", "lon_1", "lon_2")
ALL = ("lat",) + LON
ADV_COEF = 0.25
DIFF_COEF = 0.15
COS_CUT = math.cos(55.0 * math.pi / 180.0)
LANES = 128
THIRDS = 3
AT_ONCE = 2
MIB = 1024 * 1024


def fourier_tables(parts, width):
    points, many, short = parts * width, THIRDS * parts, width // THIRDS
    m = np.arange(short)
    angle = 2.0 * np.pi * (np.outer(m, m) % short) / short
    matrix = np.zeros((2 * LANES, 2 * LANES))
    matrix[:short, :short] = np.cos(angle)
    matrix[:short, LANES : LANES + short] = -np.sin(angle)
    matrix[LANES : LANES + short, :short] = np.sin(angle)
    matrix[LANES : LANES + short, LANES : LANES + short] = np.cos(angle)
    high = matrix.astype(np.float32).astype(jnp.bfloat16)
    low = (matrix - high.astype(np.float64)).astype(np.float32).astype(jnp.bfloat16)
    stacked = np.concatenate([high, high, low], axis=0)
    k1 = np.arange(many)
    turn = 2.0 * np.pi * np.outer(k1, m) / points
    twiddle = np.zeros((2, many, LANES), np.float32)
    twiddle[0, :, :short] = np.cos(turn)
    twiddle[1, :, :short] = -np.sin(turn)
    wave = k1[:, None] + many * m[None, :]
    sine_sq = np.ones((many, LANES), np.float32)
    sine_sq[:, :short] = np.sin(np.pi * wave / points) ** 2
    return stacked, twiddle, sine_sq


def four_point(a, b, c, d):
    pr, pi = a[0] + c[0], a[1] + c[1]
    mr, mi = a[0] - c[0], a[1] - c[1]
    qr, qi = b[0] + d[0], b[1] + d[1]
    nr, ni = b[0] - d[0], b[1] - d[1]
    return (pr + qr, pi + qi), (mr + ni, mi - nr), (pr - qr, pi - qi), (mr - ni, mi + nr)


def turned(x, e):
    re, im = x
    if e == 0:
        return x
    if e == 4:
        return im, -re
    h = math.sqrt(0.5)
    if e == 2:
        return (re + im) * h, (im - re) * h
    if e == 6:
        return (im - re) * h, -(re + im) * h
    c, s = math.cos(2 * math.pi * e / 16), math.sin(2 * math.pi * e / 16)
    return re * c + im * s, im * c - re * s


def sixteen_point(x):
    inner = [four_point(x[s], x[4 + s], x[8 + s], x[12 + s]) for s in range(4)]
    out = [None] * 16
    for a in range(4):
        col = four_point(*[turned(inner[s][a], s * a) for s in range(4)])
        for b in range(4):
            out[a + 4 * b] = col[b]
    return out


def three_point(a, b, c):
    h = math.sqrt(0.75)
    sr, si = b[0] + c[0], b[1] + c[1]
    dr, di = (b[0] - c[0]) * h, (b[1] - c[1]) * h
    mr, mi = a[0] - 0.5 * sr, a[1] - 0.5 * si
    return (a[0] + sr, a[1] + si), (mr + di, mi - dr), (mr - di, mi + dr)


def many_point(x):
    inner = [sixteen_point(x[e::THIRDS]) for e in range(THIRDS)]
    out = [None] * len(x)
    for a in range(16):
        col = [inner[0][a]]
        for e in (1, 2):
            re, im = inner[e][a]
            co, si = math.cos(2 * math.pi * e * a / 48), math.sin(2 * math.pi * e * a / 48)
            col.append((re * co + im * si, im * co - re * si) if a else (re, im))
        for b, value in enumerate(three_point(*col)):
            out[a + 16 * b] = value
    return out


def pack_kernel(u_ref, v_ref, out_ref):
    parts, _, sub, wide = out_ref.shape
    count, width, rows = u_ref.shape
    short = width // THIRDS
    blank = jnp.zeros((LANES - short, rows), jnp.float32)
    for level in range(count):
        for i, ref in enumerate((u_ref, v_ref)):
            for e in range(THIRDS):
                piece = ref[level, e * short : (e + 1) * short]
                piece = jnp.concatenate([piece, blank], axis=0).T.reshape(parts, sub, LANES)
                out_ref[:, 2 * level + i, :, e * LANES : (e + 1) * LANES] = piece


def pack(u, v, parts, wide):
    levels, width, rows = u.shape
    sub = rows // parts
    spec = pl.BlockSpec((AT_ONCE, width, rows), lambda g: (g, 0, 0))
    return pl.pallas_call(
        pack_kernel,
        grid=(levels // AT_ONCE,),
        in_specs=[spec, spec],
        out_specs=pl.BlockSpec((parts, 2 * AT_ONCE, sub, wide), lambda g: (0, g, 0, 0)),
        out_shape=jax.ShapeDtypeStruct((parts, 2 * levels, sub, wide), jnp.float32),
        compiler_params=pltpu.CompilerParams(vmem_limit_bytes=8 * MIB),
        name="pack",
    )(u, v)


def split_dot(x, stacked):
    top = x.astype(jnp.bfloat16)
    rest = (x - top.astype(jnp.float32)).astype(jnp.bfloat16)
    return jnp.dot(
        jnp.concatenate([top, rest, top], axis=1), stacked, preferred_element_type=jnp.float32
    )


def filter_kernel(width, x_ref, keep_ref, stacked_ref, twiddle_ref, sine_ref, out_hbm, a_ref, out_ref, sems):
    parts, planes, sub, wide = x_ref.shape
    many, group, _ = a_ref.shape
    levels = planes // 2
    points, short = parts * width, width // THIRDS
    real, imag = slice(0, LANES), slice(LANES, 2 * LANES)
    spans = [slice(e * LANES, (e + 1) * LANES) for e in range(THIRDS)]
    lane = lax.broadcasted_iota(jnp.int32, (sub, LANES), 1)

    def twisted(k, re, im):
        co, si = twiddle_ref[0, k : k + 1], twiddle_ref[1, k : k + 1]
        return re * co - im * si, re * si + im * co

    for level in range(levels):
        rows = slice(level * sub, (level + 1) * sub)
        y = many_point(
            [
                (x_ref[d, 2 * level, :, lanes], x_ref[d, 2 * level + 1, :, lanes])
                for d in range(parts)
                for lanes in spans
            ]
        )
        for k in range(many):
            a_ref[k, rows, real], a_ref[k, rows, imag] = twisted(k, *y[k])

    z = split_dot(a_ref[...].reshape(many * group, 2 * LANES), stacked_ref[...])
    z = z.reshape(many, levels, sub, 2 * LANES)
    keep = jnp.broadcast_to(keep_ref[...], (sub, LANES))[None]
    damping = keep / jnp.maximum(sine_ref[...][:, None, :], keep) * (1.0 / points)
    damping = damping[:, None]
    a_ref[:, :, real] = (z[..., real] * damping).reshape(many, group, LANES)
    a_ref[:, :, imag] = (z[..., imag] * -damping).reshape(many, group, LANES)
    z = split_dot(a_ref[...].reshape(many * group, 2 * LANES), stacked_ref[...])
    a_ref[...] = z.reshape(many, group, 2 * LANES)

    stores = []
    for level in range(levels):
        rows = slice(level * sub, (level + 1) * sub)
        y = many_point([twisted(k, a_ref[k, rows, real], a_ref[k, rows, imag]) for k in range(many)])
        for i in range(2):
            values = [-y[j][1] if i else y[j][0] for j in range(many)]
            for d in range(parts):
                for e in range(THIRDS):
                    value = values[THIRDS * d + e]
                    if e == THIRDS - 1:
                        west = pltpu.roll(values[(THIRDS * d - 1) % many], LANES - short, 1)
                        east = pltpu.roll(values[(THIRDS * d + THIRDS) % many], short, 1)
                        value = jnp.where(lane == LANES - 1, west, jnp.where(lane == short, east, value))
                    out_ref[d, 2 * level + i, :, spans[e]] = value
        pair = slice(2 * level, 2 * level + 2)
        stores.append(pltpu.make_async_copy(out_ref.at[:, pair], out_hbm.at[:, pair], sems.at[level]))
        stores[-1].start()
    for store in stores:
        store.wait()


def polar_filter(blocks, keep, tables, width):
    parts, planes, sub, wide = blocks.shape
    whole = pl.BlockSpec(memory_space=pltpu.VMEM)
    return pl.pallas_call(
        lambda *refs: filter_kernel(width, *refs),
        in_specs=[whole] * 5,
        out_specs=pl.BlockSpec(memory_space=pltpu.HBM),
        out_shape=pltpu.HBM(blocks.shape, jnp.float32),
        scratch_shapes=[
            pltpu.VMEM((THIRDS * parts, planes // 2 * sub, 2 * LANES), jnp.float32),
            pltpu.VMEM(blocks.shape, jnp.float32),
            pltpu.SemaphoreType.DMA((planes // 2,)),
        ],
        compiler_params=pltpu.CompilerParams(vmem_limit_bytes=16 * MIB),
        name="polar_filter",
    )(blocks, keep, *tables)


def edges_kernel(t_ref, q_ref, rows_out, first_out, last_out):
    levels, width, rows = t_ref.shape
    wide = rows_out.shape[1]
    count = 2 * levels
    lane = lax.broadcasted_iota(jnp.int32, (width, rows), 1)
    picked = jnp.zeros((width, rows), jnp.float32)
    for i, ref in enumerate((t_ref, q_ref)):
        for level in range(levels):
            plane = i * levels + level
            x = ref[level]
            first_out[plane : plane + 1] = x[:1]
            last_out[plane : plane + 1] = x[width - 1 :]
            first = pltpu.roll(x, plane, 1) if plane else x
            picked = jnp.where(lane == plane, first, picked)
            picked = jnp.where(lane == count + plane, pltpu.roll(x, count + plane + 1, 1), picked)
    blank = jnp.zeros((wide - width, rows), jnp.float32)
    rows_out[...] = jnp.concatenate([picked, blank], axis=0).T[: 2 * count]


def edges_of(t, q, wide):
    levels, width, rows = t.shape
    whole = pl.BlockSpec(memory_space=pltpu.VMEM)
    column = jax.ShapeDtypeStruct((2 * levels, rows), jnp.float32)
    return pl.pallas_call(
        edges_kernel,
        in_specs=[whole] * 2,
        out_specs=[whole] * 3,
        out_shape=[jax.ShapeDtypeStruct((4 * levels, wide), jnp.float32), column, column],
        compiler_params=pltpu.CompilerParams(vmem_limit_bytes=4 * MIB),
        name="edges",
    )(t, q)


def stepped(f, east, west, south, north, u, v, upper, lower):
    rows = f.shape[1]
    row = lax.broadcasted_iota(jnp.int32, f.shape, 1)
    above = jnp.where(row == rows - 1, north, pltpu.roll(f, rows - 1, 1))
    below = jnp.where(row == 0, south, pltpu.roll(f, 1, 1))
    advect = u * (east - west) * 0.5 + v * (above - below) * 0.5
    spread = (east - 2.0 * f + west) + (upper * (above - f) - lower * (f - below))
    return f - ADV_COEF * advect + DIFF_COEF * spread


def rims_of(south_ref, north_ref, planes):
    rims = [ref[pl.ds(plane, 1)] for plane in planes for ref in (south_ref, north_ref)]
    return jnp.concatenate(rims + rims, axis=0).T


def joined(block, short):
    parts, sub, wide = block.shape
    spans = [slice(e * LANES, (e + 1) * LANES) for e in range(THIRDS)]
    pieces = [block[:, :, lanes].reshape(parts * sub, LANES).T for lanes in spans]
    return jnp.concatenate([x[:short] for x in pieces[:-1]] + pieces[-1:], axis=0)


def tracer_kernel(w_ref, t_ref, q_ref, south_ref, north_ref, west_ref, east_ref, row_ref, t_out, q_out):
    count, width, rows = t_ref.shape
    levels, short = pl.num_programs(0) * count, width // THIRDS
    upper, lower = row_ref[0:1], row_ref[1:2]
    at = lax.broadcasted_iota(jnp.int32, (width, rows), 0)
    for n in range(count):
        level = pl.program_id(0) * count + n
        u, v = [joined(w_ref[:, 2 * level + i], short)[:width] for i in range(2)]
        rims = rims_of(south_ref, north_ref, (level, levels + level))
        for i, (ref, out) in enumerate(((t_ref, t_out), (q_ref, q_out))):
            f = ref[n]
            side = pl.ds(i * levels + level, 1)
            west = jnp.where(at == 0, west_ref[side], pltpu.roll(f, 1, 0))
            east = jnp.where(at == width - 1, east_ref[side], pltpu.roll(f, width - 1, 0))
            south, north = rims[:width, 2 * i : 2 * i + 1], rims[:width, 2 * i + 1 : 2 * i + 2]
            out[n] = stepped(f, east, west, south, north, u, v, upper, lower)


def wind_kernel(w_ref, south_ref, north_ref, row_ref, u_out, v_out):
    count, width, rows = u_out.shape
    short = width // THIRDS
    upper, lower = row_ref[0:1], row_ref[1:2]
    for n in range(count):
        level = pl.program_id(0) * count + n
        full = [joined(w_ref[:, 2 * level + i], short) for i in range(2)]
        u, v = [x[:width] for x in full]
        rims = rims_of(south_ref, north_ref, (2 * level, 2 * level + 1))
        rims = jnp.concatenate([rims[e * LANES : e * LANES + short] for e in range(THIRDS)], axis=0)
        for i, out in enumerate((u_out, v_out)):
            west = pltpu.roll(full[i], 1, 0)[:width]
            east = pltpu.roll(full[i], full[i].shape[0] - 1, 0)[:width]
            south, north = rims[:, 2 * i : 2 * i + 1], rims[:, 2 * i + 1 : 2 * i + 2]
            out[n] = stepped((u, v)[i], east, west, south, north, u, v, upper, lower)


def step_tracers(winds, t, q, *small):
    levels, width, rows = t.shape
    field = pl.BlockSpec((AT_ONCE, width, rows), lambda g: (g, 0, 0))
    shape = jax.ShapeDtypeStruct(t.shape, jnp.float32)
    return pl.pallas_call(
        tracer_kernel,
        grid=(levels // AT_ONCE,),
        in_specs=[pl.BlockSpec(memory_space=pltpu.VMEM), field, field] + [all_of(x) for x in small],
        out_specs=[field] * 2,
        out_shape=[shape] * 2,
        compiler_params=pltpu.CompilerParams(vmem_limit_bytes=12 * MIB),
        name="tracers",
    )(winds, t, q, *small)


def step_winds(winds, width, rows, *small):
    levels = winds.shape[1] // 2
    field = pl.BlockSpec((AT_ONCE, width, rows), lambda g: (g, 0, 0))
    shape = jax.ShapeDtypeStruct((levels, width, rows), jnp.float32)
    return pl.pallas_call(
        wind_kernel,
        grid=(levels // AT_ONCE,),
        in_specs=[pl.BlockSpec(memory_space=pltpu.VMEM)] + [all_of(x) for x in small],
        out_specs=[field] * 2,
        out_shape=[shape] * 2,
        compiler_params=pltpu.CompilerParams(vmem_limit_bytes=12 * MIB),
        name="winds",
    )(winds, *small)


def all_of(x):
    return pl.BlockSpec(x.shape, lambda g: (0, 0))


def beyond_band(first, last, band, bands, z_low, sign):
    lon_rest = lax.axis_size(LON) // 2

    def place(step):
        half, at = divmod(step % (2 * bands), bands)
        return half, (at if half == 0 else bands - 1 - at)

    pairs = []
    for step in range(2 * bands):
        for rest in range(lon_rest):
            (h0, b0), (h1, b1) = place(step), place(step + 1)
            pairs.append(((b0 * 2 + h0) * lon_rest + rest, (b1 * 2 + h1) * lon_rest + rest))
    onward = jnp.where(z_low == 0, last, first)
    backward = jnp.where(z_low == 0, first, last)
    from_before = lax.ppermute(onward, ALL, pairs)
    from_after = lax.ppermute(backward, ALL, [(b, a) for a, b in pairs])
    south = jnp.where(z_low == 0, from_before, from_after)
    north = jnp.where(z_low == 0, from_after, from_before)
    south = jnp.where(band == 0, sign * south, south)
    north = jnp.where(band == bands - 1, sign * north, north)
    return south, north


def on_device(east_flow_speed, north_flow_speed, thermal_anomaly, moisture_anomaly):
    levels, rows, width = east_flow_speed.shape
    bands = lax.axis_size("lat")
    parts = lax.axis_size(LON)
    total_rows = rows * bands
    band = lax.axis_index("lat")
    column = lax.axis_index(LON)
    z_low = lax.axis_index("lon_0")
    wide = THIRDS * LANES
    sub = rows // parts
    count = 2 * levels
    tables = [jnp.asarray(x) for x in fourier_tables(parts, width)]
    u, v, t, q = [
        jnp.swapaxes(x, 1, 2)
        for x in (east_flow_speed, north_flow_speed, thermal_anomaly, moisture_anomaly)
    ]

    sent = pack(u, v, parts, wide)
    circles = lax.all_to_all(sent, LON, split_axis=0, concat_axis=0, tiled=True)

    edge_rows, firsts, lasts = edges_of(t, q, wide)
    south, north = beyond_band(edge_rows[:count], edge_rows[count:], band, bands, z_low, 1.0)
    ring = [(i, (i + 1) % parts) for i in range(parts)]
    west = lax.ppermute(lasts, LON, ring)
    east = lax.ppermute(firsts, LON, [(b, a) for a, b in ring])

    circles, south, north, west, east = lax.optimization_barrier((circles, south, north, west, east))
    own_rows = (band * rows + column * sub + jnp.arange(sub, dtype=jnp.int32)).astype(jnp.float32)
    keep = (jnp.sin((own_rows + 0.5) * (math.pi / total_rows)) / COS_CUT) ** 2
    filtered = polar_filter(circles, keep[:, None], tables, width)
    winds = lax.all_to_all(filtered, LON, split_axis=0, concat_axis=0, tiled=True)

    row_index = (band * rows + jnp.arange(rows, dtype=jnp.int32)).astype(jnp.float32)
    centre = jnp.sin((row_index + 0.5) * (math.pi / total_rows))
    lower_edge = jnp.sin(row_index * (math.pi / total_rows))
    upper_edge = jnp.sin((row_index + 1.0) * (math.pi / total_rows))
    factors = jnp.stack([upper_edge / centre, lower_edge / centre], axis=0)

    by_rows = [winds[at, :, row].reshape(levels, 2, wide) for at, row in ((0, 0), (-1, -1))]
    wind_rims = [x.reshape(2 * levels, wide) for x in beyond_band(*by_rows, band, bands, z_low, -1.0)]
    next_t, next_q = step_tracers(winds, t, q, south, north, west, east, factors)
    next_u, next_v = step_winds(winds, width, rows, *wind_rims, factors)
    return tuple(jnp.swapaxes(x, 1, 2) for x in (next_u, next_v, next_t, next_q))


def solution(mesh):
    torus = Mesh(
        mesh.devices.reshape(mesh.shape["lat"], 2, 4, 2), ("lat", "lon_0", "lon_1", "lon_2")
    )
    placed = (P(None, "lat", LON),) * 4
    return jax.shard_map(
        on_device, mesh=torus, in_specs=placed, out_specs=placed, check_vma=False
    )
```

time: 83.5 us -> 77.8 us (0.932)
  Pallas kernels: 22.9 us -> 14 us
  local copies, waits for them, and re-layouts: 0.07 us -> 2.9 us
  waiting for transfers between devices: 34.9 us -> 32.6 us
  other arithmetic: 0.22 us -> 1.53 us
  starting transfers between devices: 24.3 us -> 25.6 us
    pallas_call x1, Pallas kernels: 10.7 us -> 4.48 us  [polar_filter(): pl.pallas_call(lambda *refs: filter_kernel(width, *refs), in_specs=[whole...]
    pallas_call x3, Pallas kernels: 11.4 us -> 8.3 us  [the longest x1 3.45 us: step_tracers(): pl.pallas_call(tracer_kernel, grid=(levels // AT_ONCE,), in_specs=[pl.Blo...]
    unnamed x8 -> x16, local copies, waits for them, and re-layouts: 0.02 us -> 2.85 us
    all_to_all x1, starting transfers between devices: 5.34 us -> 6.65 us  [on_device(): lax.all_to_all(filtered, LON, split_axis=0, concat_axis=0, tiled=True)]
    ppermute x2, starting transfers between devices: 5.63 us -> 4.45 us  [beyond_band(): from_before = lax.ppermute(onward, ALL, pairs)]
    ppermute x2, starting transfers between devices: 3.41 us -> 4.54 us  [beyond_band(): from_after = lax.ppermute(backward, ALL, [(b, a) for a, b in pairs])]
    ppermute x2, waiting for transfers between devices: 1.21 us -> 0.24 us  [beyond_band(): from_before = lax.ppermute(onward, ALL, pairs)]
  transfers between devices with their start and end apart: 8 -> 8, of which waited for: 5 -> 4; matrix products, arithmetic and copies ran while one was open for 0% -> 2% of each run, Pallas kernels for 6% -> 6%
where the time goes in v3:
time: 77.8 us; the launch traced here: 77.4 us
  waiting for transfers between devices  32.6 us (42%)
  starting transfers between devices  25.6 us (33%)
  Pallas kernels  14 us (18%)
  local copies, waits for them, and re-layouts  2.9 us (4%)
  other arithmetic  1.53 us (2%)
    all_to_all x1, waiting for transfers between devices, on_device(): lax.all_to_all(filtered, LON, split_axis=0, concat_axis=0, tiled=True)  22 us
    ppermute x2, waiting for transfers between devices, beyond_band(): from_after = lax.ppermute(backward, ALL, [(b, a) for a, b in pairs])  10.2 us
    all_to_all x1, starting transfers between devices, on_device(): lax.all_to_all(filtered, LON, split_axis=0, concat_axis=0, tiled=True)  6.65 us
    all_to_all x1, starting transfers between devices, on_device(): circles = lax.all_to_all(sent, LON, split_axis=0, concat_axis=0, tiled=True)  6.06 us
    ppermute x2, starting transfers between devices, beyond_band(): from_after = lax.ppermute(backward, ALL, [(b, a) for a, b in pairs])  4.54 us
    pallas_call x1, Pallas kernels, polar_filter(): pl.pallas_call(lambda *refs: filter_kernel(width, *refs), in_specs=[whole...  4.48 us
    ppermute x2, starting transfers between devices, beyond_band(): from_before = lax.ppermute(onward, ALL, pairs)  4.45 us
    ppermute x1, starting transfers between devices, on_device(): east = lax.ppermute(firsts, LON, [(b, a) for a, b in ring])  3.85 us
  transfers between devices with their start and end apart: 8, of which 4 were waited for; matrix products, arithmetic and copies ran while one was open for 2% of the time, Pallas kernels for 6%

profile of v3, /device:TPU:6, one launch (start us, length us, event | category | flops | bytes accessed | tf_op | source)
XLA Modules:
  0.0 77.4 jit_solution(13852584460450956975)
XLA Ops:
  0.6 0.0 copy-start.2
  0.6 1.1 %copy-done.2 = f32[4,128,360]{1,2,0:T(8,128)S(1)} copy-done((f32[4,128,360]{1,2,0:T(8,128)S(1)}, f32[4,128,360]{1,2,0:T(8,128)}, u32[]{:S(2)}) %copy-start.2) | copy-done | bytes 737304
  1.7 0.0 copy-start.3
  1.7 1.1 %copy-done.3 = f32[4,128,360]{1,2,0:T(8,128)S(1)} copy-done((f32[4,128,360]{1,2,0:T(8,128)S(1)}, f32[4,128,360]{1,2,0:T(8,128)}, u32[]{:S(2)}) %copy-start.3) | copy-done | bytes 737304
  2.9 1.5 %pack.1 = f32[16,8,8,384]{3,2,1,0:T(8,128)} custom-call(f32[4,360,128]{2,1,0:T(8,128)S(1)} %bitcast.12, f32[4,360,128]{2,1,0:T(8,128)S(1)} %bitcast.13), custom_call_target="tpu_custom_call" | custom-call | tf_op jit(solution)/shard_map/pack/pallas_call | solution.py:118
  4.3 0.0 copy-start
  4.3 0.0 copy-start.1
  4.3 6.1 %all-to-all-start = ((f32[16,8,8,384]{3,2,1,0:T(8,128)}), f32[16,8,8,384]{3,2,1,0:T(8,128)S(1)}, u32[]{:S(2)}, u32[]{:S(2)}) async-start(f32[16,8,8,384]{3,2,1,0:T(8,128)} %pack.1), calls=%async_computation | async-start | bytes 3145728 | tf_op jit(solution)/shard_map/all_to_all | solution.py:376
  10.4 0.0 copy-start.4
  10.4 0.0 copy-start.5
  10.4 0.0 copy-start.6
  10.4 0.0 copy-done
  10.5 0.0 copy-done.1
  10.5 1.3 %edges.1 = (f32[16,384]{1,0:T(8,128)S(1)}, f32[8,128]{1,0:T(8,128)S(1)}, f32[8,128]{1,0:T(8,128)}) custom-call(f32[4,360,128]{2,1,0:T(8,128)S(1)} %bitcast.8, f32[4,360,128]{2,1,0:T(8,128)S(1)} %bitcast.10), custom_call_target="tpu_custom_call" | custom-call | tf_op jit(solution)/shard_map/edges/pallas_call | solution.py:234
  11.7 0.6 slice_select_fusion
  12.3 3.6 %collective-permute-start = (f32[8,384]{1,0:T(8,128)}, f32[8,384]{1,0:T(8,128)S(1)}, u32[]{:S(2)}, u32[]{:S(2)}) collective-permute-start(f32[8,384]{1,0:T(8,128)} %get-tuple-element.35), channel_id=1, source_target_pairs={{0,16},{1,17},{2,18},{3,19},{4,20},{5,21},{6,22},{7,23},{16,32},{1... | collective-permute-start | bytes 36872 | tf_op jit(solution)/shard_map/ppermute | solution.py:349
  15.9 0.8 %collective-permute-start.1 = (f32[8,384]{1,0:T(8,128)S(1)}, f32[8,384]{1,0:T(8,128)}, u32[]{:S(2)}, u32[]{:S(2)}) collective-permute-start(f32[8,384]{1,0:T(8,128)S(1)} %get-tuple-element.34), channel_id=1, source_target_pairs={{16,0},{17,1},{18,2},{19,3},{20,4},{21,5},{22,6},{23,7},{32,16},{3... | collective-permute-start | bytes 36872 | tf_op jit(solution)/shard_map/ppermute | solution.py:350
  16.8 0.0 collective-permute-start.2
  16.8 3.9 %collective-permute-start.3 = (f32[8,128]{1,0:T(8,128)S(1)}, f32[8,128]{1,0:T(8,128)S(1)}, u32[]{:S(2)}, u32[]{:S(2)}) collective-permute-start(f32[8,128]{1,0:T(8,128)S(1)} %get-tuple-element.18), channel_id=1, source_target_pairs={{1,0},{2,1},{3,2},{4,3},{5,4},{6,5},{7,6},{8,7},{9,8},{10,9},{11,1... | collective-permute-start | bytes 12296 | tf_op jit(solution)/shard_map/ppermute | solution.py:382
  20.7 0.2 collective-permute-done
  20.9 0.0 copy-start.7
  20.9 0.6 copy-done.7
  21.5 10.1 %collective-permute-done.1 = f32[8,384]{1,0:T(8,128)} collective-permute-done((f32[8,384]{1,0:T(8,128)S(1)}, f32[8,384]{1,0:T(8,128)}, u32[]{:S(2)}, u32[]{:S(2)}) %collective-permute-start.1) | collective-permute-done | bytes 12320 | tf_op jit(solution)/shard_map/ppermute | solution.py:350
  31.7 0.7 broadcast_select_fusion.2
  32.4 0.0 collective-permute-done.2.west_ref
  32.4 0.0 collective-permute-done.3.east_ref
  32.4 0.1 all-to-all-done.refs_0_
  32.5 0.0 copy-done.4
  32.5 0.0 copy-done.5
  32.5 0.0 copy-done.6
  32.5 4.5 %polar_filter.1 = f32[16,8,8,384]{3,2,1,0:T(8,128)} custom-call(f32[16,8,8,384]{3,2,1,0:T(8,128)S(1)} %all-to-all-done.refs_0_, f32[8,1]{1,0:T(8,128)S(1)} %multiply_multiply_fusion.refs_1_, bf16[768,256]{1,0:T(8,128)(2,1)S(1)} %copy-done.4, f32[2,48,128]{2,1,0:T(8,128)S(1)} %copy-done.5, f32[48,128]{1,0:T(8,128)S(1)} %copy-done.6), custom_call_target="tpu_custom_call" | custom-call | tf_op jit(solution)/shard_map/polar_filter/pallas_call | solution.py:196
  37.0 6.6 %all-to-all-start.1 = ((f32[16,8,8,384]{3,2,1,0:T(8,128)}), f32[16,8,8,384]{3,2,1,0:T(8,128)S(1)}, u32[]{:S(2)}, u32[]{:S(2)}) async-start(f32[16,8,8,384]{3,2,1,0:T(8,128)} %polar_filter.1), calls=%async_computation.1 | async-start | bytes 3145728 | tf_op jit(solution)/shard_map/all_to_all | solution.py:388
  43.7 0.1 sine_divide_fusion
  43.8 22.0 %all-to-all-done.1.w_ref = f32[16,8,8,384]{3,2,1,0:T(8,128)S(1)} async-done(((f32[16,8,8,384]{3,2,1,0:T(8,128)}), f32[16,8,8,384]{3,2,1,0:T(8,128)S(1)}, u32[]{:S(2)}, u32[]{:S(2)}) %all-to-all-start.1) | async-done | bytes 1572896 | tf_op jit(solution)/shard_map/all_to_all | solution.py:388
  65.8 0.1 fusion.1
  65.9 0.9 %collective-permute-start.4 = (f32[4,2,384]{2,1,0:T(2,128)S(1)}, f32[4,2,384]{2,1,0:T(2,128)S(1)}, u32[]{:S(2)}, u32[]{:S(2)}) collective-permute-start(f32[4,2,384]{2,1,0:T(2,128)S(1)} %select_n.73), channel_id=1, source_target_pairs={{0,16},{1,17},{2,18},{3,19},{4,20},{5,21},{6,22},{7,23},{16,32},{1... | collective-permute-start | bytes 36872 | tf_op jit(solution)/shard_map/ppermute | solution.py:349
  66.8 3.7 %collective-permute-start.5 = (f32[4,2,384]{2,1,0:T(2,128)S(1)}, f32[4,2,384]{2,1,0:T(2,128)S(1)}, u32[]{:S(2)}, u32[]{:S(2)}) collective-permute-start(f32[4,2,384]{2,1,0:T(2,128)S(1)} %select_n.75), channel_id=1, source_target_pairs={{16,0},{17,1},{18,2},{19,3},{20,4},{21,5},{22,6},{23,7},{32,16},{3... | collective-permute-start | bytes 36872 | tf_op jit(solution)/shard_map/ppermute | solution.py:350
  70.5 3.5 %tracers.1 = (f32[4,360,128]{2,1,0:T(8,128)}, f32[4,360,128]{2,1,0:T(8,128)}) custom-call(f32[16,8,8,384]{3,2,1,0:T(8,128)S(1)} %all-to-all-done.1.w_ref, f32[4,360,128]{2,1,0:T(8,128)S(1)} %bitcast.9, f32[4,360,128]{2,1,0:T(8,128)S(1)} %bitcast.11, f32[8,384]{1,0:T(8,128)S(1)} %get-tuple-element.22.south_ref, f32[8,384]{1,0:T(8,128)S(1)} %get-tuple-element.23.north_ref, ...), custom_call_target="tpu_custom_call" | custom-call | tf_op jit(solution)/shard_map/tracers/pallas_call | solution.py:305
  73.9 0.0 collective-permute-done.4
  73.9 0.0 collective-permute-done.5
  74.0 3.4 %winds.1 = (f32[4,360,128]{2,1,0:T(8,128)}, f32[4,360,128]{2,1,0:T(8,128)}) custom-call(f32[16,8,8,384]{3,2,1,0:T(8,128)S(1)} %all-to-all-done.1.w_ref, f32[8,384]{1,0:T(8,128)S(1)} %reshape.84.south_ref, f32[8,384]{1,0:T(8,128)S(1)} %reshape.85.north_ref, f32[2,128]{1,0:T(2,128)S(1)} %pad_maximum_fusion.row_ref), custom_call_target="tpu_custom_call" | custom-call | tf_op jit(solution)/shard_map/winds/pallas_call | solution.py:320
  (7 shorter events, 0.1 us)
Async XLA Ops:
  0.6 1.1 %copy-start.2 = (f32[4,128,360]{1,2,0:T(8,128)S(1)}, f32[4,128,360]{1,2,0:T(8,128)}, u32[]{:S(2)}) copy-start(f32[4,128,360]{1,2,0:T(8,128)} %param.7) | copy-start | bytes 2211844
  1.7 1.1 %copy-start.3 = (f32[4,128,360]{1,2,0:T(8,128)S(1)}, f32[4,128,360]{1,2,0:T(8,128)}, u32[]{:S(2)}) copy-start(f32[4,128,360]{1,2,0:T(8,128)} %param.8) | copy-start | bytes 2211844
  4.3 6.1 %copy-start = (f32[4,128,360]{1,2,0:T(8,128)S(1)}, f32[4,128,360]{1,2,0:T(8,128)}, u32[]{:S(2)}) copy-start(f32[4,128,360]{1,2,0:T(8,128)} %param.9) | copy-start | bytes 2211844
  4.3 6.1 %copy-start.1 = (f32[4,128,360]{1,2,0:T(8,128)S(1)}, f32[4,128,360]{1,2,0:T(8,128)}, u32[]{:S(2)}) copy-start(f32[4,128,360]{1,2,0:T(8,128)} %param.10) | copy-start | bytes 2211844
  4.3 28.2 %all-to-all-start = ((f32[16,8,8,384]{3,2,1,0:T(8,128)}), f32[16,8,8,384]{3,2,1,0:T(8,128)S(1)}, u32[]{:S(2)}, u32[]{:S(2)}) async-start(f32[16,8,8,384]{3,2,1,0:T(8,128)} %pack.1), calls=%async_computation | async-start | bytes 3145728 | tf_op jit(solution)/shard_map/all_to_all | solution.py:376
  10.4 22.1 %copy-start.4 = (bf16[768,256]{1,0:T(8,128)(2,1)S(1)}, bf16[768,256]{1,0:T(8,128)(2,1)}, u32[]{:S(2)}) copy-start(bf16[768,256]{1,0:T(8,128)(2,1)} %constant.45.clone.refs_2_) | copy-start | bytes 1179652
  10.4 22.1 %copy-start.5 = (f32[2,48,128]{2,1,0:T(8,128)S(1)}, f32[2,48,128]{2,1,0:T(8,128)}, u32[]{:S(2)}) copy-start(f32[2,48,128]{2,1,0:T(8,128)} %constant.46.clone.refs_3_) | copy-start | bytes 147460
  10.4 22.1 %copy-start.6 = (f32[48,128]{1,0:T(8,128)S(1)}, f32[48,128]{1,0:T(8,128)}, u32[]{:S(2)}) copy-start(f32[48,128]{1,0:T(8,128)} %constant.47.clone.refs_4_) | copy-start | bytes 73732
  12.3 8.6 %collective-permute-start = (f32[8,384]{1,0:T(8,128)}, f32[8,384]{1,0:T(8,128)S(1)}, u32[]{:S(2)}, u32[]{:S(2)}) collective-permute-start(f32[8,384]{1,0:T(8,128)} %get-tuple-element.35), channel_id=1, source_target_pairs={{0,16},{1,17},{2,18},{3,19},{4,20},{5,21},{6,22},{7,23},{16,32},{1... | collective-permute-start | bytes 36872 | tf_op jit(solution)/shard_map/ppermute | solution.py:349
  15.9 15.7 %collective-permute-start.1 = (f32[8,384]{1,0:T(8,128)S(1)}, f32[8,384]{1,0:T(8,128)}, u32[]{:S(2)}, u32[]{:S(2)}) collective-permute-start(f32[8,384]{1,0:T(8,128)S(1)} %get-tuple-element.34), channel_id=1, source_target_pairs={{16,0},{17,1},{18,2},{19,3},{20,4},{21,5},{22,6},{23,7},{32,16},{3... | collective-permute-start | bytes 36872 | tf_op jit(solution)/shard_map/ppermute | solution.py:350
  16.8 15.6 %collective-permute-start.2 = (f32[8,128]{1,0:T(8,128)}, f32[8,128]{1,0:T(8,128)S(1)}, u32[]{:S(2)}, u32[]{:S(2)}) collective-permute-start(f32[8,128]{1,0:T(8,128)} %get-tuple-element.17), channel_id=1, source_target_pairs={{0,1},{1,2},{2,3},{3,4},{4,5},{5,6},{6,7},{7,8},{8,9},{9,10},{10,1... | collective-permute-start | bytes 12296 | tf_op jit(solution)/shard_map/ppermute | solution.py:381
  16.8 15.6 %collective-permute-start.3 = (f32[8,128]{1,0:T(8,128)S(1)}, f32[8,128]{1,0:T(8,128)S(1)}, u32[]{:S(2)}, u32[]{:S(2)}) collective-permute-start(f32[8,128]{1,0:T(8,128)S(1)} %get-tuple-element.18), channel_id=1, source_target_pairs={{1,0},{2,1},{3,2},{4,3},{5,4},{6,5},{7,6},{8,7},{9,8},{10,9},{11,1... | collective-permute-start | bytes 12296 | tf_op jit(solution)/shard_map/ppermute | solution.py:382
  20.9 0.6 copy-start.7
  37.0 28.8 %all-to-all-start.1 = ((f32[16,8,8,384]{3,2,1,0:T(8,128)}), f32[16,8,8,384]{3,2,1,0:T(8,128)S(1)}, u32[]{:S(2)}, u32[]{:S(2)}) async-start(f32[16,8,8,384]{3,2,1,0:T(8,128)} %polar_filter.1), calls=%async_computation.1 | async-start | bytes 3145728 | tf_op jit(solution)/shard_map/all_to_all | solution.py:388
  65.9 8.0 %collective-permute-start.4 = (f32[4,2,384]{2,1,0:T(2,128)S(1)}, f32[4,2,384]{2,1,0:T(2,128)S(1)}, u32[]{:S(2)}, u32[]{:S(2)}) collective-permute-start(f32[4,2,384]{2,1,0:T(2,128)S(1)} %select_n.73), channel_id=1, source_target_pairs={{0,16},{1,17},{2,18},{3,19},{4,20},{5,21},{6,22},{7,23},{16,32},{1... | collective-permute-start | bytes 36872 | tf_op jit(solution)/shard_map/ppermute | solution.py:349
  66.8 7.2 %collective-permute-start.5 = (f32[4,2,384]{2,1,0:T(2,128)S(1)}, f32[4,2,384]{2,1,0:T(2,128)S(1)}, u32[]{:S(2)}, u32[]{:S(2)}) collective-permute-start(f32[4,2,384]{2,1,0:T(2,128)S(1)} %select_n.75), channel_id=1, source_target_pairs={{16,0},{17,1},{18,2},{19,3},{20,4},{21,5},{22,6},{23,7},{32,16},{3... | collective-permute-start | bytes 36872 | tf_op jit(solution)/shard_map/ppermute | solution.py:350

commit v4 on v3

--- a/solution.py
+++ b/solution.py
@@ -123,7 +123,7 @@
         out_shape=jax.ShapeDtypeStruct((parts, 2 * levels, sub, wide), jnp.float32),
         compiler_params=pltpu.CompilerParams(vmem_limit_bytes=8 * MIB),
         name="pack",
-    )(u, v)
+    )(*[pltpu.with_memory_space_constraint(x, pltpu.HBM) for x in (u, v)])
 
 
 def split_dot(x, stacked):
@@ -241,21 +241,6 @@
     )(t, q)
 
 
-def stepped(f, east, west, south, north, u, v, upper, lower):
-    rows = f.shape[1]
-    row = lax.broadcasted_iota(jnp.int32, f.shape, 1)
-    above = jnp.where(row == rows - 1, north, pltpu.roll(f, rows - 1, 1))
-    below = jnp.where(row == 0, south, pltpu.roll(f, 1, 1))
-    advect = u * (east - west) * 0.5 + v * (above - below) * 0.5
-    spread = (east - 2.0 * f + west) + (upper * (above - f) - lower * (f - below))
-    return f - ADV_COEF * advect + DIFF_COEF * spread
-
-
-def rims_of(south_ref, north_ref, planes):
-    rims = [ref[pl.ds(plane, 1)] for plane in planes for ref in (south_ref, north_ref)]
-    return jnp.concatenate(rims + rims, axis=0).T
-
-
 def joined(block, short):
     parts, sub, wide = block.shape
     spans = [slice(e * LANES, (e + 1) * LANES) for e in range(THIRDS)]
@@ -263,39 +248,76 @@
     return jnp.concatenate([x[:short] for x in pieces[:-1]] + pieces[-1:], axis=0)
 
 
-def tracer_kernel(w_ref, t_ref, q_ref, south_ref, north_ref, west_ref, east_ref, row_ref, t_out, q_out):
+def fill_tables(table_ref):
+    rows = LANES
+    r = lax.broadcasted_iota(jnp.int32, (rows, 2 * rows), 0)
+    c = lax.broadcasted_iota(jnp.int32, (rows, 2 * rows), 1)
+    second = c >= rows
+    c = jnp.where(second, c - rows, c)
+    own = jnp.where(r == c + 1, 1.0, 0.0) + jnp.where(r == c - 1, jnp.where(second, 1.0, -1.0), 0.0)
+    own = own - jnp.where(second & (r == c), 2.0, 0.0)
+    for i in range(table_ref.shape[0]):
+        rim = jnp.where((r == 2 * i) & (c == 0), jnp.where(second, 1.0, -1.0), 0.0)
+        rim = rim + jnp.where((r == 2 * i + 1) & (c == rows - 1), 1.0, 0.0)
+        for part, values in enumerate((own, own, rim, rim)):
+            table_ref[i, part * rows : (part + 1) * rows] = values.astype(jnp.bfloat16)
+
+
+def in_two(x):
+    top = x.astype(jnp.bfloat16)
+    return [top, (x - top.astype(jnp.float32)).astype(jnp.bfloat16)]
+
+
+def rims_of(south_ref, north_ref, planes):
+    rims = [ref[pl.ds(plane, 1)] for plane in planes for ref in (south_ref, north_ref)]
+    blank = jnp.zeros((LANES - len(rims), rims[0].shape[1]), jnp.float32)
+    return jnp.concatenate(rims + [blank], axis=0).T
+
+
+def stepped(f, east, west, rims, table, by_u, by_first, by_second):
+    both = jnp.concatenate(in_two(f) + rims, axis=1)
+    change = jnp.dot(both, table, preferred_element_type=jnp.float32)
+    rows = f.shape[1]
+    value = f - by_u * (east - west) + DIFF_COEF * (east - 2.0 * f + west)
+    return value + (change[:, :rows] * by_first + change[:, rows:] * by_second)
+
+
+def tracer_kernel(
+    w_ref, t_ref, q_ref, south_ref, north_ref, west_ref, east_ref, row_ref, t_out, q_out, table_ref
+):
     count, width, rows = t_ref.shape
     levels, short = pl.num_programs(0) * count, width // THIRDS
-    upper, lower = row_ref[0:1], row_ref[1:2]
+    pl.when(pl.program_id(0) == 0)(lambda: fill_tables(table_ref))
     at = lax.broadcasted_iota(jnp.int32, (width, rows), 0)
     for n in range(count):
         level = pl.program_id(0) * count + n
         u, v = [joined(w_ref[:, 2 * level + i], short)[:width] for i in range(2)]
-        rims = rims_of(south_ref, north_ref, (level, levels + level))
+        factors = (0.5 * ADV_COEF) * u, row_ref[1:2] - (0.5 * ADV_COEF) * v, row_ref[0:1]
+        rims = in_two(rims_of(south_ref, north_ref, (level, levels + level))[:width])
         for i, (ref, out) in enumerate(((t_ref, t_out), (q_ref, q_out))):
             f = ref[n]
             side = pl.ds(i * levels + level, 1)
             west = jnp.where(at == 0, west_ref[side], pltpu.roll(f, 1, 0))
             east = jnp.where(at == width - 1, east_ref[side], pltpu.roll(f, width - 1, 0))
-            south, north = rims[:width, 2 * i : 2 * i + 1], rims[:width, 2 * i + 1 : 2 * i + 2]
-            out[n] = stepped(f, east, west, south, north, u, v, upper, lower)
-
-
-def wind_kernel(w_ref, south_ref, north_ref, row_ref, u_out, v_out):
+            out[n] = stepped(f, east, west, rims, table_ref[i], *factors)
+
+
+def wind_kernel(w_ref, south_ref, north_ref, row_ref, u_out, v_out, table_ref):
     count, width, rows = u_out.shape
     short = width // THIRDS
-    upper, lower = row_ref[0:1], row_ref[1:2]
+    pl.when(pl.program_id(0) == 0)(lambda: fill_tables(table_ref))
     for n in range(count):
         level = pl.program_id(0) * count + n
         full = [joined(w_ref[:, 2 * level + i], short) for i in range(2)]
         u, v = [x[:width] for x in full]
+        factors = (0.5 * ADV_COEF) * u, row_ref[1:2] - (0.5 * ADV_COEF) * v, row_ref[0:1]
         rims = rims_of(south_ref, north_ref, (2 * level, 2 * level + 1))
         rims = jnp.concatenate([rims[e * LANES : e * LANES + short] for e in range(THIRDS)], axis=0)
+        rims = in_two(rims)
         for i, out in enumerate((u_out, v_out)):
             west = pltpu.roll(full[i], 1, 0)[:width]
             east = pltpu.roll(full[i], full[i].shape[0] - 1, 0)[:width]
-            south, north = rims[:, 2 * i : 2 * i + 1], rims[:, 2 * i + 1 : 2 * i + 2]
-            out[n] = stepped((u, v)[i], east, west, south, north, u, v, upper, lower)
+            out[n] = stepped((u, v)[i], east, west, rims, table_ref[i], *factors)
 
 
 def step_tracers(winds, t, q, *small):
@@ -308,6 +330,7 @@
         in_specs=[pl.BlockSpec(memory_space=pltpu.VMEM), field, field] + [all_of(x) for x in small],
         out_specs=[field] * 2,
         out_shape=[shape] * 2,
+        scratch_shapes=[pltpu.VMEM((2, 4 * LANES, 2 * LANES), jnp.bfloat16)],
         compiler_params=pltpu.CompilerParams(vmem_limit_bytes=12 * MIB),
         name="tracers",
     )(winds, t, q, *small)
@@ -323,6 +346,7 @@
         in_specs=[pl.BlockSpec(memory_space=pltpu.VMEM)] + [all_of(x) for x in small],
         out_specs=[field] * 2,
         out_shape=[shape] * 2,
+        scratch_shapes=[pltpu.VMEM((2, 4 * LANES, 2 * LANES), jnp.bfloat16)],
         compiler_params=pltpu.CompilerParams(vmem_limit_bytes=12 * MIB),
         name="winds",
     )(winds, *small)
@@ -391,7 +415,8 @@
     centre = jnp.sin((row_index + 0.5) * (math.pi / total_rows))
     lower_edge = jnp.sin(row_index * (math.pi / total_rows))
     upper_edge = jnp.sin((row_index + 1.0) * (math.pi / total_rows))
-    factors = jnp.stack([upper_edge / centre, lower_edge / centre], axis=0)
+    upper, lower = upper_edge / centre, lower_edge / centre
+    factors = (0.5 * DIFF_COEF) * jnp.stack([upper + lower, upper - lower], axis=0)
 
     by_rows = [winds[at, :, row].reshape(levels, 2, wide) for at, row in ((0, 0), (-1, -1))]
     wind_rims = [x.reshape(2 * levels, wide) for x in beyond_band(*by_rows, band, bands, z_low, -1.0)]

time: 77.8 us -> 74.4 us (0.956)
  local copies, waits for them, and re-layouts: 2.9 us -> 0.68 us
  Pallas kernels: 14 us -> 13 us
    unnamed x16 -> x12, local copies, waits for them, and re-layouts: 2.85 us -> 0.63 us
    pallas_call x1, Pallas kernels: 1.46 us -> 2.56 us  [pack(): pl.pallas_call(pack_kernel, grid=(levels // AT_ONCE,), in_specs=[spec, sp...]
    pallas_call x1, Pallas kernels: 3.45 us -> 2.37 us  [step_tracers(): pl.pallas_call(tracer_kernel, grid=(levels // AT_ONCE,), in_specs=[pl.Blo...]
    pallas_call x1, Pallas kernels: 3.38 us -> 2.36 us  [step_winds(): pl.pallas_call(wind_kernel, grid=(levels // AT_ONCE,), in_specs=[pl.Block...]
  transfers between devices with their start and end apart: 8 -> 8, of which waited for: 4 -> 4; matrix products, arithmetic and copies ran while one was open for 2% -> 2% of each run, Pallas kernels for 6% -> 5%
where the time goes in v4:
time: 74.4 us; the launch traced here: 74.1 us
  waiting for transfers between devices  32.6 us (44%)
  starting transfers between devices  25.6 us (34%)
  Pallas kernels  13 us (17%)
  other arithmetic  1.53 us (2%)
  between operations  0.75 us (1%)
    all_to_all x1, waiting for transfers between devices, on_device(): lax.all_to_all(filtered, LON, split_axis=0, concat_axis=0, tiled=True)  22 us
    ppermute x2, waiting for transfers between devices, beyond_band(): from_after = lax.ppermute(backward, ALL, [(b, a) for a, b in pairs])  10.2 us
    all_to_all x1, starting transfers between devices, on_device(): lax.all_to_all(filtered, LON, split_axis=0, concat_axis=0, tiled=True)  6.65 us
    all_to_all x1, starting transfers between devices, on_device(): circles = lax.all_to_all(sent, LON, split_axis=0, concat_axis=0, tiled=True)  6.06 us
    ppermute x2, starting transfers between devices, beyond_band(): from_after = lax.ppermute(backward, ALL, [(b, a) for a, b in pairs])  4.54 us
    ppermute x2, starting transfers between devices, beyond_band(): from_before = lax.ppermute(onward, ALL, pairs)  4.45 us
    pallas_call x1, Pallas kernels, polar_filter(): pl.pallas_call(lambda *refs: filter_kernel(width, *refs), in_specs=[whole...  4.45 us
    ppermute x1, starting transfers between devices, on_device(): east = lax.ppermute(firsts, LON, [(b, a) for a, b in ring])  3.85 us
  transfers between devices with their start and end apart: 8, of which 4 were waited for; matrix products, arithmetic and copies ran while one was open for 2% of the time, Pallas kernels for 5%

profile of v4, /device:TPU:6, one launch (start us, length us, event | category | flops | bytes accessed | tf_op | source)
XLA Modules:
  0.0 74.1 jit_solution(8373654283519819543)
XLA Ops:
  0.6 2.6 %pack.1 = f32[16,8,8,384]{3,2,1,0:T(8,128)} custom-call(f32[4,360,128]{2,1,0:T(8,128)} %bitcast.12, f32[4,360,128]{2,1,0:T(8,128)} %bitcast.13), custom_call_target="tpu_custom_call" | custom-call | tf_op jit(solution)/shard_map/pack/pallas_call | solution.py:118
  3.2 0.0 copy-start
  3.2 0.0 copy-start.1
  3.2 6.1 %all-to-all-start = ((f32[16,8,8,384]{3,2,1,0:T(8,128)}), f32[16,8,8,384]{3,2,1,0:T(8,128)S(1)}, u32[]{:S(2)}, u32[]{:S(2)}) async-start(f32[16,8,8,384]{3,2,1,0:T(8,128)} %pack.1), calls=%async_computation | async-start | bytes 3145728 | tf_op jit(solution)/shard_map/all_to_all | solution.py:400
  9.3 0.0 copy-start.2
  9.3 0.0 copy-start.3
  9.3 0.0 copy-start.4
  9.3 0.0 copy-done
  9.3 0.0 copy-done.1
  9.3 1.3 %edges.1 = (f32[16,384]{1,0:T(8,128)S(1)}, f32[8,128]{1,0:T(8,128)S(1)}, f32[8,128]{1,0:T(8,128)}) custom-call(f32[4,360,128]{2,1,0:T(8,128)S(1)} %bitcast.8, f32[4,360,128]{2,1,0:T(8,128)S(1)} %bitcast.10), custom_call_target="tpu_custom_call" | custom-call | tf_op jit(solution)/shard_map/edges/pallas_call | solution.py:234
  10.6 0.6 slice_select_fusion
  11.2 3.6 %collective-permute-start = (f32[8,384]{1,0:T(8,128)}, f32[8,384]{1,0:T(8,128)S(1)}, u32[]{:S(2)}, u32[]{:S(2)}) collective-permute-start(f32[8,384]{1,0:T(8,128)} %get-tuple-element.35), channel_id=1, source_target_pairs={{0,16},{1,17},{2,18},{3,19},{4,20},{5,21},{6,22},{7,23},{16,32},{1... | collective-permute-start | bytes 36872 | tf_op jit(solution)/shard_map/ppermute | solution.py:373
  14.8 0.8 %collective-permute-start.1 = (f32[8,384]{1,0:T(8,128)S(1)}, f32[8,384]{1,0:T(8,128)}, u32[]{:S(2)}, u32[]{:S(2)}) collective-permute-start(f32[8,384]{1,0:T(8,128)S(1)} %get-tuple-element.34), channel_id=1, source_target_pairs={{16,0},{17,1},{18,2},{19,3},{20,4},{21,5},{22,6},{23,7},{32,16},{3... | collective-permute-start | bytes 36872 | tf_op jit(solution)/shard_map/ppermute | solution.py:374
  15.6 0.0 collective-permute-start.2
  15.6 3.9 %collective-permute-start.3 = (f32[8,128]{1,0:T(8,128)S(1)}, f32[8,128]{1,0:T(8,128)S(1)}, u32[]{:S(2)}, u32[]{:S(2)}) collective-permute-start(f32[8,128]{1,0:T(8,128)S(1)} %get-tuple-element.18), channel_id=1, source_target_pairs={{1,0},{2,1},{3,2},{4,3},{5,4},{6,5},{7,6},{8,7},{9,8},{10,9},{11,1... | collective-permute-start | bytes 12296 | tf_op jit(solution)/shard_map/ppermute | solution.py:406
  19.5 0.2 collective-permute-done
  19.8 0.0 copy-start.5
  19.8 0.6 copy-done.5
  20.4 10.1 %collective-permute-done.1 = f32[8,384]{1,0:T(8,128)} collective-permute-done((f32[8,384]{1,0:T(8,128)S(1)}, f32[8,384]{1,0:T(8,128)}, u32[]{:S(2)}, u32[]{:S(2)}) %collective-permute-start.1) | collective-permute-done | bytes 12320 | tf_op jit(solution)/shard_map/ppermute | solution.py:374
  30.5 0.7 broadcast_select_fusion.2
  31.2 0.0 collective-permute-done.2.west_ref
  31.2 0.0 collective-permute-done.3.east_ref
  31.3 0.1 all-to-all-done.refs_0_
  31.4 0.0 copy-done.2
  31.4 0.0 copy-done.3
  31.4 0.0 copy-done.4
  31.4 4.4 %polar_filter.1 = f32[16,8,8,384]{3,2,1,0:T(8,128)} custom-call(f32[16,8,8,384]{3,2,1,0:T(8,128)S(1)} %all-to-all-done.refs_0_, f32[8,1]{1,0:T(8,128)S(1)} %multiply_multiply_fusion.refs_1_, bf16[768,256]{1,0:T(8,128)(2,1)S(1)} %copy-done.2, f32[2,48,128]{2,1,0:T(8,128)S(1)} %copy-done.3, f32[48,128]{1,0:T(8,128)S(1)} %copy-done.4), custom_call_target="tpu_custom_call" | custom-call | tf_op jit(solution)/shard_map/polar_filter/pallas_call | solution.py:196
  35.9 6.6 %all-to-all-start.1 = ((f32[16,8,8,384]{3,2,1,0:T(8,128)}), f32[16,8,8,384]{3,2,1,0:T(8,128)S(1)}, u32[]{:S(2)}, u32[]{:S(2)}) async-start(f32[16,8,8,384]{3,2,1,0:T(8,128)} %polar_filter.1), calls=%async_computation.1 | async-start | bytes 3145728 | tf_op jit(solution)/shard_map/all_to_all | solution.py:412
  42.5 0.1 fusion.2
  42.6 22.0 %all-to-all-done.1.w_ref = f32[16,8,8,384]{3,2,1,0:T(8,128)S(1)} async-done(((f32[16,8,8,384]{3,2,1,0:T(8,128)}), f32[16,8,8,384]{3,2,1,0:T(8,128)S(1)}, u32[]{:S(2)}, u32[]{:S(2)}) %all-to-all-start.1) | async-done | bytes 1572896 | tf_op jit(solution)/shard_map/all_to_all | solution.py:412
  64.6 0.1 fusion.1
  64.7 0.9 %collective-permute-start.4 = (f32[4,2,384]{2,1,0:T(2,128)S(1)}, f32[4,2,384]{2,1,0:T(2,128)S(1)}, u32[]{:S(2)}, u32[]{:S(2)}) collective-permute-start(f32[4,2,384]{2,1,0:T(2,128)S(1)} %select_n.73), channel_id=1, source_target_pairs={{0,16},{1,17},{2,18},{3,19},{4,20},{5,21},{6,22},{7,23},{16,32},{1... | collective-permute-start | bytes 36872 | tf_op jit(solution)/shard_map/ppermute | solution.py:373
  65.6 3.7 %collective-permute-start.5 = (f32[4,2,384]{2,1,0:T(2,128)S(1)}, f32[4,2,384]{2,1,0:T(2,128)S(1)}, u32[]{:S(2)}, u32[]{:S(2)}) collective-permute-start(f32[4,2,384]{2,1,0:T(2,128)S(1)} %select_n.75), channel_id=1, source_target_pairs={{16,0},{17,1},{18,2},{19,3},{20,4},{21,5},{22,6},{23,7},{32,16},{3... | collective-permute-start | bytes 36872 | tf_op jit(solution)/shard_map/ppermute | solution.py:374
  69.3 2.4 %tracers.1 = (f32[4,360,128]{2,1,0:T(8,128)}, f32[4,360,128]{2,1,0:T(8,128)}) custom-call(f32[16,8,8,384]{3,2,1,0:T(8,128)S(1)} %all-to-all-done.1.w_ref, f32[4,360,128]{2,1,0:T(8,128)S(1)} %bitcast.9, f32[4,360,128]{2,1,0:T(8,128)S(1)} %bitcast.11, f32[8,384]{1,0:T(8,128)S(1)} %get-tuple-element.22.south_ref, f32[8,384]{1,0:T(8,128)S(1)} %get-tuple-element.23.north_ref, ...), custom_call_target="tpu_custom_call" | custom-call | tf_op jit(solution)/shard_map/tracers/pallas_call | solution.py:327
  71.7 0.0 collective-permute-done.4
  71.7 0.0 collective-permute-done.5
  71.7 2.4 %winds.1 = (f32[4,360,128]{2,1,0:T(8,128)}, f32[4,360,128]{2,1,0:T(8,128)}) custom-call(f32[16,8,8,384]{3,2,1,0:T(8,128)S(1)} %all-to-all-done.1.w_ref, f32[8,384]{1,0:T(8,128)S(1)} %reshape.90.south_ref, f32[8,384]{1,0:T(8,128)S(1)} %reshape.91.north_ref, f32[2,128]{1,0:T(2,128)S(1)} %maximum_multiply_fusion.row_ref), custom_call_target="tpu_custom_call" | custom-call | tf_op jit(solution)/shard_map/winds/pallas_call | solution.py:343
  (7 shorter events, 0.1 us)
Async XLA Ops:
  3.2 6.1 %copy-start = (f32[4,128,360]{1,2,0:T(8,128)S(1)}, f32[4,128,360]{1,2,0:T(8,128)}, u32[]{:S(2)}) copy-start(f32[4,128,360]{1,2,0:T(8,128)} %param.9) | copy-start | bytes 2211844
  3.2 6.1 %copy-start.1 = (f32[4,128,360]{1,2,0:T(8,128)S(1)}, f32[4,128,360]{1,2,0:T(8,128)}, u32[]{:S(2)}) copy-start(f32[4,128,360]{1,2,0:T(8,128)} %param.10) | copy-start | bytes 2211844
  3.2 28.2 %all-to-all-start = ((f32[16,8,8,384]{3,2,1,0:T(8,128)}), f32[16,8,8,384]{3,2,1,0:T(8,128)S(1)}, u32[]{:S(2)}, u32[]{:S(2)}) async-start(f32[16,8,8,384]{3,2,1,0:T(8,128)} %pack.1), calls=%async_computation | async-start | bytes 3145728 | tf_op jit(solution)/shard_map/all_to_all | solution.py:400
  9.3 22.1 %copy-start.2 = (bf16[768,256]{1,0:T(8,128)(2,1)S(1)}, bf16[768,256]{1,0:T(8,128)(2,1)}, u32[]{:S(2)}) copy-start(bf16[768,256]{1,0:T(8,128)(2,1)} %constant.47.clone.refs_2_) | copy-start | bytes 1179652
  9.3 22.1 %copy-start.3 = (f32[2,48,128]{2,1,0:T(8,128)S(1)}, f32[2,48,128]{2,1,0:T(8,128)}, u32[]{:S(2)}) copy-start(f32[2,48,128]{2,1,0:T(8,128)} %constant.48.clone.refs_3_) | copy-start | bytes 147460
  9.3 22.1 %copy-start.4 = (f32[48,128]{1,0:T(8,128)S(1)}, f32[48,128]{1,0:T(8,128)}, u32[]{:S(2)}) copy-start(f32[48,128]{1,0:T(8,128)} %constant.49.clone.refs_4_) | copy-start | bytes 73732
  11.2 8.6 %collective-permute-start = (f32[8,384]{1,0:T(8,128)}, f32[8,384]{1,0:T(8,128)S(1)}, u32[]{:S(2)}, u32[]{:S(2)}) collective-permute-start(f32[8,384]{1,0:T(8,128)} %get-tuple-element.35), channel_id=1, source_target_pairs={{0,16},{1,17},{2,18},{3,19},{4,20},{5,21},{6,22},{7,23},{16,32},{1... | collective-permute-start | bytes 36872 | tf_op jit(solution)/shard_map/ppermute | solution.py:373
  14.8 15.7 %collective-permute-start.1 = (f32[8,384]{1,0:T(8,128)S(1)}, f32[8,384]{1,0:T(8,128)}, u32[]{:S(2)}, u32[]{:S(2)}) collective-permute-start(f32[8,384]{1,0:T(8,128)S(1)} %get-tuple-element.34), channel_id=1, source_target_pairs={{16,0},{17,1},{18,2},{19,3},{20,4},{21,5},{22,6},{23,7},{32,16},{3... | collective-permute-start | bytes 36872 | tf_op jit(solution)/shard_map/ppermute | solution.py:374
  15.6 15.6 %collective-permute-start.2 = (f32[8,128]{1,0:T(8,128)}, f32[8,128]{1,0:T(8,128)S(1)}, u32[]{:S(2)}, u32[]{:S(2)}) collective-permute-start(f32[8,128]{1,0:T(8,128)} %get-tuple-element.17), channel_id=1, source_target_pairs={{0,1},{1,2},{2,3},{3,4},{4,5},{5,6},{6,7},{7,8},{8,9},{9,10},{10,1... | collective-permute-start | bytes 12296 | tf_op jit(solution)/shard_map/ppermute | solution.py:405
  15.6 15.6 %collective-permute-start.3 = (f32[8,128]{1,0:T(8,128)S(1)}, f32[8,128]{1,0:T(8,128)S(1)}, u32[]{:S(2)}, u32[]{:S(2)}) collective-permute-start(f32[8,128]{1,0:T(8,128)S(1)} %get-tuple-element.18), channel_id=1, source_target_pairs={{1,0},{2,1},{3,2},{4,3},{5,4},{6,5},{7,6},{8,7},{9,8},{10,9},{11,1... | collective-permute-start | bytes 12296 | tf_op jit(solution)/shard_map/ppermute | solution.py:406
  19.8 0.6 copy-start.5
  35.9 28.8 %all-to-all-start.1 = ((f32[16,8,8,384]{3,2,1,0:T(8,128)}), f32[16,8,8,384]{3,2,1,0:T(8,128)S(1)}, u32[]{:S(2)}, u32[]{:S(2)}) async-start(f32[16,8,8,384]{3,2,1,0:T(8,128)} %polar_filter.1), calls=%async_computation.1 | async-start | bytes 3145728 | tf_op jit(solution)/shard_map/all_to_all | solution.py:412
  64.7 7.0 %collective-permute-start.4 = (f32[4,2,384]{2,1,0:T(2,128)S(1)}, f32[4,2,384]{2,1,0:T(2,128)S(1)}, u32[]{:S(2)}, u32[]{:S(2)}) collective-permute-start(f32[4,2,384]{2,1,0:T(2,128)S(1)} %select_n.73), channel_id=1, source_target_pairs={{0,16},{1,17},{2,18},{3,19},{4,20},{5,21},{6,22},{7,23},{16,32},{1... | collective-permute-start | bytes 36872 | tf_op jit(solution)/shard_map/ppermute | solution.py:373
  65.6 6.1 %collective-permute-start.5 = (f32[4,2,384]{2,1,0:T(2,128)S(1)}, f32[4,2,384]{2,1,0:T(2,128)S(1)}, u32[]{:S(2)}, u32[]{:S(2)}) collective-permute-start(f32[4,2,384]{2,1,0:T(2,128)S(1)} %select_n.75), channel_id=1, source_target_pairs={{16,0},{17,1},{18,2},{19,3},{20,4},{21,5},{22,6},{23,7},{32,16},{3... | collective-permute-start | bytes 36872 | tf_op jit(solution)/shard_map/ppermute | solution.py:374

commit v5 on v4

--- a/solution.py
+++ b/solution.py
@@ -134,10 +134,10 @@
     )
 
 
-def filter_kernel(width, x_ref, keep_ref, stacked_ref, twiddle_ref, sine_ref, out_hbm, a_ref, out_ref, sems):
+def filter_kernel(width, x_ref, keep_ref, stacked_ref, twiddle_ref, sine_ref, out_hbm, out_ref, sems, *held):
     parts, planes, sub, wide = x_ref.shape
-    many, group, _ = a_ref.shape
-    levels = planes // 2
+    many, group, _ = held[0].shape
+    per_part = group // sub
     points, short = parts * width, width // THIRDS
     real, imag = slice(0, LANES), slice(LANES, 2 * LANES)
     spans = [slice(e * LANES, (e + 1) * LANES) for e in range(THIRDS)]
@@ -147,45 +147,55 @@
         co, si = twiddle_ref[0, k : k + 1], twiddle_ref[1, k : k + 1]
         return re * co - im * si, re * si + im * co
 
-    for level in range(levels):
-        rows = slice(level * sub, (level + 1) * sub)
-        y = many_point(
-            [
-                (x_ref[d, 2 * level, :, lanes], x_ref[d, 2 * level + 1, :, lanes])
-                for d in range(parts)
-                for lanes in spans
-            ]
-        )
-        for k in range(many):
-            a_ref[k, rows, real], a_ref[k, rows, imag] = twisted(k, *y[k])
-
-    z = split_dot(a_ref[...].reshape(many * group, 2 * LANES), stacked_ref[...])
-    z = z.reshape(many, levels, sub, 2 * LANES)
     keep = jnp.broadcast_to(keep_ref[...], (sub, LANES))[None]
     damping = keep / jnp.maximum(sine_ref[...][:, None, :], keep) * (1.0 / points)
     damping = damping[:, None]
-    a_ref[:, :, real] = (z[..., real] * damping).reshape(many, group, LANES)
-    a_ref[:, :, imag] = (z[..., imag] * -damping).reshape(many, group, LANES)
-    z = split_dot(a_ref[...].reshape(many * group, 2 * LANES), stacked_ref[...])
-    a_ref[...] = z.reshape(many, group, 2 * LANES)
-
     stores = []
-    for level in range(levels):
-        rows = slice(level * sub, (level + 1) * sub)
-        y = many_point([twisted(k, a_ref[k, rows, real], a_ref[k, rows, imag]) for k in range(many)])
-        for i in range(2):
-            values = [-y[j][1] if i else y[j][0] for j in range(many)]
-            for d in range(parts):
-                for e in range(THIRDS):
-                    value = values[THIRDS * d + e]
-                    if e == THIRDS - 1:
-                        west = pltpu.roll(values[(THIRDS * d - 1) % many], LANES - short, 1)
-                        east = pltpu.roll(values[(THIRDS * d + THIRDS) % many], short, 1)
-                        value = jnp.where(lane == LANES - 1, west, jnp.where(lane == short, east, value))
-                    out_ref[d, 2 * level + i, :, spans[e]] = value
-        pair = slice(2 * level, 2 * level + 2)
-        stores.append(pltpu.make_async_copy(out_ref.at[:, pair], out_hbm.at[:, pair], sems.at[level]))
+
+    def gather(part, first):
+        for level in range(per_part):
+            rows = slice(level * sub, (level + 1) * sub)
+            at = 2 * (first + level)
+            y = many_point(
+                [(x_ref[d, at, :, lanes], x_ref[d, at + 1, :, lanes]) for d in range(parts) for lanes in spans]
+            )
+            for k in range(many):
+                part[k, rows, real], part[k, rows, imag] = twisted(k, *y[k])
+
+    def forward(part):
+        z = split_dot(part[...].reshape(many * group, 2 * LANES), stacked_ref[...])
+        z = z.reshape(many, per_part, sub, 2 * LANES)
+        part[:, :, real] = (z[..., real] * damping).reshape(many, group, LANES)
+        part[:, :, imag] = (z[..., imag] * -damping).reshape(many, group, LANES)
+
+    def backward(part):
+        z = split_dot(part[...].reshape(many * group, 2 * LANES), stacked_ref[...])
+        part[...] = z.reshape(many, group, 2 * LANES)
+
+    def scatter(part, first):
+        for level in range(per_part):
+            rows = slice(level * sub, (level + 1) * sub)
+            y = many_point([twisted(k, part[k, rows, real], part[k, rows, imag]) for k in range(many)])
+            for i in range(2):
+                plane = 2 * (first + level) + i
+                values = [-y[j][1] if i else y[j][0] for j in range(many)]
+                for d in range(parts):
+                    for e in range(THIRDS):
+                        value = values[THIRDS * d + e]
+                        if e == THIRDS - 1:
+                            west = pltpu.roll(values[(THIRDS * d - 1) % many], LANES - short, 1)
+                            east = pltpu.roll(values[(THIRDS * d + THIRDS) % many], short, 1)
+                            value = jnp.where(lane == LANES - 1, west, jnp.where(lane == short, east, value))
+                        out_ref[d, plane, :, spans[e]] = value
+        pair = slice(2 * first, 2 * (first + per_part))
+        stores.append(pltpu.make_async_copy(out_ref.at[:, pair], out_hbm.at[:, pair], sems.at[first]))
         stores[-1].start()
+
+    for n, part in enumerate(held):
+        gather(part, n * per_part)
+        forward(part)
+        backward(part)
+        scatter(part, n * per_part)
     for store in stores:
         store.wait()
 
@@ -199,10 +209,10 @@
         out_specs=pl.BlockSpec(memory_space=pltpu.HBM),
         out_shape=pltpu.HBM(blocks.shape, jnp.float32),
         scratch_shapes=[
-            pltpu.VMEM((THIRDS * parts, planes // 2 * sub, 2 * LANES), jnp.float32),
             pltpu.VMEM(blocks.shape, jnp.float32),
             pltpu.SemaphoreType.DMA((planes // 2,)),
-        ],
+        ]
+        + [pltpu.VMEM((THIRDS * parts, 1 * sub, 2 * LANES), jnp.float32)] * (planes // 2 // 1),
         compiler_params=pltpu.CompilerParams(vmem_limit_bytes=16 * MIB),
         name="polar_filter",
     )(blocks, keep, *tables)
@@ -282,8 +292,8 @@
     return value + (change[:, :rows] * by_first + change[:, rows:] * by_second)
 
 
-def tracer_kernel(
-    w_ref, t_ref, q_ref, south_ref, north_ref, west_ref, east_ref, row_ref, t_out, q_out, table_ref
+def inside_kernel(
+    w_ref, t_ref, q_ref, south_ref, north_ref, west_ref, east_ref, row_ref, t_out, q_out, u_out, v_out, table_ref
 ):
     count, width, rows = t_ref.shape
     levels, short = pl.num_programs(0) * count, width // THIRDS
@@ -291,8 +301,13 @@
     at = lax.broadcasted_iota(jnp.int32, (width, rows), 0)
     for n in range(count):
         level = pl.program_id(0) * count + n
-        u, v = [joined(w_ref[:, 2 * level + i], short)[:width] for i in range(2)]
+        full = [joined(w_ref[:, 2 * level + i], short) for i in range(2)]
+        u, v = [x[:width] for x in full]
         factors = (0.5 * ADV_COEF) * u, row_ref[1:2] - (0.5 * ADV_COEF) * v, row_ref[0:1]
+        for i, out in enumerate((u_out, v_out)):
+            west = pltpu.roll(full[i], 1, 0)[:width]
+            east = pltpu.roll(full[i], full[i].shape[0] - 1, 0)[:width]
+            out[n] = 2.0 * stepped((u, v)[i], east, west, [], table_ref[0, : 2 * LANES], *factors)
         rims = in_two(rims_of(south_ref, north_ref, (level, levels + level))[:width])
         for i, (ref, out) in enumerate(((t_ref, t_out), (q_ref, q_out))):
             f = ref[n]
@@ -302,54 +317,56 @@
             out[n] = stepped(f, east, west, rims, table_ref[i], *factors)
 
 
-def wind_kernel(w_ref, south_ref, north_ref, row_ref, u_out, v_out, table_ref):
+def rims_kernel(w_ref, u_ref, v_ref, south_ref, north_ref, row_ref, u_out, v_out):
+    parts, _, sub, wide = w_ref.shape
     count, width, rows = u_out.shape
     short = width // THIRDS
-    pl.when(pl.program_id(0) == 0)(lambda: fill_tables(table_ref))
+    first_factor = row_ref[0:1, 0:1] - row_ref[1:2, 0:1]
+    last_factor = row_ref[0:1, rows - 1 :] + row_ref[1:2, rows - 1 :]
+    at = lax.broadcasted_iota(jnp.int32, (sub, wide), 0)
+    blank = jnp.zeros((rows - 2 * sub, wide), jnp.float32)
     for n in range(count):
         level = pl.program_id(0) * count + n
-        full = [joined(w_ref[:, 2 * level + i], short) for i in range(2)]
-        u, v = [x[:width] for x in full]
-        factors = (0.5 * ADV_COEF) * u, row_ref[1:2] - (0.5 * ADV_COEF) * v, row_ref[0:1]
-        rims = rims_of(south_ref, north_ref, (2 * level, 2 * level + 1))
-        rims = jnp.concatenate([rims[e * LANES : e * LANES + short] for e in range(THIRDS)], axis=0)
-        rims = in_two(rims)
-        for i, out in enumerate((u_out, v_out)):
-            west = pltpu.roll(full[i], 1, 0)[:width]
-            east = pltpu.roll(full[i], full[i].shape[0] - 1, 0)[:width]
-            out[n] = stepped((u, v)[i], east, west, rims, table_ref[i], *factors)
-
-
-def step_tracers(winds, t, q, *small):
+        by_first = first_factor + (0.5 * ADV_COEF) * w_ref[0, 2 * level + 1, :1]
+        by_last = last_factor - (0.5 * ADV_COEF) * w_ref[parts - 1, 2 * level + 1, sub - 1 :]
+        for i, (ref, out) in enumerate(((u_ref, u_out), (v_ref, v_out))):
+            plane = pl.ds(2 * level + i, 1)
+            first = jnp.where(at == 0, south_ref[plane] * by_first, 0.0)
+            last = jnp.where(at == sub - 1, north_ref[plane] * by_last, 0.0)
+            added = jnp.concatenate([first, blank, last], axis=0)
+            for e in range(THIRDS):
+                piece = added[:, e * LANES : (e + 1) * LANES].T[:short]
+                span = slice(e * short, (e + 1) * short)
+                out[n, span] = ref[n, span] + piece
+
+
+def step_inside(winds, t, q, *small):
     levels, width, rows = t.shape
     field = pl.BlockSpec((AT_ONCE, width, rows), lambda g: (g, 0, 0))
-    shape = jax.ShapeDtypeStruct(t.shape, jnp.float32)
     return pl.pallas_call(
-        tracer_kernel,
+        inside_kernel,
+        grid=(levels // AT_ONCE,),
+        in_specs=[pl.BlockSpec(memory_space=pltpu.VMEM), field, field] + [all_of(x) for x in small],
+        out_specs=[field] * 4,
+        out_shape=[jax.ShapeDtypeStruct(t.shape, jnp.float32)] * 4,
+        scratch_shapes=[pltpu.VMEM((2, 4 * LANES, 2 * LANES), jnp.bfloat16)],
+        compiler_params=pltpu.CompilerParams(vmem_limit_bytes=12 * MIB),
+        name="inside",
+    )(winds, t, q, *small)
+
+
+def step_rims(winds, u, v, *small):
+    levels, width, rows = u.shape
+    field = pl.BlockSpec((AT_ONCE, width, rows), lambda g: (g, 0, 0))
+    return pl.pallas_call(
+        rims_kernel,
         grid=(levels // AT_ONCE,),
         in_specs=[pl.BlockSpec(memory_space=pltpu.VMEM), field, field] + [all_of(x) for x in small],
         out_specs=[field] * 2,
-        out_shape=[shape] * 2,
-        scratch_shapes=[pltpu.VMEM((2, 4 * LANES, 2 * LANES), jnp.bfloat16)],
-        compiler_params=pltpu.CompilerParams(vmem_limit_bytes=12 * MIB),
-        name="tracers",
-    )(winds, t, q, *small)
-
-
-def step_winds(winds, width, rows, *small):
-    levels = winds.shape[1] // 2
-    field = pl.BlockSpec((AT_ONCE, width, rows), lambda g: (g, 0, 0))
-    shape = jax.ShapeDtypeStruct((levels, width, rows), jnp.float32)
-    return pl.pallas_call(
-        wind_kernel,
-        grid=(levels // AT_ONCE,),
-        in_specs=[pl.BlockSpec(memory_space=pltpu.VMEM)] + [all_of(x) for x in small],
-        out_specs=[field] * 2,
-        out_shape=[shape] * 2,
-        scratch_shapes=[pltpu.VMEM((2, 4 * LANES, 2 * LANES), jnp.bfloat16)],
-        compiler_params=pltpu.CompilerParams(vmem_limit_bytes=12 * MIB),
-        name="winds",
-    )(winds, *small)
+        out_shape=[jax.ShapeDtypeStruct(u.shape, jnp.float32)] * 2,
+        compiler_params=pltpu.CompilerParams(vmem_limit_bytes=8 * MIB),
+        name="rims",
+    )(winds, u, v, *small)
 
 
 def all_of(x):
@@ -420,8 +437,8 @@
 
     by_rows = [winds[at, :, row].reshape(levels, 2, wide) for at, row in ((0, 0), (-1, -1))]
     wind_rims = [x.reshape(2 * levels, wide) for x in beyond_band(*by_rows, band, bands, z_low, -1.0)]
-    next_t, next_q = step_tracers(winds, t, q, south, north, west, east, factors)
-    next_u, next_v = step_winds(winds, width, rows, *wind_rims, factors)
+    next_t, next_q, next_u, next_v = step_inside(winds, t, q, south, north, west, east, factors)
+    next_u, next_v = step_rims(winds, 0.5 * next_u, 0.5 * next_v, *wind_rims, factors)
     return tuple(jnp.swapaxes(x, 1, 2) for x in (next_u, next_v, next_t, next_q))
 
 

time: 74.4 us -> 73.6 us (0.989)
  starting transfers between devices: 25.6 us -> 24.5 us
    ppermute x1, waiting for transfers between devices: 0.01 us -> 3.8 us  [on_device(): west = lax.ppermute(lasts, LON, ring)]
    ppermute x2, waiting for transfers between devices: 10.2 us -> 7.04 us  [beyond_band(): from_after = lax.ppermute(backward, ALL, [(b, a) for a, b in pairs])]
    ppermute x2, starting transfers between devices: 4.45 us -> 1.61 us  [beyond_band(): from_before = lax.ppermute(onward, ALL, pairs)]
    ppermute x2, starting transfers between devices: 4.54 us -> 6.74 us  [beyond_band(): from_after = lax.ppermute(backward, ALL, [(b, a) for a, b in pairs])]
    pallas_call x1, Pallas kernels: 4.45 us -> 3.57 us  [polar_filter(): pl.pallas_call(lambda *refs: filter_kernel(width, *refs), in_specs=[whole...]
  transfers between devices with their start and end apart: 8 -> 8, of which waited for: 4 -> 4; matrix products, arithmetic and copies ran while one was open for 2% -> 2% of each run, Pallas kernels for 5% -> 7%
where the time goes in v5:
time: 73.6 us; the launch traced here: 73.3 us
  waiting for transfers between devices  33.1 us (45%)
  starting transfers between devices  24.5 us (33%)
  Pallas kernels  12.5 us (17%)
  other arithmetic  1.64 us (2%)
  between operations  0.79 us (1%)
    all_to_all x1, waiting for transfers between devices, on_device(): lax.all_to_all(filtered, LON, split_axis=0, concat_axis=0, tiled=True)  22 us
    ppermute x2, waiting for transfers between devices, beyond_band(): from_after = lax.ppermute(backward, ALL, [(b, a) for a, b in pairs])  7.04 us
    ppermute x2, starting transfers between devices, beyond_band(): from_after = lax.ppermute(backward, ALL, [(b, a) for a, b in pairs])  6.74 us
    all_to_all x1, starting transfers between devices, on_device(): lax.all_to_all(filtered, LON, split_axis=0, concat_axis=0, tiled=True)  6.28 us
    all_to_all x1, starting transfers between devices, on_device(): circles = lax.all_to_all(sent, LON, split_axis=0, concat_axis=0, tiled=True)  6.06 us
    ppermute x1, waiting for transfers between devices, on_device(): west = lax.ppermute(lasts, LON, ring)  3.8 us
    pallas_call x1, Pallas kernels, polar_filter(): pl.pallas_call(lambda *refs: filter_kernel(width, *refs), in_specs=[whole...  3.57 us
    pallas_call x1, Pallas kernels, step_inside(): pl.pallas_call(inside_kernel, grid=(levels // AT_ONCE,), in_specs=[pl.Blo...  3.55 us
  transfers between devices with their start and end apart: 8, of which 4 were waited for; matrix products, arithmetic and copies ran while one was open for 2% of the time, Pallas kernels for 7%

profile of v5, /device:TPU:6, one launch (start us, length us, event | category | flops | bytes accessed | tf_op | source)
XLA Modules:
  0.0 73.3 jit_solution(7949463282328421249)
XLA Ops:
  0.6 2.6 %pack.1 = f32[16,8,8,384]{3,2,1,0:T(8,128)} custom-call(f32[4,360,128]{2,1,0:T(8,128)} %bitcast.12, f32[4,360,128]{2,1,0:T(8,128)} %bitcast.13), custom_call_target="tpu_custom_call" | custom-call | tf_op jit(solution)/shard_map/pack/pallas_call | solution.py:118
  3.2 0.0 copy-start
  3.2 0.0 copy-start.1
  3.2 6.1 %all-to-all-start = ((f32[16,8,8,384]{3,2,1,0:T(8,128)}), f32[16,8,8,384]{3,2,1,0:T(8,128)S(1)}, u32[]{:S(2)}, u32[]{:S(2)}) async-start(f32[16,8,8,384]{3,2,1,0:T(8,128)} %pack.1), calls=%async_computation | async-start | bytes 3145728 | tf_op jit(solution)/shard_map/all_to_all | solution.py:417
  9.3 0.0 copy-start.2
  9.3 0.0 copy-start.3
  9.3 0.0 copy-start.4
  9.3 0.0 copy-done
  9.3 0.0 copy-done.1
  9.3 1.3 %edges.1 = (f32[16,384]{1,0:T(8,128)S(1)}, f32[8,128]{1,0:T(8,128)S(1)}, f32[8,128]{1,0:T(8,128)}) custom-call(f32[4,360,128]{2,1,0:T(8,128)S(1)} %bitcast.8, f32[4,360,128]{2,1,0:T(8,128)S(1)} %bitcast.10), custom_call_target="tpu_custom_call" | custom-call | tf_op jit(solution)/shard_map/edges/pallas_call | solution.py:244
  10.6 0.4 collective-permute-start.2
  11.0 3.5 %collective-permute-start.3 = (f32[8,128]{1,0:T(8,128)S(1)}, f32[8,128]{1,0:T(8,128)S(1)}, u32[]{:S(2)}, u32[]{:S(2)}) collective-permute-start(f32[8,128]{1,0:T(8,128)S(1)} %get-tuple-element.20), channel_id=1, source_target_pairs={{1,0},{2,1},{3,2},{4,3},{5,4},{6,5},{7,6},{8,7},{9,8},{10,9},{11,1... | collective-permute-start | bytes 12296 | tf_op jit(solution)/shard_map/ppermute | solution.py:423
  14.4 0.6 slice_select_fusion
  15.0 3.8 %collective-permute-start.1 = (f32[8,384]{1,0:T(8,128)}, f32[8,384]{1,0:T(8,128)S(1)}, u32[]{:S(2)}, u32[]{:S(2)}) collective-permute-start(f32[8,384]{1,0:T(8,128)} %get-tuple-element.38), channel_id=1, source_target_pairs={{16,0},{17,1},{18,2},{19,3},{20,4},{21,5},{22,6},{23,7},{32,16},{3... | collective-permute-start | bytes 36872 | tf_op jit(solution)/shard_map/ppermute | solution.py:391
  18.9 0.0 collective-permute-start
  18.9 7.0 %collective-permute-done.1 = f32[8,384]{1,0:T(8,128)S(1)} collective-permute-done((f32[8,384]{1,0:T(8,128)}, f32[8,384]{1,0:T(8,128)S(1)}, u32[]{:S(2)}, u32[]{:S(2)}) %collective-permute-start.1) | collective-permute-done | bytes 12320 | tf_op jit(solution)/shard_map/ppermute | solution.py:391
  26.0 0.0 copy-start.5
  26.0 0.6 copy-done.5
  26.6 0.0 collective-permute-done
  26.6 0.7 broadcast_select_fusion.2
  27.3 3.8 %collective-permute-done.2.west_ref = f32[8,128]{1,0:T(8,128)S(1)} collective-permute-done((f32[8,128]{1,0:T(8,128)}, f32[8,128]{1,0:T(8,128)S(1)}, u32[]{:S(2)}, u32[]{:S(2)}) %collective-permute-start.2) | collective-permute-done | bytes 4128 | tf_op jit(solution)/shard_map/ppermute | solution.py:422
  31.1 0.0 collective-permute-done.3.east_ref
  31.1 0.3 all-to-all-done.refs_0_
  31.4 0.0 copy-done.2
  31.4 0.0 copy-done.3
  31.4 0.0 copy-done.4
  31.4 3.6 %polar_filter.1 = f32[16,8,8,384]{3,2,1,0:T(8,128)} custom-call(f32[16,8,8,384]{3,2,1,0:T(8,128)S(1)} %all-to-all-done.refs_0_, f32[8,1]{1,0:T(8,128)S(1)} %multiply_multiply_fusion.refs_1_, bf16[768,256]{1,0:T(8,128)(2,1)S(1)} %copy-done.2, f32[2,48,128]{2,1,0:T(8,128)S(1)} %copy-done.3, f32[48,128]{1,0:T(8,128)S(1)} %copy-done.4), custom_call_target="tpu_custom_call" | custom-call | tf_op jit(solution)/shard_map/polar_filter/pallas_call | solution.py:206
  35.0 6.3 %all-to-all-start.1 = ((f32[16,8,8,384]{3,2,1,0:T(8,128)}), f32[16,8,8,384]{3,2,1,0:T(8,128)S(1)}, u32[]{:S(2)}, u32[]{:S(2)}) async-start(f32[16,8,8,384]{3,2,1,0:T(8,128)} %polar_filter.1), calls=%async_computation.1 | async-start | bytes 3145728 | tf_op jit(solution)/shard_map/all_to_all | solution.py:429
  41.3 0.1 fusion.2
  41.4 22.0 %all-to-all-done.1.w_ref = f32[16,8,8,384]{3,2,1,0:T(8,128)S(1)} async-done(((f32[16,8,8,384]{3,2,1,0:T(8,128)}), f32[16,8,8,384]{3,2,1,0:T(8,128)S(1)}, u32[]{:S(2)}, u32[]{:S(2)}) %all-to-all-start.1) | async-done | bytes 1572896 | tf_op jit(solution)/shard_map/all_to_all | solution.py:429
  63.4 0.1 fusion.1
  63.5 1.6 %collective-permute-start.4 = (f32[4,2,384]{2,1,0:T(2,128)S(1)}, f32[4,2,384]{2,1,0:T(2,128)S(1)}, u32[]{:S(2)}, u32[]{:S(2)}) collective-permute-start(f32[4,2,384]{2,1,0:T(2,128)S(1)} %select_n.73), channel_id=1, source_target_pairs={{0,16},{1,17},{2,18},{3,19},{4,20},{5,21},{6,22},{7,23},{16,32},{1... | collective-permute-start | bytes 36872 | tf_op jit(solution)/shard_map/ppermute | solution.py:390
  65.1 2.9 %collective-permute-start.5 = (f32[4,2,384]{2,1,0:T(2,128)S(1)}, f32[4,2,384]{2,1,0:T(2,128)S(1)}, u32[]{:S(2)}, u32[]{:S(2)}) collective-permute-start(f32[4,2,384]{2,1,0:T(2,128)S(1)} %select_n.75), channel_id=1, source_target_pairs={{16,0},{17,1},{18,2},{19,3},{20,4},{21,5},{22,6},{23,7},{32,16},{3... | collective-permute-start | bytes 36872 | tf_op jit(solution)/shard_map/ppermute | solution.py:391
  68.0 3.6 %inside.1 = (f32[4,360,128]{2,1,0:T(8,128)}, f32[4,360,128]{2,1,0:T(8,128)}, f32[4,360,128]{2,1,0:T(8,128)S(1)}, f32[4,360,128]{2,1,0:T(8,128)S(1)}) custom-call(f32[16,8,8,384]{3,2,1,0:T(8,128)S(1)} %all-to-all-done.1.w_ref, f32[4,360,128]{2,1,0:T(8,128)S(1)} %bitcast.9, f32[4,360,128]{2,1,0:T(8,128)S(1)} %bitcast.11, ...), custom_call_target="tpu_custom_call" | custom-call | tf_op jit(solution)/shard_map/inside/pallas_call | solution.py:346
  71.6 0.1 broadcast_multiply_fusion.v_ref
  71.6 0.0 collective-permute-done.4
  71.7 0.0 collective-permute-done.5
  71.7 1.5 %rims.1 = (f32[4,360,128]{2,1,0:T(8,128)}, f32[4,360,128]{2,1,0:T(8,128)}) custom-call(f32[16,8,8,384]{3,2,1,0:T(8,128)S(1)} %all-to-all-done.1.w_ref, f32[4,360,128]{2,1,0:T(8,128)S(1)} %broadcast_multiply_fusion.1.u_ref, f32[4,360,128]{2,1,0:T(8,128)S(1)} %broadcast_multiply_fusion.v_ref, f32[8,384]{1,0:T(8,128)S(1)} %reshape.90.south_ref, ...), custom_call_target="tpu_custom_call" | custom-call | tf_op jit(solution)/shard_map/rims/pallas_call | solution.py:361
  (8 shorter events, 0.2 us)
Async XLA Ops:
  3.2 6.1 %copy-start = (f32[4,128,360]{1,2,0:T(8,128)S(1)}, f32[4,128,360]{1,2,0:T(8,128)}, u32[]{:S(2)}) copy-start(f32[4,128,360]{1,2,0:T(8,128)} %param.9) | copy-start | bytes 2211844
  3.2 6.1 %copy-start.1 = (f32[4,128,360]{1,2,0:T(8,128)S(1)}, f32[4,128,360]{1,2,0:T(8,128)}, u32[]{:S(2)}) copy-start(f32[4,128,360]{1,2,0:T(8,128)} %param.10) | copy-start | bytes 2211844
  3.2 28.2 %all-to-all-start = ((f32[16,8,8,384]{3,2,1,0:T(8,128)}), f32[16,8,8,384]{3,2,1,0:T(8,128)S(1)}, u32[]{:S(2)}, u32[]{:S(2)}) async-start(f32[16,8,8,384]{3,2,1,0:T(8,128)} %pack.1), calls=%async_computation | async-start | bytes 3145728 | tf_op jit(solution)/shard_map/all_to_all | solution.py:417
  9.3 22.1 %copy-start.2 = (bf16[768,256]{1,0:T(8,128)(2,1)S(1)}, bf16[768,256]{1,0:T(8,128)(2,1)}, u32[]{:S(2)}) copy-start(bf16[768,256]{1,0:T(8,128)(2,1)} %constant.48.clone.refs_2_) | copy-start | bytes 1179652
  9.3 22.1 %copy-start.3 = (f32[2,48,128]{2,1,0:T(8,128)S(1)}, f32[2,48,128]{2,1,0:T(8,128)}, u32[]{:S(2)}) copy-start(f32[2,48,128]{2,1,0:T(8,128)} %constant.49.clone.refs_3_) | copy-start | bytes 147460
  9.3 22.1 %copy-start.4 = (f32[48,128]{1,0:T(8,128)S(1)}, f32[48,128]{1,0:T(8,128)}, u32[]{:S(2)}) copy-start(f32[48,128]{1,0:T(8,128)} %constant.50.clone.refs_4_) | copy-start | bytes 73732
  10.6 20.5 %collective-permute-start.2 = (f32[8,128]{1,0:T(8,128)}, f32[8,128]{1,0:T(8,128)S(1)}, u32[]{:S(2)}, u32[]{:S(2)}) collective-permute-start(f32[8,128]{1,0:T(8,128)} %get-tuple-element.19), channel_id=1, source_target_pairs={{0,1},{1,2},{2,3},{3,4},{4,5},{5,6},{6,7},{7,8},{8,9},{9,10},{10,1... | collective-permute-start | bytes 12296 | tf_op jit(solution)/shard_map/ppermute | solution.py:422
  11.0 20.1 %collective-permute-start.3 = (f32[8,128]{1,0:T(8,128)S(1)}, f32[8,128]{1,0:T(8,128)S(1)}, u32[]{:S(2)}, u32[]{:S(2)}) collective-permute-start(f32[8,128]{1,0:T(8,128)S(1)} %get-tuple-element.20), channel_id=1, source_target_pairs={{1,0},{2,1},{3,2},{4,3},{5,4},{6,5},{7,6},{8,7},{9,8},{10,9},{11,1... | collective-permute-start | bytes 12296 | tf_op jit(solution)/shard_map/ppermute | solution.py:423
  15.0 10.9 %collective-permute-start.1 = (f32[8,384]{1,0:T(8,128)}, f32[8,384]{1,0:T(8,128)S(1)}, u32[]{:S(2)}, u32[]{:S(2)}) collective-permute-start(f32[8,384]{1,0:T(8,128)} %get-tuple-element.38), channel_id=1, source_target_pairs={{16,0},{17,1},{18,2},{19,3},{20,4},{21,5},{22,6},{23,7},{32,16},{3... | collective-permute-start | bytes 36872 | tf_op jit(solution)/shard_map/ppermute | solution.py:391
  18.9 7.7 %collective-permute-start = (f32[8,384]{1,0:T(8,128)}, f32[8,384]{1,0:T(8,128)}, u32[]{:S(2)}, u32[]{:S(2)}) collective-permute-start(f32[8,384]{1,0:T(8,128)} %get-tuple-element.39), channel_id=1, source_target_pairs={{0,16},{1,17},{2,18},{3,19},{4,20},{5,21},{6,22},{7,23},{16,32},{1... | collective-permute-start | bytes 36872 | tf_op jit(solution)/shard_map/ppermute | solution.py:390
  26.0 0.6 copy-start.5
  35.0 28.4 %all-to-all-start.1 = ((f32[16,8,8,384]{3,2,1,0:T(8,128)}), f32[16,8,8,384]{3,2,1,0:T(8,128)S(1)}, u32[]{:S(2)}, u32[]{:S(2)}) async-start(f32[16,8,8,384]{3,2,1,0:T(8,128)} %polar_filter.1), calls=%async_computation.1 | async-start | bytes 3145728 | tf_op jit(solution)/shard_map/all_to_all | solution.py:429
  63.5 8.2 %collective-permute-start.4 = (f32[4,2,384]{2,1,0:T(2,128)S(1)}, f32[4,2,384]{2,1,0:T(2,128)S(1)}, u32[]{:S(2)}, u32[]{:S(2)}) collective-permute-start(f32[4,2,384]{2,1,0:T(2,128)S(1)} %select_n.73), channel_id=1, source_target_pairs={{0,16},{1,17},{2,18},{3,19},{4,20},{5,21},{6,22},{7,23},{16,32},{1... | collective-permute-start | bytes 36872 | tf_op jit(solution)/shard_map/ppermute | solution.py:390
  65.1 6.6 %collective-permute-start.5 = (f32[4,2,384]{2,1,0:T(2,128)S(1)}, f32[4,2,384]{2,1,0:T(2,128)S(1)}, u32[]{:S(2)}, u32[]{:S(2)}) collective-permute-start(f32[4,2,384]{2,1,0:T(2,128)S(1)} %select_n.75), channel_id=1, source_target_pairs={{16,0},{17,1},{18,2},{19,3},{20,4},{21,5},{22,6},{23,7},{32,16},{3... | collective-permute-start | bytes 36872 | tf_op jit(solution)/shard_map/ppermute | solution.py:391

commit v6 on v5

--- a/solution.py
+++ b/solution.py
@@ -17,6 +17,7 @@
 LANES = 128
 THIRDS = 3
 AT_ONCE = 2
+SPARE = 8
 MIB = 1024 * 1024
 
 
@@ -98,30 +99,88 @@
     return out
 
 
-def pack_kernel(u_ref, v_ref, out_ref):
-    parts, _, sub, wide = out_ref.shape
-    count, width, rows = u_ref.shape
+def host_of(group):
+    return THIRDS * (group // 2) + group % 2
+
+
+def guest_lanes(tile, group, shift):
+    axis = tile.ndim - 1
+    lane = lax.broadcasted_iota(jnp.int32, tile.shape, axis)
+    start = SPARE * group if shift > 0 else LANES - SPARE
+    turn = (SPARE * group + SPARE if shift > 0 else LANES - SPARE - SPARE * group) % LANES
+    inside = (lane >= start) & (lane < start + SPARE)
+    return inside, pltpu.roll(tile, turn, axis) if turn else tile
+
+
+def with_guest(tile, guest, group):
+    inside, turned_guest = guest_lanes(guest, group, -1)
+    return jnp.where(inside, turned_guest, tile)
+
+
+def guest_of(tile_at):
+    guest = tile_at(host_of(LANES // SPARE - 1))
+    for group in range(LANES // SPARE - 1):
+        inside, value = guest_lanes(tile_at(host_of(group)), group, 1)
+        guest = jnp.where(inside, value, guest)
+    return guest
+
+
+def pack_kernel(u_hbm, v_hbm, out_hbm, u_ref, v_ref, out_ref, in_sems, out_sems):
+    levels, width, rows = u_ref.shape
+    parts, tiles, sub, _ = out_ref.shape
     short = width // THIRDS
     blank = jnp.zeros((LANES - short, rows), jnp.float32)
-    for level in range(count):
-        for i, ref in enumerate((u_ref, v_ref)):
-            for e in range(THIRDS):
-                piece = ref[level, e * short : (e + 1) * short]
-                piece = jnp.concatenate([piece, blank], axis=0).T.reshape(parts, sub, LANES)
-                out_ref[:, 2 * level + i, :, e * LANES : (e + 1) * LANES] = piece
-
-
-def pack(u, v, parts, wide):
+    pairs = list(range(levels - AT_ONCE, -1, -AT_ONCE))
+    loads = {}
+    for first in pairs:
+        span = slice(first, first + AT_ONCE)
+        for i, (hbm, ref) in enumerate(((u_hbm, u_ref), (v_hbm, v_ref))):
+            load = pltpu.make_async_copy(hbm.at[span], ref.at[span], in_sems.at[2 * first + i])
+            load.start()
+            loads[first, i] = load
+
+    def piece(level, i, e):
+        part = (u_ref, v_ref)[i][level, e * short : (e + 1) * short]
+        return jnp.concatenate([part, blank], axis=0).T.reshape(parts, sub, LANES)
+
+    stores = []
+    guest = None
+    for first in pairs:
+        for i in range(2):
+            loads[first, i].wait()
+        if guest is None:
+            guest = piece(levels - 1, 1, THIRDS - 1)
+        for level in range(first + AT_ONCE - 1, first - 1, -1):
+            for i in range(2):
+                for e in range(THIRDS):
+                    tile, group = THIRDS * (2 * level + i) + e, 2 * (2 * level + i) + e
+                    if tile < tiles:
+                        value = piece(level, i, e)
+                        out_ref[:, tile] = with_guest(value, guest, group) if e < 2 else value
+            span = slice(2 * THIRDS * level, min(2 * THIRDS * (level + 1), tiles))
+            stores.append(pltpu.make_async_copy(out_ref.at[:, span], out_hbm.at[:, span], out_sems.at[level]))
+            stores[-1].start()
+    for store in stores:
+        store.wait()
+
+
+def pack(u, v, parts):
     levels, width, rows = u.shape
-    sub = rows // parts
-    spec = pl.BlockSpec((AT_ONCE, width, rows), lambda g: (g, 0, 0))
+    shape = (parts, 2 * levels * THIRDS - 1, rows // parts, LANES)
+    apart = pl.BlockSpec(memory_space=pltpu.HBM)
     return pl.pallas_call(
         pack_kernel,
-        grid=(levels // AT_ONCE,),
-        in_specs=[spec, spec],
-        out_specs=pl.BlockSpec((parts, 2 * AT_ONCE, sub, wide), lambda g: (0, g, 0, 0)),
-        out_shape=jax.ShapeDtypeStruct((parts, 2 * levels, sub, wide), jnp.float32),
-        compiler_params=pltpu.CompilerParams(vmem_limit_bytes=8 * MIB),
+        in_specs=[apart, apart],
+        out_specs=apart,
+        out_shape=pltpu.HBM(shape, jnp.float32),
+        scratch_shapes=[
+            pltpu.VMEM(u.shape, jnp.float32),
+            pltpu.VMEM(v.shape, jnp.float32),
+            pltpu.VMEM(shape, jnp.float32),
+            pltpu.SemaphoreType.DMA((2 * levels,)),
+            pltpu.SemaphoreType.DMA((levels,)),
+        ],
+        compiler_params=pltpu.CompilerParams(vmem_limit_bytes=12 * MIB),
         name="pack",
     )(*[pltpu.with_memory_space_constraint(x, pltpu.HBM) for x in (u, v)])
 
@@ -134,13 +193,13 @@
     )
 
 
-def filter_kernel(width, x_ref, keep_ref, stacked_ref, twiddle_ref, sine_ref, out_hbm, out_ref, sems, *held):
-    parts, planes, sub, wide = x_ref.shape
+def filter_kernel(width, x_ref, keep_ref, stacked_ref, twiddle_ref, sine_ref, out_hbm, out_ref, guest_ref, sems, *held):
+    parts, tiles, sub, _ = x_ref.shape
     many, group, _ = held[0].shape
     per_part = group // sub
+    levels = len(held) * per_part
     points, short = parts * width, width // THIRDS
     real, imag = slice(0, LANES), slice(LANES, 2 * LANES)
-    spans = [slice(e * LANES, (e + 1) * LANES) for e in range(THIRDS)]
     lane = lax.broadcasted_iota(jnp.int32, (sub, LANES), 1)
 
     def twisted(k, re, im):
@@ -151,13 +210,17 @@
     damping = keep / jnp.maximum(sine_ref[...][:, None, :], keep) * (1.0 / points)
     damping = damping[:, None]
     stores = []
+
+    def arrived(d, plane, e):
+        tile = THIRDS * plane + e
+        return x_ref[d, tile] if tile < tiles else guest_of(lambda host: x_ref[d, host])
 
     def gather(part, first):
         for level in range(per_part):
             rows = slice(level * sub, (level + 1) * sub)
             at = 2 * (first + level)
             y = many_point(
-                [(x_ref[d, at, :, lanes], x_ref[d, at + 1, :, lanes]) for d in range(parts) for lanes in spans]
+                [(arrived(d, at, e), arrived(d, at + 1, e)) for d in range(parts) for e in range(THIRDS)]
             )
             for k in range(many):
                 part[k, rows, real], part[k, rows, imag] = twisted(k, *y[k])
@@ -176,22 +239,30 @@
         for level in range(per_part):
             rows = slice(level * sub, (level + 1) * sub)
             y = many_point([twisted(k, part[k, rows, real], part[k, rows, imag]) for k in range(many)])
+            values = [[y[j][0] for j in range(many)], [-y[j][1] for j in range(many)]]
+            for i in range(2):
+                for d in range(parts):
+                    j = THIRDS * d + THIRDS - 1
+                    west = pltpu.roll(values[i][j - THIRDS], LANES - short, 1)
+                    east = pltpu.roll(values[i][(j + 1) % many], short, 1)
+                    value = jnp.where(lane == LANES - 1, west, jnp.where(lane == short, east, values[i][j]))
+                    tile = THIRDS * (2 * (first + level) + i) + THIRDS - 1
+                    if tile < tiles:
+                        out_ref[d, tile] = value
+                    else:
+                        guest_ref[d] = value
             for i in range(2):
                 plane = 2 * (first + level) + i
-                values = [-y[j][1] if i else y[j][0] for j in range(many)]
                 for d in range(parts):
-                    for e in range(THIRDS):
-                        value = values[THIRDS * d + e]
-                        if e == THIRDS - 1:
-                            west = pltpu.roll(values[(THIRDS * d - 1) % many], LANES - short, 1)
-                            east = pltpu.roll(values[(THIRDS * d + THIRDS) % many], short, 1)
-                            value = jnp.where(lane == LANES - 1, west, jnp.where(lane == short, east, value))
-                        out_ref[d, plane, :, spans[e]] = value
-        pair = slice(2 * first, 2 * (first + per_part))
-        stores.append(pltpu.make_async_copy(out_ref.at[:, pair], out_hbm.at[:, pair], sems.at[first]))
+                    for e in range(THIRDS - 1):
+                        out_ref[d, THIRDS * plane + e] = with_guest(
+                            values[i][THIRDS * d + e], guest_ref[d], 2 * plane + e
+                        )
+        span = slice(2 * THIRDS * first, min(2 * THIRDS * (first + per_part), tiles))
+        stores.append(pltpu.make_async_copy(out_ref.at[:, span], out_hbm.at[:, span], sems.at[first]))
         stores[-1].start()
 
-    for n, part in enumerate(held):
+    for n, part in reversed(list(enumerate(held))):
         gather(part, n * per_part)
         forward(part)
         backward(part)
@@ -201,7 +272,8 @@
 
 
 def polar_filter(blocks, keep, tables, width):
-    parts, planes, sub, wide = blocks.shape
+    parts, tiles, sub, _ = blocks.shape
+    levels = (tiles + 1) // (2 * THIRDS)
     whole = pl.BlockSpec(memory_space=pltpu.VMEM)
     return pl.pallas_call(
         lambda *refs: filter_kernel(width, *refs),
@@ -210,9 +282,10 @@
         out_shape=pltpu.HBM(blocks.shape, jnp.float32),
         scratch_shapes=[
             pltpu.VMEM(blocks.shape, jnp.float32),
-            pltpu.SemaphoreType.DMA((planes // 2,)),
+            pltpu.VMEM((parts, sub, LANES), jnp.float32),
+            pltpu.SemaphoreType.DMA((levels,)),
         ]
-        + [pltpu.VMEM((THIRDS * parts, 1 * sub, 2 * LANES), jnp.float32)] * (planes // 2 // 1),
+        + [pltpu.VMEM((THIRDS * parts, sub, 2 * LANES), jnp.float32)] * levels,
         compiler_params=pltpu.CompilerParams(vmem_limit_bytes=16 * MIB),
         name="polar_filter",
     )(blocks, keep, *tables)
@@ -251,10 +324,15 @@
     )(t, q)
 
 
-def joined(block, short):
-    parts, sub, wide = block.shape
-    spans = [slice(e * LANES, (e + 1) * LANES) for e in range(THIRDS)]
-    pieces = [block[:, :, lanes].reshape(parts * sub, LANES).T for lanes in spans]
+def joined(w_ref, level, i, short, guest):
+    parts, tiles, sub, _ = w_ref.shape
+    pieces = []
+    for e in range(THIRDS):
+        tile = THIRDS * (2 * level + i) + e
+        block = w_ref[:, jnp.minimum(tile, tiles - 1)]
+        if guest is not None and i == 1 and e == THIRDS - 1:
+            block = jnp.where(tile == tiles, guest, block)
+        pieces.append(block.reshape(parts * sub, LANES).T)
     return jnp.concatenate([x[:short] for x in pieces[:-1]] + pieces[-1:], axis=0)
 
 
@@ -301,7 +379,8 @@
     at = lax.broadcasted_iota(jnp.int32, (width, rows), 0)
     for n in range(count):
         level = pl.program_id(0) * count + n
-        full = [joined(w_ref[:, 2 * level + i], short) for i in range(2)]
+        guest = guest_of(lambda host: w_ref[:, host]) if n == count - 1 else None
+        full = [joined(w_ref, level, i, short, guest) for i in range(2)]
         u, v = [x[:width] for x in full]
         factors = (0.5 * ADV_COEF) * u, row_ref[1:2] - (0.5 * ADV_COEF) * v, row_ref[0:1]
         for i, out in enumerate((u_out, v_out)):
@@ -318,26 +397,39 @@
 
 
 def rims_kernel(w_ref, u_ref, v_ref, south_ref, north_ref, row_ref, u_out, v_out):
-    parts, _, sub, wide = w_ref.shape
+    parts, tiles, sub, _ = w_ref.shape
     count, width, rows = u_out.shape
     short = width // THIRDS
     first_factor = row_ref[0:1, 0:1] - row_ref[1:2, 0:1]
     last_factor = row_ref[0:1, rows - 1 :] + row_ref[1:2, rows - 1 :]
-    at = lax.broadcasted_iota(jnp.int32, (sub, wide), 0)
-    blank = jnp.zeros((rows - 2 * sub, wide), jnp.float32)
+    at = lax.broadcasted_iota(jnp.int32, (sub, LANES), 0)
+    blank = jnp.zeros((rows - 2 * sub, LANES), jnp.float32)
+
+    def rim_tiles(ref):
+        return lambda tile: jnp.broadcast_to(ref[pl.ds(tile, 1)], (sub, LANES))
+
+    def own_tiles(part):
+        return lambda tile: w_ref[part, tile]
+
+    sources = [rim_tiles(south_ref), rim_tiles(north_ref), own_tiles(0), own_tiles(parts - 1)]
+    guests = [guest_of(source) for source in sources]
     for n in range(count):
         level = pl.program_id(0) * count + n
-        by_first = first_factor + (0.5 * ADV_COEF) * w_ref[0, 2 * level + 1, :1]
-        by_last = last_factor - (0.5 * ADV_COEF) * w_ref[parts - 1, 2 * level + 1, sub - 1 :]
-        for i, (ref, out) in enumerate(((u_ref, u_out), (v_ref, v_out))):
-            plane = pl.ds(2 * level + i, 1)
-            first = jnp.where(at == 0, south_ref[plane] * by_first, 0.0)
-            last = jnp.where(at == sub - 1, north_ref[plane] * by_last, 0.0)
-            added = jnp.concatenate([first, blank, last], axis=0)
-            for e in range(THIRDS):
-                piece = added[:, e * LANES : (e + 1) * LANES].T[:short]
-                span = slice(e * short, (e + 1) * short)
-                out[n, span] = ref[n, span] + piece
+
+        def piece(source, i, e):
+            tile = THIRDS * (2 * level + i) + e
+            value = sources[source](jnp.minimum(tile, tiles - 1))
+            last = n == count - 1 and i == 1 and e == THIRDS - 1
+            return jnp.where(tile == tiles, guests[source], value) if last else value
+
+        for e in range(THIRDS):
+            by_first = first_factor + (0.5 * ADV_COEF) * piece(2, 1, e)[:1]
+            by_last = last_factor - (0.5 * ADV_COEF) * piece(3, 1, e)[sub - 1 :]
+            span = slice(e * short, (e + 1) * short)
+            for i, (ref, out) in enumerate(((u_ref, u_out), (v_ref, v_out))):
+                first = jnp.where(at == 0, piece(0, i, e) * by_first, 0.0)
+                last = jnp.where(at == sub - 1, piece(1, i, e) * by_last, 0.0)
+                out[n, span] = ref[n, span] + jnp.concatenate([first, blank, last], axis=0).T[:short]
 
 
 def step_inside(winds, t, q, *small):
@@ -413,7 +505,7 @@
         for x in (east_flow_speed, north_flow_speed, thermal_anomaly, moisture_anomaly)
     ]
 
-    sent = pack(u, v, parts, wide)
+    sent = pack(u, v, parts)
     circles = lax.all_to_all(sent, LON, split_axis=0, concat_axis=0, tiled=True)
 
     edge_rows, firsts, lasts = edges_of(t, q, wide)
@@ -435,8 +527,8 @@
     upper, lower = upper_edge / centre, lower_edge / centre
     factors = (0.5 * DIFF_COEF) * jnp.stack([upper + lower, upper - lower], axis=0)
 
-    by_rows = [winds[at, :, row].reshape(levels, 2, wide) for at, row in ((0, 0), (-1, -1))]
-    wind_rims = [x.reshape(2 * levels, wide) for x in beyond_band(*by_rows, band, bands, z_low, -1.0)]
+    by_rows = [winds[at, :, row] for at, row in ((0, 0), (-1, -1))]
+    wind_rims = beyond_band(*by_rows, band, bands, z_low, -1.0)
     next_t, next_q, next_u, next_v = step_inside(winds, t, q, south, north, west, east, factors)
     next_u, next_v = step_rims(winds, 0.5 * next_u, 0.5 * next_v, *wind_rims, factors)
     return tuple(jnp.swapaxes(x, 1, 2) for x in (next_u, next_v, next_t, next_q))

time: 73.6 us -> 72.2 us (0.981)
  waiting for transfers between devices: 33.1 us -> 34.8 us
  starting transfers between devices: 24.5 us -> 22.9 us
  other arithmetic: 1.64 us -> 0.24 us
    ppermute x1, waiting for transfers between devices: 3.8 us -> 4.94 us  [on_device(): west = lax.ppermute(lasts, LON, ring)]
    all_to_all x1, starting transfers between devices: 6.28 us -> 5.46 us  [on_device(): lax.all_to_all(filtered, LON, split_axis=0, concat_axis=0, tiled=True)]
    ppermute x2, waiting for transfers between devices: 0.01 us -> 0.8 us  [beyond_band(): from_before = lax.ppermute(onward, ALL, pairs)]
    ppermute x2, starting transfers between devices: 6.74 us -> 5.99 us  [beyond_band(): from_after = lax.ppermute(backward, ALL, [(b, a) for a, b in pairs])]
  transfers between devices with their start and end apart: 8 -> 8, of which waited for: 4 -> 5; matrix products, arithmetic and copies ran while one was open for 2% -> 0% of each run, Pallas kernels for 7% -> 6%
where the time goes in v6:
time: 72.2 us; the launch traced here: 71.9 us
  waiting for transfers between devices  34.8 us (48%)
  starting transfers between devices  22.9 us (32%)
  Pallas kernels  13.2 us (18%)
  between operations  0.78 us (1%)
    all_to_all x1, waiting for transfers between devices, on_device(): lax.all_to_all(filtered, LON, split_axis=0, concat_axis=0, tiled=True)  21.3 us
    ppermute x2, waiting for transfers between devices, beyond_band(): from_after = lax.ppermute(backward, ALL, [(b, a) for a, b in pairs])  7.47 us
    all_to_all x1, starting transfers between devices, on_device(): circles = lax.all_to_all(sent, LON, split_axis=0, concat_axis=0, tiled=True)  6.07 us
    ppermute x2, starting transfers between devices, beyond_band(): from_after = lax.ppermute(backward, ALL, [(b, a) for a, b in pairs])  5.99 us
    all_to_all x1, starting transfers between devices, on_device(): lax.all_to_all(filtered, LON, split_axis=0, concat_axis=0, tiled=True)  5.46 us
    ppermute x1, waiting for transfers between devices, on_device(): west = lax.ppermute(lasts, LON, ring)  4.94 us
    pallas_call x1, Pallas kernels, polar_filter(): pl.pallas_call(lambda *refs: filter_kernel(width, *refs), in_specs=[whole...  3.93 us
    pallas_call x1, Pallas kernels, step_inside(): pl.pallas_call(inside_kernel, grid=(levels // AT_ONCE,), in_specs=[pl.Blo...  3.72 us
  transfers between devices with their start and end apart: 8, of which 5 were waited for; matrix products, arithmetic and copies ran while one was open for 0% of the time, Pallas kernels for 6%

profile of v6, /device:TPU:6, one launch (start us, length us, event | category | flops | bytes accessed | tf_op | source)
XLA Modules:
  0.0 71.9 jit_solution(15868586885819396327)
XLA Ops:
  0.6 2.9 %pack.1 = f32[16,23,8,128]{3,2,1,0:T(8,128)} custom-call(f32[4,360,128]{2,1,0:T(8,128)} %bitcast.16, f32[4,360,128]{2,1,0:T(8,128)} %bitcast.17), custom_call_target="tpu_custom_call" | custom-call | tf_op jit(solution)/shard_map/pack/pallas_call | solution.py:171
  3.6 0.0 copy-start
  3.6 0.0 copy-start.1
  3.6 6.1 %all-to-all-start = ((f32[16,23,8,128]{3,2,1,0:T(8,128)}), f32[16,23,8,128]{3,2,1,0:T(8,128)S(1)}, u32[]{:S(2)}, u32[]{:S(2)}) async-start(f32[16,23,8,128]{3,2,1,0:T(8,128)} %pack.1), calls=%async_computation | async-start | bytes 3014656 | tf_op jit(solution)/shard_map/all_to_all | solution.py:509
  9.7 0.0 copy-start.2
  9.7 0.0 copy-start.3
  9.7 0.0 copy-start.4
  9.7 0.0 copy-done
  9.7 0.0 copy-done.1
  9.7 0.9 %edges.1 = (f32[16,384]{1,0:T(8,128)S(1)}, f32[8,128]{1,0:T(8,128)S(1)}, f32[8,128]{1,0:T(8,128)S(1)}) custom-call(f32[4,360,128]{2,1,0:T(8,128)S(1)} %bitcast.12, f32[4,360,128]{2,1,0:T(8,128)S(1)} %bitcast.14), custom_call_target="tpu_custom_call" | custom-call | tf_op jit(solution)/shard_map/edges/pallas_call | solution.py:317
  10.6 0.5 collective-permute-start.2
  11.0 3.5 %collective-permute-start.3 = (f32[8,128]{1,0:T(8,128)S(1)}, f32[8,128]{1,0:T(8,128)S(1)}, u32[]{:S(2)}, u32[]{:S(2)}) collective-permute-start(f32[8,128]{1,0:T(8,128)S(1)} %get-tuple-element.20), channel_id=1, source_target_pairs={{1,0},{2,1},{3,2},{4,3},{5,4},{6,5},{7,6},{8,7},{9,8},{10,9},{11,1... | collective-permute-start | bytes 12296 | tf_op jit(solution)/shard_map/ppermute | solution.py:515
  14.5 3.8 %collective-permute-start.1 = (f32[8,384]{1,0:T(8,128)S(1)}, f32[8,384]{1,0:T(8,128)S(1)}, u32[]{:S(2)}, u32[]{:S(2)}) collective-permute-start(f32[8,384]{1,0:T(8,128)S(1)} %get-tuple-element.38), channel_id=1, source_target_pairs={{16,0},{17,1},{18,2},{19,3},{20,4},{21,5},{22,6},{23,7},{32,16},{3... | collective-permute-start | bytes 36872 | tf_op jit(solution)/shard_map/ppermute | solution.py:483
  18.4 0.0 collective-permute-start
  18.4 7.5 %collective-permute-done.1 = f32[8,384]{1,0:T(8,128)S(1)} collective-permute-done((f32[8,384]{1,0:T(8,128)S(1)}, f32[8,384]{1,0:T(8,128)S(1)}, u32[]{:S(2)}, u32[]{:S(2)}) %collective-permute-start.1) | collective-permute-done | bytes 12320 | tf_op jit(solution)/shard_map/ppermute | solution.py:483
  25.9 0.0 collective-permute-done
  25.9 4.9 %collective-permute-done.2.west_ref = f32[8,128]{1,0:T(8,128)S(1)} collective-permute-done((f32[8,128]{1,0:T(8,128)S(1)}, f32[8,128]{1,0:T(8,128)S(1)}, u32[]{:S(2)}, u32[]{:S(2)}) %collective-permute-start.2) | collective-permute-done | bytes 4128 | tf_op jit(solution)/shard_map/ppermute | solution.py:514
  30.8 0.0 collective-permute-done.3.east_ref
  30.8 0.3 all-to-all-done.refs_0_
  31.1 0.0 copy-done.2
  31.1 0.0 copy-done.3
  31.1 0.0 copy-done.4
  31.1 3.9 %polar_filter.1 = f32[16,23,8,128]{3,2,1,0:T(8,128)} custom-call(f32[16,23,8,128]{3,2,1,0:T(8,128)S(1)} %all-to-all-done.refs_0_, f32[8,1]{1,0:T(8,128)S(1)} %multiply_multiply_fusion.refs_1_, bf16[768,256]{1,0:T(8,128)(2,1)S(1)} %copy-done.2, f32[2,48,128]{2,1,0:T(8,128)S(1)} %copy-done.3, f32[48,128]{1,0:T(8,128)S(1)} %copy-done.4), custom_call_target="tpu_custom_call" | custom-call | tf_op jit(solution)/shard_map/polar_filter/pallas_call | solution.py:278
  35.1 5.5 %all-to-all-start.1 = ((f32[16,23,8,128]{3,2,1,0:T(8,128)}), f32[16,23,8,128]{3,2,1,0:T(8,128)S(1)}, u32[]{:S(2)}, u32[]{:S(2)}) async-start(f32[16,23,8,128]{3,2,1,0:T(8,128)} %polar_filter.1), calls=%async_computation.1 | async-start | bytes 3014656 | tf_op jit(solution)/shard_map/all_to_all | solution.py:521
  40.5 0.1 fusion
  40.6 21.3 %all-to-all-done.1.w_ref = f32[16,23,8,128]{3,2,1,0:T(8,128)S(1)} async-done(((f32[16,23,8,128]{3,2,1,0:T(8,128)}), f32[16,23,8,128]{3,2,1,0:T(8,128)S(1)}, u32[]{:S(2)}, u32[]{:S(2)}) %all-to-all-start.1) | async-done | bytes 1507360 | tf_op jit(solution)/shard_map/all_to_all | solution.py:521
  62.0 2.1 %collective-permute-start.5 = (f32[23,128]{1,0:T(8,128)S(1)}, f32[23,128]{1,0:T(8,128)S(1)}, u32[]{:S(2)}, u32[]{:S(2)}) collective-permute-start(f32[23,128]{1,0:T(8,128)S(1)} %get-tuple-element.40), channel_id=1, source_target_pairs={{16,0},{17,1},{18,2},{19,3},{20,4},{21,5},{22,6},{23,7},{32,16},{3... | collective-permute-start | bytes 35336 | tf_op jit(solution)/shard_map/ppermute | solution.py:483
  64.1 1.5 %collective-permute-start.4 = (f32[23,128]{1,0:T(8,128)S(1)}, f32[23,128]{1,0:T(8,128)S(1)}, u32[]{:S(2)}, u32[]{:S(2)}) collective-permute-start(f32[23,128]{1,0:T(8,128)S(1)} %get-tuple-element.41), channel_id=1, source_target_pairs={{0,16},{1,17},{2,18},{3,19},{4,20},{5,21},{6,22},{7,23},{16,32},{1... | collective-permute-start | bytes 35336 | tf_op jit(solution)/shard_map/ppermute | solution.py:482
  65.6 3.7 %inside.1 = (f32[4,360,128]{2,1,0:T(8,128)}, f32[4,360,128]{2,1,0:T(8,128)}, f32[4,360,128]{2,1,0:T(8,128)S(1)}, f32[4,360,128]{2,1,0:T(8,128)S(1)}) custom-call(f32[16,23,8,128]{3,2,1,0:T(8,128)S(1)} %all-to-all-done.1.w_ref, f32[4,360,128]{2,1,0:T(8,128)S(1)} %bitcast.13, f32[4,360,128]{2,1,0:T(8,128)S(1)} %bitcast.15, ...), custom_call_target="tpu_custom_call" | custom-call | tf_op jit(solution)/shard_map/inside/pallas_call | solution.py:438
  69.3 0.1 broadcast_multiply_fusion.v_ref
  69.4 0.0 collective-permute-done.5
  69.4 0.8 %collective-permute-done.4 = f32[23,128]{1,0:T(8,128)S(1)} collective-permute-done((f32[23,128]{1,0:T(8,128)S(1)}, f32[23,128]{1,0:T(8,128)S(1)}, u32[]{:S(2)}, u32[]{:S(2)}) %collective-permute-start.4) | collective-permute-done | bytes 11808 | tf_op jit(solution)/shard_map/ppermute | solution.py:482
  70.2 1.7 %rims.1 = (f32[4,360,128]{2,1,0:T(8,128)}, f32[4,360,128]{2,1,0:T(8,128)}) custom-call(f32[16,23,8,128]{3,2,1,0:T(8,128)S(1)} %all-to-all-done.1.w_ref, f32[4,360,128]{2,1,0:T(8,128)S(1)} %broadcast_multiply_fusion.1.u_ref, f32[4,360,128]{2,1,0:T(8,128)S(1)} %broadcast_multiply_fusion.v_ref, f32[23,128]{1,0:T(8,128)S(1)} %get-tuple-element.35.south_ref, ...), custom_call_target="tpu_custom_call" | custom-call | tf_op jit(solution)/shard_map/rims/pallas_call | solution.py:453
  (8 shorter events, 0.1 us)
Async XLA Ops:
  3.6 6.1 %copy-start = (f32[4,128,360]{1,2,0:T(8,128)S(1)}, f32[4,128,360]{1,2,0:T(8,128)}, u32[]{:S(2)}) copy-start(f32[4,128,360]{1,2,0:T(8,128)} %param.9) | copy-start | bytes 2211844
  3.6 6.1 %copy-start.1 = (f32[4,128,360]{1,2,0:T(8,128)S(1)}, f32[4,128,360]{1,2,0:T(8,128)}, u32[]{:S(2)}) copy-start(f32[4,128,360]{1,2,0:T(8,128)} %param.10) | copy-start | bytes 2211844
  3.6 27.5 %all-to-all-start = ((f32[16,23,8,128]{3,2,1,0:T(8,128)}), f32[16,23,8,128]{3,2,1,0:T(8,128)S(1)}, u32[]{:S(2)}, u32[]{:S(2)}) async-start(f32[16,23,8,128]{3,2,1,0:T(8,128)} %pack.1), calls=%async_computation | async-start | bytes 3014656 | tf_op jit(solution)/shard_map/all_to_all | solution.py:509
  9.7 21.4 %copy-start.2 = (bf16[768,256]{1,0:T(8,128)(2,1)S(1)}, bf16[768,256]{1,0:T(8,128)(2,1)}, u32[]{:S(2)}) copy-start(bf16[768,256]{1,0:T(8,128)(2,1)} %constant.48.clone.refs_2_) | copy-start | bytes 1179652
  9.7 21.4 %copy-start.3 = (f32[2,48,128]{2,1,0:T(8,128)S(1)}, f32[2,48,128]{2,1,0:T(8,128)}, u32[]{:S(2)}) copy-start(f32[2,48,128]{2,1,0:T(8,128)} %constant.49.clone.refs_3_) | copy-start | bytes 147460
  9.7 21.4 %copy-start.4 = (f32[48,128]{1,0:T(8,128)S(1)}, f32[48,128]{1,0:T(8,128)}, u32[]{:S(2)}) copy-start(f32[48,128]{1,0:T(8,128)} %constant.50.clone.refs_4_) | copy-start | bytes 73732
  10.6 20.2 %collective-permute-start.2 = (f32[8,128]{1,0:T(8,128)S(1)}, f32[8,128]{1,0:T(8,128)S(1)}, u32[]{:S(2)}, u32[]{:S(2)}) collective-permute-start(f32[8,128]{1,0:T(8,128)S(1)} %get-tuple-element.19), channel_id=1, source_target_pairs={{0,1},{1,2},{2,3},{3,4},{4,5},{5,6},{6,7},{7,8},{8,9},{9,10},{10,1... | collective-permute-start | bytes 12296 | tf_op jit(solution)/shard_map/ppermute | solution.py:514
  11.0 19.8 %collective-permute-start.3 = (f32[8,128]{1,0:T(8,128)S(1)}, f32[8,128]{1,0:T(8,128)S(1)}, u32[]{:S(2)}, u32[]{:S(2)}) collective-permute-start(f32[8,128]{1,0:T(8,128)S(1)} %get-tuple-element.20), channel_id=1, source_target_pairs={{1,0},{2,1},{3,2},{4,3},{5,4},{6,5},{7,6},{8,7},{9,8},{10,9},{11,1... | collective-permute-start | bytes 12296 | tf_op jit(solution)/shard_map/ppermute | solution.py:515
  14.5 11.4 %collective-permute-start.1 = (f32[8,384]{1,0:T(8,128)S(1)}, f32[8,384]{1,0:T(8,128)S(1)}, u32[]{:S(2)}, u32[]{:S(2)}) collective-permute-start(f32[8,384]{1,0:T(8,128)S(1)} %get-tuple-element.38), channel_id=1, source_target_pairs={{16,0},{17,1},{18,2},{19,3},{20,4},{21,5},{22,6},{23,7},{32,16},{3... | collective-permute-start | bytes 36872 | tf_op jit(solution)/shard_map/ppermute | solution.py:483
  18.4 7.5 %collective-permute-start = (f32[8,384]{1,0:T(8,128)S(1)}, f32[8,384]{1,0:T(8,128)S(1)}, u32[]{:S(2)}, u32[]{:S(2)}) collective-permute-start(f32[8,384]{1,0:T(8,128)S(1)} %get-tuple-element.39), channel_id=1, source_target_pairs={{0,16},{1,17},{2,18},{3,19},{4,20},{5,21},{6,22},{7,23},{16,32},{1... | collective-permute-start | bytes 36872 | tf_op jit(solution)/shard_map/ppermute | solution.py:482
  35.1 26.9 %all-to-all-start.1 = ((f32[16,23,8,128]{3,2,1,0:T(8,128)}), f32[16,23,8,128]{3,2,1,0:T(8,128)S(1)}, u32[]{:S(2)}, u32[]{:S(2)}) async-start(f32[16,23,8,128]{3,2,1,0:T(8,128)} %polar_filter.1), calls=%async_computation.1 | async-start | bytes 3014656 | tf_op jit(solution)/shard_map/all_to_all | solution.py:521
  62.0 7.4 %collective-permute-start.5 = (f32[23,128]{1,0:T(8,128)S(1)}, f32[23,128]{1,0:T(8,128)S(1)}, u32[]{:S(2)}, u32[]{:S(2)}) collective-permute-start(f32[23,128]{1,0:T(8,128)S(1)} %get-tuple-element.40), channel_id=1, source_target_pairs={{16,0},{17,1},{18,2},{19,3},{20,4},{21,5},{22,6},{23,7},{32,16},{3... | collective-permute-start | bytes 35336 | tf_op jit(solution)/shard_map/ppermute | solution.py:483
  64.1 6.1 %collective-permute-start.4 = (f32[23,128]{1,0:T(8,128)S(1)}, f32[23,128]{1,0:T(8,128)S(1)}, u32[]{:S(2)}, u32[]{:S(2)}) collective-permute-start(f32[23,128]{1,0:T(8,128)S(1)} %get-tuple-element.41), channel_id=1, source_target_pairs={{0,16},{1,17},{2,18},{3,19},{4,20},{5,21},{6,22},{7,23},{16,32},{1... | collective-permute-start | bytes 35336 | tf_op jit(solution)/shard_map/ppermute | solution.py:482

commit v7 on v6

--- a/solution.py
+++ b/solution.py
@@ -139,24 +139,21 @@
             load.start()
             loads[first, i] = load
 
-    def piece(level, i, e):
-        part = (u_ref, v_ref)[i][level, e * short : (e + 1) * short]
-        return jnp.concatenate([part, blank], axis=0).T.reshape(parts, sub, LANES)
-
     stores = []
-    guest = None
     for first in pairs:
         for i in range(2):
             loads[first, i].wait()
-        if guest is None:
-            guest = piece(levels - 1, 1, THIRDS - 1)
         for level in range(first + AT_ONCE - 1, first - 1, -1):
             for i in range(2):
                 for e in range(THIRDS):
-                    tile, group = THIRDS * (2 * level + i) + e, 2 * (2 * level + i) + e
+                    tile, start = THIRDS * (2 * level + i) + e, (2 * (2 * level + i) + e) * SPARE
                     if tile < tiles:
-                        value = piece(level, i, e)
-                        out_ref[:, tile] = with_guest(value, guest, group) if e < 2 else value
+                        part = (u_ref, v_ref)[i][level, e * short : (e + 1) * short]
+                        rest = blank
+                        if e < THIRDS - 1 and start < short:
+                            rest = v_ref[levels - 1, width - short + start : width - short + start + SPARE]
+                        part = jnp.concatenate([part, rest], axis=0)
+                        out_ref[:, tile] = part.T.reshape(parts, sub, LANES)
             span = slice(2 * THIRDS * level, min(2 * THIRDS * (level + 1), tiles))
             stores.append(pltpu.make_async_copy(out_ref.at[:, span], out_hbm.at[:, span], out_sems.at[level]))
             stores[-1].start()
@@ -324,15 +321,18 @@
     )(t, q)
 
 
-def joined(w_ref, level, i, short, guest):
+def joined(w_ref, level, i, short, guest_ref, is_last):
     parts, tiles, sub, _ = w_ref.shape
     pieces = []
     for e in range(THIRDS):
         tile = THIRDS * (2 * level + i) + e
-        block = w_ref[:, jnp.minimum(tile, tiles - 1)]
-        if guest is not None and i == 1 and e == THIRDS - 1:
-            block = jnp.where(tile == tiles, guest, block)
-        pieces.append(block.reshape(parts * sub, LANES).T)
+        piece = w_ref[:, jnp.minimum(tile, tiles - 1)].reshape(parts * sub, LANES).T
+        if e < THIRDS - 1:
+            start = pl.multiple_of((2 * (2 * level + i) + e) * SPARE, SPARE)
+            guest_ref[pl.ds(start, SPARE)] = piece[short:]
+        elif is_last:
+            piece = jnp.where(tile == tiles, guest_ref[...], piece)
+        pieces.append(piece)
     return jnp.concatenate([x[:short] for x in pieces[:-1]] + pieces[-1:], axis=0)
 
 
@@ -371,7 +371,7 @@
 
 
 def inside_kernel(
-    w_ref, t_ref, q_ref, south_ref, north_ref, west_ref, east_ref, row_ref, t_out, q_out, u_out, v_out, table_ref
+    w_ref, t_ref, q_ref, south_ref, north_ref, west_ref, east_ref, row_ref, t_out, q_out, u_out, v_out, table_ref, guest_ref
 ):
     count, width, rows = t_ref.shape
     levels, short = pl.num_programs(0) * count, width // THIRDS
@@ -379,8 +379,7 @@
     at = lax.broadcasted_iota(jnp.int32, (width, rows), 0)
     for n in range(count):
         level = pl.program_id(0) * count + n
-        guest = guest_of(lambda host: w_ref[:, host]) if n == count - 1 else None
-        full = [joined(w_ref, level, i, short, guest) for i in range(2)]
+        full = [joined(w_ref, level, i, short, guest_ref, n == count - 1 and i == 1) for i in range(2)]
         u, v = [x[:width] for x in full]
         factors = (0.5 * ADV_COEF) * u, row_ref[1:2] - (0.5 * ADV_COEF) * v, row_ref[0:1]
         for i, out in enumerate((u_out, v_out)):
@@ -441,7 +440,10 @@
         in_specs=[pl.BlockSpec(memory_space=pltpu.VMEM), field, field] + [all_of(x) for x in small],
         out_specs=[field] * 4,
         out_shape=[jax.ShapeDtypeStruct(t.shape, jnp.float32)] * 4,
-        scratch_shapes=[pltpu.VMEM((2, 4 * LANES, 2 * LANES), jnp.bfloat16)],
+        scratch_shapes=[
+            pltpu.VMEM((2, 4 * LANES, 2 * LANES), jnp.bfloat16),
+            pltpu.VMEM((LANES, rows), jnp.float32),
+        ],
         compiler_params=pltpu.CompilerParams(vmem_limit_bytes=12 * MIB),
         name="inside",
     )(winds, t, q, *small)

time: 72.2 us -> 71.8 us (level)
  no operation moved by 1% of the time
where the time goes in v7:
time: 71.8 us; the launch traced here: 71.5 us
  waiting for transfers between devices  34.9 us (49%)
  starting transfers between devices  22.9 us (32%)
  Pallas kernels  12.6 us (18%)
  between operations  0.78 us (1%)
    all_to_all x1, waiting for transfers between devices, on_device(): lax.all_to_all(filtered, LON, split_axis=0, concat_axis=0, tiled=True)  21.3 us
    ppermute x2, waiting for transfers between devices, beyond_band(): from_after = lax.ppermute(backward, ALL, [(b, a) for a, b in pairs])  7.47 us
    all_to_all x1, starting transfers between devices, on_device(): circles = lax.all_to_all(sent, LON, split_axis=0, concat_axis=0, tiled=True)  6.07 us
    ppermute x2, starting transfers between devices, beyond_band(): from_after = lax.ppermute(backward, ALL, [(b, a) for a, b in pairs])  5.98 us
    all_to_all x1, starting transfers between devices, on_device(): lax.all_to_all(filtered, LON, split_axis=0, concat_axis=0, tiled=True)  5.46 us
    ppermute x1, waiting for transfers between devices, on_device(): west = lax.ppermute(lasts, LON, ring)  4.94 us
    pallas_call x1, Pallas kernels, polar_filter(): pl.pallas_call(lambda *refs: filter_kernel(width, *refs), in_specs=[whole...  3.93 us
    pallas_call x1, Pallas kernels, step_inside(): pl.pallas_call(inside_kernel, grid=(levels // AT_ONCE,), in_specs=[pl.Blo...  3.59 us
  transfers between devices with their start and end apart: 8, of which 5 were waited for; matrix products, arithmetic and copies ran while one was open for 0% of the time, Pallas kernels for 6%

profile of v7, /device:TPU:6, one launch (start us, length us, event | category | flops | bytes accessed | tf_op | source)
XLA Modules:
  0.0 71.5 jit_solution(16070406744496956992)
XLA Ops:
  0.6 2.6 %pack.1 = f32[16,23,8,128]{3,2,1,0:T(8,128)} custom-call(f32[4,360,128]{2,1,0:T(8,128)} %bitcast.16, f32[4,360,128]{2,1,0:T(8,128)} %bitcast.17), custom_call_target="tpu_custom_call" | custom-call | tf_op jit(solution)/shard_map/pack/pallas_call | solution.py:168
  3.2 0.0 copy-start
  3.2 0.0 copy-start.1
  3.2 6.1 %all-to-all-start = ((f32[16,23,8,128]{3,2,1,0:T(8,128)}), f32[16,23,8,128]{3,2,1,0:T(8,128)S(1)}, u32[]{:S(2)}, u32[]{:S(2)}) async-start(f32[16,23,8,128]{3,2,1,0:T(8,128)} %pack.1), calls=%async_computation | async-start | bytes 3014656 | tf_op jit(solution)/shard_map/all_to_all | solution.py:511
  9.3 0.0 copy-start.2
  9.3 0.0 copy-start.3
  9.3 0.0 copy-start.4
  9.3 0.0 copy-done
  9.3 0.0 copy-done.1
  9.4 0.9 %edges.1 = (f32[16,384]{1,0:T(8,128)S(1)}, f32[8,128]{1,0:T(8,128)S(1)}, f32[8,128]{1,0:T(8,128)S(1)}) custom-call(f32[4,360,128]{2,1,0:T(8,128)S(1)} %bitcast.12, f32[4,360,128]{2,1,0:T(8,128)S(1)} %bitcast.14), custom_call_target="tpu_custom_call" | custom-call | tf_op jit(solution)/shard_map/edges/pallas_call | solution.py:314
  10.2 0.5 collective-permute-start.2
  10.7 3.5 %collective-permute-start.3 = (f32[8,128]{1,0:T(8,128)S(1)}, f32[8,128]{1,0:T(8,128)S(1)}, u32[]{:S(2)}, u32[]{:S(2)}) collective-permute-start(f32[8,128]{1,0:T(8,128)S(1)} %get-tuple-element.20), channel_id=1, source_target_pairs={{1,0},{2,1},{3,2},{4,3},{5,4},{6,5},{7,6},{8,7},{9,8},{10,9},{11,1... | collective-permute-start | bytes 12296 | tf_op jit(solution)/shard_map/ppermute | solution.py:517
  14.1 3.8 %collective-permute-start.1 = (f32[8,384]{1,0:T(8,128)S(1)}, f32[8,384]{1,0:T(8,128)S(1)}, u32[]{:S(2)}, u32[]{:S(2)}) collective-permute-start(f32[8,384]{1,0:T(8,128)S(1)} %get-tuple-element.38), channel_id=1, source_target_pairs={{16,0},{17,1},{18,2},{19,3},{20,4},{21,5},{22,6},{23,7},{32,16},{3... | collective-permute-start | bytes 36872 | tf_op jit(solution)/shard_map/ppermute | solution.py:485
  18.0 0.0 collective-permute-start
  18.0 7.5 %collective-permute-done.1 = f32[8,384]{1,0:T(8,128)S(1)} collective-permute-done((f32[8,384]{1,0:T(8,128)S(1)}, f32[8,384]{1,0:T(8,128)S(1)}, u32[]{:S(2)}, u32[]{:S(2)}) %collective-permute-start.1) | collective-permute-done | bytes 12320 | tf_op jit(solution)/shard_map/ppermute | solution.py:485
  25.5 0.0 collective-permute-done
  25.5 4.9 %collective-permute-done.2.west_ref = f32[8,128]{1,0:T(8,128)S(1)} collective-permute-done((f32[8,128]{1,0:T(8,128)S(1)}, f32[8,128]{1,0:T(8,128)S(1)}, u32[]{:S(2)}, u32[]{:S(2)}) %collective-permute-start.2) | collective-permute-done | bytes 4128 | tf_op jit(solution)/shard_map/ppermute | solution.py:516
  30.4 0.0 collective-permute-done.3.east_ref
  30.5 0.3 all-to-all-done.refs_0_
  30.7 0.0 copy-done.2
  30.7 0.0 copy-done.3
  30.7 0.0 copy-done.4
  30.7 3.9 %polar_filter.1 = f32[16,23,8,128]{3,2,1,0:T(8,128)} custom-call(f32[16,23,8,128]{3,2,1,0:T(8,128)S(1)} %all-to-all-done.refs_0_, f32[8,1]{1,0:T(8,128)S(1)} %multiply_multiply_fusion.refs_1_, bf16[768,256]{1,0:T(8,128)(2,1)S(1)} %copy-done.2, f32[2,48,128]{2,1,0:T(8,128)S(1)} %copy-done.3, f32[48,128]{1,0:T(8,128)S(1)} %copy-done.4), custom_call_target="tpu_custom_call" | custom-call | tf_op jit(solution)/shard_map/polar_filter/pallas_call | solution.py:275
  34.7 5.5 %all-to-all-start.1 = ((f32[16,23,8,128]{3,2,1,0:T(8,128)}), f32[16,23,8,128]{3,2,1,0:T(8,128)S(1)}, u32[]{:S(2)}, u32[]{:S(2)}) async-start(f32[16,23,8,128]{3,2,1,0:T(8,128)} %polar_filter.1), calls=%async_computation.1 | async-start | bytes 3014656 | tf_op jit(solution)/shard_map/all_to_all | solution.py:523
  40.2 0.1 fusion
  40.2 21.3 %all-to-all-done.1.w_ref = f32[16,23,8,128]{3,2,1,0:T(8,128)S(1)} async-done(((f32[16,23,8,128]{3,2,1,0:T(8,128)}), f32[16,23,8,128]{3,2,1,0:T(8,128)S(1)}, u32[]{:S(2)}, u32[]{:S(2)}) %all-to-all-start.1) | async-done | bytes 1507360 | tf_op jit(solution)/shard_map/all_to_all | solution.py:523
  61.6 2.1 %collective-permute-start.5 = (f32[23,128]{1,0:T(8,128)S(1)}, f32[23,128]{1,0:T(8,128)S(1)}, u32[]{:S(2)}, u32[]{:S(2)}) collective-permute-start(f32[23,128]{1,0:T(8,128)S(1)} %get-tuple-element.40), channel_id=1, source_target_pairs={{16,0},{17,1},{18,2},{19,3},{20,4},{21,5},{22,6},{23,7},{32,16},{3... | collective-permute-start | bytes 35336 | tf_op jit(solution)/shard_map/ppermute | solution.py:485
  63.7 1.5 %collective-permute-start.4 = (f32[23,128]{1,0:T(8,128)S(1)}, f32[23,128]{1,0:T(8,128)S(1)}, u32[]{:S(2)}, u32[]{:S(2)}) collective-permute-start(f32[23,128]{1,0:T(8,128)S(1)} %get-tuple-element.41), channel_id=1, source_target_pairs={{0,16},{1,17},{2,18},{3,19},{4,20},{5,21},{6,22},{7,23},{16,32},{1... | collective-permute-start | bytes 35336 | tf_op jit(solution)/shard_map/ppermute | solution.py:484
  65.2 3.6 %inside.1 = (f32[4,360,128]{2,1,0:T(8,128)}, f32[4,360,128]{2,1,0:T(8,128)}, f32[4,360,128]{2,1,0:T(8,128)S(1)}, f32[4,360,128]{2,1,0:T(8,128)S(1)}) custom-call(f32[16,23,8,128]{3,2,1,0:T(8,128)S(1)} %all-to-all-done.1.w_ref, f32[4,360,128]{2,1,0:T(8,128)S(1)} %bitcast.13, f32[4,360,128]{2,1,0:T(8,128)S(1)} %bitcast.15, ...), custom_call_target="tpu_custom_call" | custom-call | tf_op jit(solution)/shard_map/inside/pallas_call | solution.py:437
  68.8 0.1 broadcast_multiply_fusion.v_ref
  68.9 0.0 collective-permute-done.5
  68.9 0.9 %collective-permute-done.4 = f32[23,128]{1,0:T(8,128)S(1)} collective-permute-done((f32[23,128]{1,0:T(8,128)S(1)}, f32[23,128]{1,0:T(8,128)S(1)}, u32[]{:S(2)}, u32[]{:S(2)}) %collective-permute-start.4) | collective-permute-done | bytes 11808 | tf_op jit(solution)/shard_map/ppermute | solution.py:484
  69.8 1.7 %rims.1 = (f32[4,360,128]{2,1,0:T(8,128)}, f32[4,360,128]{2,1,0:T(8,128)}) custom-call(f32[16,23,8,128]{3,2,1,0:T(8,128)S(1)} %all-to-all-done.1.w_ref, f32[4,360,128]{2,1,0:T(8,128)S(1)} %broadcast_multiply_fusion.1.u_ref, f32[4,360,128]{2,1,0:T(8,128)S(1)} %broadcast_multiply_fusion.v_ref, f32[23,128]{1,0:T(8,128)S(1)} %get-tuple-element.35.south_ref, ...), custom_call_target="tpu_custom_call" | custom-call | tf_op jit(solution)/shard_map/rims/pallas_call | solution.py:455
  (8 shorter events, 0.1 us)
Async XLA Ops:
  3.2 6.1 %copy-start = (f32[4,128,360]{1,2,0:T(8,128)S(1)}, f32[4,128,360]{1,2,0:T(8,128)}, u32[]{:S(2)}) copy-start(f32[4,128,360]{1,2,0:T(8,128)} %param.9) | copy-start | bytes 2211844
  3.2 6.1 %copy-start.1 = (f32[4,128,360]{1,2,0:T(8,128)S(1)}, f32[4,128,360]{1,2,0:T(8,128)}, u32[]{:S(2)}) copy-start(f32[4,128,360]{1,2,0:T(8,128)} %param.10) | copy-start | bytes 2211844
  3.2 27.5 %all-to-all-start = ((f32[16,23,8,128]{3,2,1,0:T(8,128)}), f32[16,23,8,128]{3,2,1,0:T(8,128)S(1)}, u32[]{:S(2)}, u32[]{:S(2)}) async-start(f32[16,23,8,128]{3,2,1,0:T(8,128)} %pack.1), calls=%async_computation | async-start | bytes 3014656 | tf_op jit(solution)/shard_map/all_to_all | solution.py:511
  9.3 21.4 %copy-start.2 = (bf16[768,256]{1,0:T(8,128)(2,1)S(1)}, bf16[768,256]{1,0:T(8,128)(2,1)}, u32[]{:S(2)}) copy-start(bf16[768,256]{1,0:T(8,128)(2,1)} %constant.48.clone.refs_2_) | copy-start | bytes 1179652
  9.3 21.4 %copy-start.3 = (f32[2,48,128]{2,1,0:T(8,128)S(1)}, f32[2,48,128]{2,1,0:T(8,128)}, u32[]{:S(2)}) copy-start(f32[2,48,128]{2,1,0:T(8,128)} %constant.49.clone.refs_3_) | copy-start | bytes 147460
  9.3 21.4 %copy-start.4 = (f32[48,128]{1,0:T(8,128)S(1)}, f32[48,128]{1,0:T(8,128)}, u32[]{:S(2)}) copy-start(f32[48,128]{1,0:T(8,128)} %constant.50.clone.refs_4_) | copy-start | bytes 73732
  10.2 20.2 %collective-permute-start.2 = (f32[8,128]{1,0:T(8,128)S(1)}, f32[8,128]{1,0:T(8,128)S(1)}, u32[]{:S(2)}, u32[]{:S(2)}) collective-permute-start(f32[8,128]{1,0:T(8,128)S(1)} %get-tuple-element.19), channel_id=1, source_target_pairs={{0,1},{1,2},{2,3},{3,4},{4,5},{5,6},{6,7},{7,8},{8,9},{9,10},{10,1... | collective-permute-start | bytes 12296 | tf_op jit(solution)/shard_map/ppermute | solution.py:516
  10.7 19.8 %collective-permute-start.3 = (f32[8,128]{1,0:T(8,128)S(1)}, f32[8,128]{1,0:T(8,128)S(1)}, u32[]{:S(2)}, u32[]{:S(2)}) collective-permute-start(f32[8,128]{1,0:T(8,128)S(1)} %get-tuple-element.20), channel_id=1, source_target_pairs={{1,0},{2,1},{3,2},{4,3},{5,4},{6,5},{7,6},{8,7},{9,8},{10,9},{11,1... | collective-permute-start | bytes 12296 | tf_op jit(solution)/shard_map/ppermute | solution.py:517
  14.1 11.4 %collective-permute-start.1 = (f32[8,384]{1,0:T(8,128)S(1)}, f32[8,384]{1,0:T(8,128)S(1)}, u32[]{:S(2)}, u32[]{:S(2)}) collective-permute-start(f32[8,384]{1,0:T(8,128)S(1)} %get-tuple-element.38), channel_id=1, source_target_pairs={{16,0},{17,1},{18,2},{19,3},{20,4},{21,5},{22,6},{23,7},{32,16},{3... | collective-permute-start | bytes 36872 | tf_op jit(solution)/shard_map/ppermute | solution.py:485
  18.0 7.5 %collective-permute-start = (f32[8,384]{1,0:T(8,128)S(1)}, f32[8,384]{1,0:T(8,128)S(1)}, u32[]{:S(2)}, u32[]{:S(2)}) collective-permute-start(f32[8,384]{1,0:T(8,128)S(1)} %get-tuple-element.39), channel_id=1, source_target_pairs={{0,16},{1,17},{2,18},{3,19},{4,20},{5,21},{6,22},{7,23},{16,32},{1... | collective-permute-start | bytes 36872 | tf_op jit(solution)/shard_map/ppermute | solution.py:484
  34.7 26.9 %all-to-all-start.1 = ((f32[16,23,8,128]{3,2,1,0:T(8,128)}), f32[16,23,8,128]{3,2,1,0:T(8,128)S(1)}, u32[]{:S(2)}, u32[]{:S(2)}) async-start(f32[16,23,8,128]{3,2,1,0:T(8,128)} %polar_filter.1), calls=%async_computation.1 | async-start | bytes 3014656 | tf_op jit(solution)/shard_map/all_to_all | solution.py:523
  61.6 7.3 %collective-permute-start.5 = (f32[23,128]{1,0:T(8,128)S(1)}, f32[23,128]{1,0:T(8,128)S(1)}, u32[]{:S(2)}, u32[]{:S(2)}) collective-permute-start(f32[23,128]{1,0:T(8,128)S(1)} %get-tuple-element.40), channel_id=1, source_target_pairs={{16,0},{17,1},{18,2},{19,3},{20,4},{21,5},{22,6},{23,7},{32,16},{3... | collective-permute-start | bytes 35336 | tf_op jit(solution)/shard_map/ppermute | solution.py:485
  63.7 6.1 %collective-permute-start.4 = (f32[23,128]{1,0:T(8,128)S(1)}, f32[23,128]{1,0:T(8,128)S(1)}, u32[]{:S(2)}, u32[]{:S(2)}) collective-permute-start(f32[23,128]{1,0:T(8,128)S(1)} %get-tuple-element.41), channel_id=1, source_target_pairs={{0,16},{1,17},{2,18},{3,19},{4,20},{5,21},{6,22},{7,23},{16,32},{1... | collective-permute-start | bytes 35336 | tf_op jit(solution)/shard_map/ppermute | solution.py:484

commit v8 on v7

--- a/solution.py
+++ b/solution.py
@@ -362,11 +362,11 @@
     return jnp.concatenate(rims + [blank], axis=0).T
 
 
-def stepped(f, east, west, rims, table, by_u, by_first, by_second):
+def stepped(f, east, west, rims, table, by_east, by_west, by_first, by_second):
     both = jnp.concatenate(in_two(f) + rims, axis=1)
     change = jnp.dot(both, table, preferred_element_type=jnp.float32)
     rows = f.shape[1]
-    value = f - by_u * (east - west) + DIFF_COEF * (east - 2.0 * f + west)
+    value = (1.0 - 2.0 * DIFF_COEF) * f + by_east * east + by_west * west
     return value + (change[:, :rows] * by_first + change[:, rows:] * by_second)
 
 
@@ -376,12 +376,13 @@
     count, width, rows = t_ref.shape
     levels, short = pl.num_programs(0) * count, width // THIRDS
     pl.when(pl.program_id(0) == 0)(lambda: fill_tables(table_ref))
-    at = lax.broadcasted_iota(jnp.int32, (width, rows), 0)
+    at = lax.broadcasted_iota(jnp.int32, (SPARE, rows), 0)
     for n in range(count):
         level = pl.program_id(0) * count + n
         full = [joined(w_ref, level, i, short, guest_ref, n == count - 1 and i == 1) for i in range(2)]
         u, v = [x[:width] for x in full]
-        factors = (0.5 * ADV_COEF) * u, row_ref[1:2] - (0.5 * ADV_COEF) * v, row_ref[0:1]
+        by_u = (0.5 * ADV_COEF) * u
+        factors = DIFF_COEF - by_u, DIFF_COEF + by_u, row_ref[1:2] - (0.5 * ADV_COEF) * v, row_ref[0:1]
         for i, out in enumerate((u_out, v_out)):
             west = pltpu.roll(full[i], 1, 0)[:width]
             east = pltpu.roll(full[i], full[i].shape[0] - 1, 0)[:width]
@@ -390,8 +391,11 @@
         for i, (ref, out) in enumerate(((t_ref, t_out), (q_ref, q_out))):
             f = ref[n]
             side = pl.ds(i * levels + level, 1)
-            west = jnp.where(at == 0, west_ref[side], pltpu.roll(f, 1, 0))
-            east = jnp.where(at == width - 1, east_ref[side], pltpu.roll(f, width - 1, 0))
+            west, east = pltpu.roll(f, 1, 0), pltpu.roll(f, width - 1, 0)
+            first = jnp.where(at == 0, west_ref[side], west[:SPARE])
+            last = jnp.where(at == SPARE - 1, east_ref[side], east[width - SPARE :])
+            west = jnp.concatenate([first, west[SPARE:]], axis=0)
+            east = jnp.concatenate([east[: width - SPARE], last], axis=0)
             out[n] = stepped(f, east, west, rims, table_ref[i], *factors)
 
 

time: 71.8 us -> 71.8 us (level)
  no operation moved by 1% of the time
where the time goes in v8:
time: 71.8 us; the launch traced here: 71.5 us
  waiting for transfers between devices  35.2 us (49%)
  starting transfers between devices  22.9 us (32%)
  Pallas kernels  12.4 us (17%)
  between operations  0.78 us (1%)
    all_to_all x1, waiting for transfers between devices, on_device(): lax.all_to_all(filtered, LON, split_axis=0, concat_axis=0, tiled=True)  21.3 us
    ppermute x2, waiting for transfers between devices, beyond_band(): from_after = lax.ppermute(backward, ALL, [(b, a) for a, b in pairs])  7.47 us
    all_to_all x1, starting transfers between devices, on_device(): circles = lax.all_to_all(sent, LON, split_axis=0, concat_axis=0, tiled=True)  6.07 us
    ppermute x2, starting transfers between devices, beyond_band(): from_after = lax.ppermute(backward, ALL, [(b, a) for a, b in pairs])  5.98 us
    all_to_all x1, starting transfers between devices, on_device(): lax.all_to_all(filtered, LON, split_axis=0, concat_axis=0, tiled=True)  5.46 us
    ppermute x1, waiting for transfers between devices, on_device(): west = lax.ppermute(lasts, LON, ring)  4.94 us
    pallas_call x1, Pallas kernels, polar_filter(): pl.pallas_call(lambda *refs: filter_kernel(width, *refs), in_specs=[whole...  3.93 us
    ppermute x1, starting transfers between devices, on_device(): east = lax.ppermute(firsts, LON, [(b, a) for a, b in ring])  3.47 us
  transfers between devices with their start and end apart: 8, of which 5 were waited for; matrix products, arithmetic and copies ran while one was open for 0% of the time, Pallas kernels for 6%

profile of v8, /device:TPU:6, one launch (start us, length us, event | category | flops | bytes accessed | tf_op | source)
XLA Modules:
  0.0 71.5 jit_solution(12150602296923202476)
XLA Ops:
  0.6 2.6 %pack.1 = f32[16,23,8,128]{3,2,1,0:T(8,128)} custom-call(f32[4,360,128]{2,1,0:T(8,128)} %bitcast.16, f32[4,360,128]{2,1,0:T(8,128)} %bitcast.17), custom_call_target="tpu_custom_call" | custom-call | tf_op jit(solution)/shard_map/pack/pallas_call | solution.py:168
  3.2 0.0 copy-start
  3.2 0.0 copy-start.1
  3.2 6.1 %all-to-all-start = ((f32[16,23,8,128]{3,2,1,0:T(8,128)}), f32[16,23,8,128]{3,2,1,0:T(8,128)S(1)}, u32[]{:S(2)}, u32[]{:S(2)}) async-start(f32[16,23,8,128]{3,2,1,0:T(8,128)} %pack.1), calls=%async_computation | async-start | bytes 3014656 | tf_op jit(solution)/shard_map/all_to_all | solution.py:515
  9.3 0.0 copy-start.2
  9.3 0.0 copy-start.3
  9.3 0.0 copy-start.4
  9.3 0.0 copy-done
  9.3 0.0 copy-done.1
  9.4 0.9 %edges.1 = (f32[16,384]{1,0:T(8,128)S(1)}, f32[8,128]{1,0:T(8,128)S(1)}, f32[8,128]{1,0:T(8,128)S(1)}) custom-call(f32[4,360,128]{2,1,0:T(8,128)S(1)} %bitcast.12, f32[4,360,128]{2,1,0:T(8,128)S(1)} %bitcast.14), custom_call_target="tpu_custom_call" | custom-call | tf_op jit(solution)/shard_map/edges/pallas_call | solution.py:314
  10.2 0.5 collective-permute-start.2
  10.7 3.5 %collective-permute-start.3 = (f32[8,128]{1,0:T(8,128)S(1)}, f32[8,128]{1,0:T(8,128)S(1)}, u32[]{:S(2)}, u32[]{:S(2)}) collective-permute-start(f32[8,128]{1,0:T(8,128)S(1)} %get-tuple-element.20), channel_id=1, source_target_pairs={{1,0},{2,1},{3,2},{4,3},{5,4},{6,5},{7,6},{8,7},{9,8},{10,9},{11,1... | collective-permute-start | bytes 12296 | tf_op jit(solution)/shard_map/ppermute | solution.py:521
  14.1 3.8 %collective-permute-start.1 = (f32[8,384]{1,0:T(8,128)S(1)}, f32[8,384]{1,0:T(8,128)S(1)}, u32[]{:S(2)}, u32[]{:S(2)}) collective-permute-start(f32[8,384]{1,0:T(8,128)S(1)} %get-tuple-element.38), channel_id=1, source_target_pairs={{16,0},{17,1},{18,2},{19,3},{20,4},{21,5},{22,6},{23,7},{32,16},{3... | collective-permute-start | bytes 36872 | tf_op jit(solution)/shard_map/ppermute | solution.py:489
  18.0 0.0 collective-permute-start
  18.0 7.5 %collective-permute-done.1 = f32[8,384]{1,0:T(8,128)S(1)} collective-permute-done((f32[8,384]{1,0:T(8,128)S(1)}, f32[8,384]{1,0:T(8,128)S(1)}, u32[]{:S(2)}, u32[]{:S(2)}) %collective-permute-start.1) | collective-permute-done | bytes 12320 | tf_op jit(solution)/shard_map/ppermute | solution.py:489
  25.5 0.0 collective-permute-done
  25.5 4.9 %collective-permute-done.2.west_ref = f32[8,128]{1,0:T(8,128)S(1)} collective-permute-done((f32[8,128]{1,0:T(8,128)S(1)}, f32[8,128]{1,0:T(8,128)S(1)}, u32[]{:S(2)}, u32[]{:S(2)}) %collective-permute-start.2) | collective-permute-done | bytes 4128 | tf_op jit(solution)/shard_map/ppermute | solution.py:520
  30.4 0.0 collective-permute-done.3.east_ref
  30.5 0.3 all-to-all-done.refs_0_
  30.7 0.0 copy-done.2
  30.7 0.0 copy-done.3
  30.7 0.0 copy-done.4
  30.7 3.9 %polar_filter.1 = f32[16,23,8,128]{3,2,1,0:T(8,128)} custom-call(f32[16,23,8,128]{3,2,1,0:T(8,128)S(1)} %all-to-all-done.refs_0_, f32[8,1]{1,0:T(8,128)S(1)} %multiply_multiply_fusion.refs_1_, bf16[768,256]{1,0:T(8,128)(2,1)S(1)} %copy-done.2, f32[2,48,128]{2,1,0:T(8,128)S(1)} %copy-done.3, f32[48,128]{1,0:T(8,128)S(1)} %copy-done.4), custom_call_target="tpu_custom_call" | custom-call | tf_op jit(solution)/shard_map/polar_filter/pallas_call | solution.py:275
  34.7 5.5 %all-to-all-start.1 = ((f32[16,23,8,128]{3,2,1,0:T(8,128)}), f32[16,23,8,128]{3,2,1,0:T(8,128)S(1)}, u32[]{:S(2)}, u32[]{:S(2)}) async-start(f32[16,23,8,128]{3,2,1,0:T(8,128)} %polar_filter.1), calls=%async_computation.1 | async-start | bytes 3014656 | tf_op jit(solution)/shard_map/all_to_all | solution.py:527
  40.2 0.1 fusion
  40.2 21.3 %all-to-all-done.1.w_ref = f32[16,23,8,128]{3,2,1,0:T(8,128)S(1)} async-done(((f32[16,23,8,128]{3,2,1,0:T(8,128)}), f32[16,23,8,128]{3,2,1,0:T(8,128)S(1)}, u32[]{:S(2)}, u32[]{:S(2)}) %all-to-all-start.1) | async-done | bytes 1507360 | tf_op jit(solution)/shard_map/all_to_all | solution.py:527
  61.6 2.1 %collective-permute-start.5 = (f32[23,128]{1,0:T(8,128)S(1)}, f32[23,128]{1,0:T(8,128)S(1)}, u32[]{:S(2)}, u32[]{:S(2)}) collective-permute-start(f32[23,128]{1,0:T(8,128)S(1)} %get-tuple-element.40), channel_id=1, source_target_pairs={{16,0},{17,1},{18,2},{19,3},{20,4},{21,5},{22,6},{23,7},{32,16},{3... | collective-permute-start | bytes 35336 | tf_op jit(solution)/shard_map/ppermute | solution.py:489
  63.7 1.5 %collective-permute-start.4 = (f32[23,128]{1,0:T(8,128)S(1)}, f32[23,128]{1,0:T(8,128)S(1)}, u32[]{:S(2)}, u32[]{:S(2)}) collective-permute-start(f32[23,128]{1,0:T(8,128)S(1)} %get-tuple-element.41), channel_id=1, source_target_pairs={{0,16},{1,17},{2,18},{3,19},{4,20},{5,21},{6,22},{7,23},{16,32},{1... | collective-permute-start | bytes 35336 | tf_op jit(solution)/shard_map/ppermute | solution.py:488
  65.2 3.3 %inside.1 = (f32[4,360,128]{2,1,0:T(8,128)}, f32[4,360,128]{2,1,0:T(8,128)}, f32[4,360,128]{2,1,0:T(8,128)S(1)}, f32[4,360,128]{2,1,0:T(8,128)S(1)}) custom-call(f32[16,23,8,128]{3,2,1,0:T(8,128)S(1)} %all-to-all-done.1.w_ref, f32[4,360,128]{2,1,0:T(8,128)S(1)} %bitcast.13, f32[4,360,128]{2,1,0:T(8,128)S(1)} %bitcast.15, ...), custom_call_target="tpu_custom_call" | custom-call | tf_op jit(solution)/shard_map/inside/pallas_call | solution.py:441
  68.6 0.1 broadcast_multiply_fusion.v_ref
  68.6 0.0 collective-permute-done.5
  68.6 1.2 %collective-permute-done.4 = f32[23,128]{1,0:T(8,128)S(1)} collective-permute-done((f32[23,128]{1,0:T(8,128)S(1)}, f32[23,128]{1,0:T(8,128)S(1)}, u32[]{:S(2)}, u32[]{:S(2)}) %collective-permute-start.4) | collective-permute-done | bytes 11808 | tf_op jit(solution)/shard_map/ppermute | solution.py:488
  69.8 1.7 %rims.1 = (f32[4,360,128]{2,1,0:T(8,128)}, f32[4,360,128]{2,1,0:T(8,128)}) custom-call(f32[16,23,8,128]{3,2,1,0:T(8,128)S(1)} %all-to-all-done.1.w_ref, f32[4,360,128]{2,1,0:T(8,128)S(1)} %broadcast_multiply_fusion.1.u_ref, f32[4,360,128]{2,1,0:T(8,128)S(1)} %broadcast_multiply_fusion.v_ref, f32[23,128]{1,0:T(8,128)S(1)} %get-tuple-element.35.south_ref, ...), custom_call_target="tpu_custom_call" | custom-call | tf_op jit(solution)/shard_map/rims/pallas_call | solution.py:459
  (8 shorter events, 0.1 us)
Async XLA Ops:
  3.2 6.1 %copy-start = (f32[4,128,360]{1,2,0:T(8,128)S(1)}, f32[4,128,360]{1,2,0:T(8,128)}, u32[]{:S(2)}) copy-start(f32[4,128,360]{1,2,0:T(8,128)} %param.9) | copy-start | bytes 2211844
  3.2 6.1 %copy-start.1 = (f32[4,128,360]{1,2,0:T(8,128)S(1)}, f32[4,128,360]{1,2,0:T(8,128)}, u32[]{:S(2)}) copy-start(f32[4,128,360]{1,2,0:T(8,128)} %param.10) | copy-start | bytes 2211844
  3.2 27.5 %all-to-all-start = ((f32[16,23,8,128]{3,2,1,0:T(8,128)}), f32[16,23,8,128]{3,2,1,0:T(8,128)S(1)}, u32[]{:S(2)}, u32[]{:S(2)}) async-start(f32[16,23,8,128]{3,2,1,0:T(8,128)} %pack.1), calls=%async_computation | async-start | bytes 3014656 | tf_op jit(solution)/shard_map/all_to_all | solution.py:515
  9.3 21.4 %copy-start.2 = (bf16[768,256]{1,0:T(8,128)(2,1)S(1)}, bf16[768,256]{1,0:T(8,128)(2,1)}, u32[]{:S(2)}) copy-start(bf16[768,256]{1,0:T(8,128)(2,1)} %constant.48.clone.refs_2_) | copy-start | bytes 1179652
  9.3 21.4 %copy-start.3 = (f32[2,48,128]{2,1,0:T(8,128)S(1)}, f32[2,48,128]{2,1,0:T(8,128)}, u32[]{:S(2)}) copy-start(f32[2,48,128]{2,1,0:T(8,128)} %constant.49.clone.refs_3_) | copy-start | bytes 147460
  9.3 21.4 %copy-start.4 = (f32[48,128]{1,0:T(8,128)S(1)}, f32[48,128]{1,0:T(8,128)}, u32[]{:S(2)}) copy-start(f32[48,128]{1,0:T(8,128)} %constant.50.clone.refs_4_) | copy-start | bytes 73732
  10.2 20.2 %collective-permute-start.2 = (f32[8,128]{1,0:T(8,128)S(1)}, f32[8,128]{1,0:T(8,128)S(1)}, u32[]{:S(2)}, u32[]{:S(2)}) collective-permute-start(f32[8,128]{1,0:T(8,128)S(1)} %get-tuple-element.19), channel_id=1, source_target_pairs={{0,1},{1,2},{2,3},{3,4},{4,5},{5,6},{6,7},{7,8},{8,9},{9,10},{10,1... | collective-permute-start | bytes 12296 | tf_op jit(solution)/shard_map/ppermute | solution.py:520
  10.7 19.8 %collective-permute-start.3 = (f32[8,128]{1,0:T(8,128)S(1)}, f32[8,128]{1,0:T(8,128)S(1)}, u32[]{:S(2)}, u32[]{:S(2)}) collective-permute-start(f32[8,128]{1,0:T(8,128)S(1)} %get-tuple-element.20), channel_id=1, source_target_pairs={{1,0},{2,1},{3,2},{4,3},{5,4},{6,5},{7,6},{8,7},{9,8},{10,9},{11,1... | collective-permute-start | bytes 12296 | tf_op jit(solution)/shard_map/ppermute | solution.py:521
  14.1 11.4 %collective-permute-start.1 = (f32[8,384]{1,0:T(8,128)S(1)}, f32[8,384]{1,0:T(8,128)S(1)}, u32[]{:S(2)}, u32[]{:S(2)}) collective-permute-start(f32[8,384]{1,0:T(8,128)S(1)} %get-tuple-element.38), channel_id=1, source_target_pairs={{16,0},{17,1},{18,2},{19,3},{20,4},{21,5},{22,6},{23,7},{32,16},{3... | collective-permute-start | bytes 36872 | tf_op jit(solution)/shard_map/ppermute | solution.py:489
  18.0 7.5 %collective-permute-start = (f32[8,384]{1,0:T(8,128)S(1)}, f32[8,384]{1,0:T(8,128)S(1)}, u32[]{:S(2)}, u32[]{:S(2)}) collective-permute-start(f32[8,384]{1,0:T(8,128)S(1)} %get-tuple-element.39), channel_id=1, source_target_pairs={{0,16},{1,17},{2,18},{3,19},{4,20},{5,21},{6,22},{7,23},{16,32},{1... | collective-permute-start | bytes 36872 | tf_op jit(solution)/shard_map/ppermute | solution.py:488
  34.7 26.9 %all-to-all-start.1 = ((f32[16,23,8,128]{3,2,1,0:T(8,128)}), f32[16,23,8,128]{3,2,1,0:T(8,128)S(1)}, u32[]{:S(2)}, u32[]{:S(2)}) async-start(f32[16,23,8,128]{3,2,1,0:T(8,128)} %polar_filter.1), calls=%async_computation.1 | async-start | bytes 3014656 | tf_op jit(solution)/shard_map/all_to_all | solution.py:527
  61.6 7.1 %collective-permute-start.5 = (f32[23,128]{1,0:T(8,128)S(1)}, f32[23,128]{1,0:T(8,128)S(1)}, u32[]{:S(2)}, u32[]{:S(2)}) collective-permute-start(f32[23,128]{1,0:T(8,128)S(1)} %get-tuple-element.40), channel_id=1, source_target_pairs={{16,0},{17,1},{18,2},{19,3},{20,4},{21,5},{22,6},{23,7},{32,16},{3... | collective-permute-start | bytes 35336 | tf_op jit(solution)/shard_map/ppermute | solution.py:489
  63.7 6.1 %collective-permute-start.4 = (f32[23,128]{1,0:T(8,128)S(1)}, f32[23,128]{1,0:T(8,128)S(1)}, u32[]{:S(2)}, u32[]{:S(2)}) collective-permute-start(f32[23,128]{1,0:T(8,128)S(1)} %get-tuple-element.41), channel_id=1, source_target_pairs={{0,16},{1,17},{2,18},{3,19},{4,20},{5,21},{6,22},{7,23},{16,32},{1... | collective-permute-start | bytes 35336 | tf_op jit(solution)/shard_map/ppermute | solution.py:488
